TPU v7x, 32 devices: a whole 2x2x4 slice. The times are simulated.
32 devices in a mesh: row: 4 (over y, x), col: 8 (over z, core).
Axes of the slice: x: 2, y: 2, z: 4, core: 2. Of those that a mesh axis runs over, the one named last changes fastest.
Arguments:
- inputs: bfloat16 [2, 8192, 2048], P(None, 'row', 'col'), may hold values from -8 to 8
- piece_starts: int32 [2, 8, 2], P(None, 'col'), may hold values from 0 to 768, as said below
- first_gain: float32 [2048], P('col'), may hold values from 0.1 to 1.9
- first_shift: float32 [2048], P('col'), may hold values from -1.75 to 1.75
- second_gain: float32 [2048], P('col'), may hold values from 0.1 to 1.9
- second_shift: float32 [2048], P('col'), may hold values from -1.75 to 1.75
- merged_weight: bfloat16 [2048, 6144], P('col', 'row'), may hold values from -0.125 to 0.125
- merged_bias: float32 [6144], P('row'), may hold values from -1.75 to 1.75
- output_weight: bfloat16 [2048, 2048], P('row', 'col'), may hold values from -1 to 1
- output_bias: float32 [2048], P('col'), may hold values from -1.75 to 1.75
- expand_weight: bfloat16 [2048, 8192], P('col', 'row'), may hold values from -0.125 to 0.125
- expand_bias: float32 [8192], P('row'), may hold values from -1.75 to 1.75
- reduce_weight: bfloat16 [8192, 2048], P('row', 'col'), may hold values from -0.0625 to 0.0625
- reduce_bias: float32 [2048], P('col'), may hold values from -1.75 to 1.75
- cotangent: bfloat16 [2, 8192, 2048], P(None, 'row', 'col'), may hold values from -8 to 8
Outputs:
- result: bfloat16 [2, 8192, 2048], P(None, 'row', 'col')
- input_grad: float32 [2, 8192, 2048], P(None, 'row', 'col')
- first_gain_grad: float32 [2048], P('col')
- first_shift_grad: float32 [2048], P('col')
- second_gain_grad: float32 [2048], P('col')
- second_shift_grad: float32 [2048], P('col')
- merged_weight_grad: float32 [2048, 6144], P('col', 'row')
- merged_bias_grad: float32 [6144], P('row')
- output_weight_grad: float32 [2048, 2048], P('row', 'col')
- output_bias_grad: float32 [2048], P('col')
- expand_weight_grad: float32 [2048, 8192], P('col', 'row')
- expand_bias_grad: float32 [8192], P('row')
- reduce_weight_grad: float32 [8192, 2048], P('row', 'col')
- reduce_bias_grad: float32 [2048], P('col')
Inputs may be any that keep to these rules, and one draw needn't show every extreme that they name: `piece_starts`: piece k of a sequence starts between k * 512 and (k + 1) * 512 - 256, so pieces never intersect; in every draw some piece starts at 0 and some at 768.
All inputs are finite; a program needn't handle non-finite values.
Results may differ from a plain program's by a relative error of at most 0.01.
Values may be sent and summed in bfloat16 or wider, within the bound.
A program may use at most 512 MiB of HBM per device.

v0:
```python
import jax
import jax.numpy as jnp
from jax import lax
from jax.sharding import PartitionSpec as P

D = 2048
HEAD = 256
ROT = 64
L = 1024
PIECE = 256


norm_eps = 1e-05
theta_base = 10000.0


def contract_last(left, right):
    return lax.dot_general(
        left, right, (((1,), (1,)), ((), ())), preferred_element_type=jnp.float32
    )


def contract_first(left, right):
    return lax.dot_general(
        left, right, (((0,), (0,)), ((), ())), preferred_element_type=jnp.float32
    )


def turn_segment(segment, cosine, sine_table):
    half_dims = cosine.shape[1]
    leading = segment[:, :half_dims]
    trailing = segment[:, half_dims : 2 * half_dims]
    return jnp.concatenate(
        [
            leading * cosine - trailing * sine_table,
            trailing * cosine + leading * sine_table,
            segment[:, 2 * half_dims :],
        ],
        axis=1,
    )


def rotate_heads(merged_block, positions):
    half_dims = ROT // 2
    freq_steps = jnp.arange(half_dims, dtype=jnp.float32)
    inverse = jnp.power(theta_base, -(2.0 * freq_steps) / ROT)
    angles = positions.astype(jnp.float32)[:, None] * inverse[None, :]
    cosine = jnp.cos(angles)
    sine_table = jnp.sin(angles)
    segments = []
    for head_index in range(merged_block.shape[1] // (3 * HEAD)):
        offset = 3 * head_index * HEAD
        segments.append(turn_segment(merged_block[:, offset : offset + HEAD], cosine, sine_table))
        segments.append(
            turn_segment(merged_block[:, offset + HEAD : offset + 2 * HEAD], cosine, sine_table)
        )
        segments.append(merged_block[:, offset + 2 * HEAD : offset + 3 * HEAD])
    return jnp.concatenate(segments, axis=1)


def visible_mask(query_pos, key_pos, seq_bounds):
    allowed = key_pos[None, :] <= query_pos[:, None]
    for piece_index in range(seq_bounds.shape[0]):
        lower_edge = seq_bounds[piece_index]
        inside_query = (query_pos >= lower_edge) & (query_pos < lower_edge + PIECE)
        inside_key = (key_pos >= lower_edge) & (key_pos < lower_edge + PIECE)
        allowed = allowed | inside_query[:, None] & inside_key[None, :]
    return allowed


def exact_gelu(values):
    return jax.nn.gelu(values, approximate=False)


def body(
    inputs,
    piece_starts,
    first_gain,
    first_shift,
    second_gain,
    second_shift,
    merged_weight,
    merged_bias,
    output_weight,
    output_bias,
    expand_weight,
    expand_bias,
    reduce_weight,
    reduce_bias,
    cotangent,
):
    micro_count = inputs.shape[0]
    own_tokens = inputs.shape[1]
    width_cols = inputs.shape[2]
    merged_cols = merged_weight.shape[1]
    attn_cols = output_weight.shape[0]
    head_count = merged_cols // (3 * HEAD)
    seq_count = piece_starts.shape[1]
    seq_rows = seq_count * L
    block_rows = min(512, L)
    score_scale = HEAD ** (-0.5)
    positions = jnp.arange(seq_rows, dtype=jnp.int32) % L
    token_pos = jnp.arange(L, dtype=jnp.int32)
    own_start = lax.axis_index("row") * own_tokens

    def rotate_local(block_in):
        return rotate_heads(block_in, positions)

    merged_whole, expand_whole, output_whole, reduce_whole = (
        lax.all_gather(merged_weight, "col", axis=0, tiled=True),
        lax.all_gather(expand_weight, "col", axis=0, tiled=True),
        lax.all_gather(output_weight, "col", axis=1, tiled=True),
        lax.all_gather(reduce_weight, "col", axis=1, tiled=True),
    )
    first_gain_acc = jnp.zeros(first_gain.shape, jnp.float32)
    first_shift_acc = jnp.zeros(first_shift.shape, jnp.float32)
    second_gain_acc = jnp.zeros(second_gain.shape, jnp.float32)
    second_shift_acc = jnp.zeros(second_shift.shape, jnp.float32)
    merged_w_acc = jnp.zeros(merged_weight.shape, jnp.float32)
    merged_b_acc = jnp.zeros(merged_bias.shape, jnp.float32)
    output_w_acc = jnp.zeros(output_weight.shape, jnp.float32)
    shift_out_acc = jnp.zeros(output_bias.shape, jnp.float32)
    expand_w_acc = jnp.zeros(expand_weight.shape, jnp.float32)
    expand_b_acc = jnp.zeros(expand_bias.shape, jnp.float32)
    reduce_w_acc = jnp.zeros(reduce_weight.shape, jnp.float32)
    results = []
    input_grads = []
    for micro_index in range(micro_count):
        local_rows = inputs[micro_index]
        gathered = lax.all_gather(local_rows, "row", axis=0, tiled=True)
        gathered_f = gathered.astype(jnp.float32)
        stat_sums = lax.psum(
            (jnp.sum(gathered_f, axis=1), jnp.sum(gathered_f * gathered_f, axis=1)), "col"
        )
        centers = stat_sums[0] / D
        inverse_std = lax.rsqrt(stat_sums[1] / D - centers * centers + norm_eps)
        normed = (gathered_f - centers[:, None]) * inverse_std[:, None]
        attend_in = (normed * first_gain + first_shift).astype(jnp.bfloat16)
        expand_in = (normed * second_gain + second_shift).astype(jnp.bfloat16)
        attend_seq, expand_seq = (
            lax.all_to_all(attend_in, "col", split_axis=0, concat_axis=1, tiled=True),
            lax.all_to_all(expand_in, "col", split_axis=0, concat_axis=1, tiled=True),
        )
        hidden = jnp.concatenate(
            [
                jnp.dot(attend_seq, merged_whole, preferred_element_type=jnp.float32),
                jnp.dot(expand_seq, expand_whole, preferred_element_type=jnp.float32),
            ],
            axis=1,
        )
        merged_pre = hidden[:, :merged_cols] + merged_bias
        expand_pre = hidden[:, merged_cols:] + expand_bias
        turned = rotate_local(merged_pre).astype(jnp.bfloat16)
        log_tables = []
        seq_index = 0
        seq_first = seq_index * L
        seq_bounds = piece_starts[micro_index, seq_index]
        head_outputs = []
        for head_index in range(head_count):
            offset = 3 * head_index * HEAD
            key_seq = turned[seq_first : seq_first + L, offset + HEAD : offset + 2 * HEAD]
            value_seq = turned[seq_first : seq_first + L, offset + 2 * HEAD : offset + 3 * HEAD]
            block_outputs = []
            block_logs = []
            for block_first in range(0, L, block_rows):
                query_blk = turned[
                    seq_first + block_first : seq_first + block_first + block_rows,
                    offset : offset + HEAD,
                ]
                visible = visible_mask(
                    token_pos[block_first : block_first + block_rows], token_pos, seq_bounds
                )
                scores = jnp.where(
                    visible, contract_last(query_blk, key_seq) * score_scale, -jnp.inf
                )
                row_max = jnp.max(scores, axis=1, keepdims=True)
                exp_scores = jnp.exp(scores - row_max)
                row_total = jnp.sum(exp_scores, axis=1, keepdims=True)
                prob_blk = (exp_scores / row_total).astype(jnp.bfloat16)
                block_outputs.append(
                    jnp.dot(prob_blk, value_seq, preferred_element_type=jnp.float32).astype(
                        jnp.bfloat16
                    )
                )
                block_logs.append(row_max[:, 0] + jnp.log(row_total[:, 0]))
            head_outputs.append(jnp.concatenate(block_outputs, axis=0))
            log_tables.append(block_logs)
        seq_outputs = jnp.concatenate(head_outputs, axis=1)
        activated = exact_gelu(expand_pre).astype(jnp.bfloat16)
        attn_all, act_all = (
            lax.all_gather(seq_outputs, "col", axis=0, tiled=True),
            lax.all_gather(activated, "col", axis=0, tiled=True),
        )
        attn_part = jnp.dot(attn_all, output_weight, preferred_element_type=jnp.float32)
        act_part = jnp.dot(act_all, reduce_weight, preferred_element_type=jnp.float32)
        branch_total = lax.psum_scatter(
            jnp.concatenate([attn_part, act_part], axis=1), "row", scatter_dimension=0, tiled=True
        )
        mixed_sum = branch_total[:, :width_cols] + branch_total[:, width_cols:]
        local_f = local_rows.astype(jnp.float32)
        results.append((local_f + mixed_sum + output_bias + reduce_bias).astype(jnp.bfloat16))
        grad_local = cotangent[micro_index]
        grad_all = lax.all_gather(grad_local, "row", axis=0, tiled=True)
        output_w_acc = output_w_acc + contract_first(attn_all, grad_all)
        reduce_w_acc = reduce_w_acc + contract_first(act_all, grad_all)
        shift_out_acc = shift_out_acc + jnp.sum(grad_all.astype(jnp.float32), axis=0)
        grad_seq = lax.all_to_all(grad_all, "col", split_axis=0, concat_axis=1, tiled=True)
        back_total = jnp.concatenate(
            [contract_last(grad_seq, output_whole), contract_last(grad_seq, reduce_whole)], axis=1
        )
        grad_mix = back_total[:, :attn_cols].astype(jnp.bfloat16)
        grad_act = back_total[:, attn_cols:]
        grad_expand = jax.vjp(exact_gelu, expand_pre)[1](grad_act)[0].astype(jnp.bfloat16)
        seq_index = 0
        seq_first = seq_index * L
        seq_bounds = piece_starts[micro_index, seq_index]
        head_grads = []
        for head_index in range(head_count):
            offset = 3 * head_index * HEAD
            query_seq = turned[seq_first : seq_first + L, offset : offset + HEAD]
            key_seq = turned[seq_first : seq_first + L, offset + HEAD : offset + 2 * HEAD]
            value_seq = turned[seq_first : seq_first + L, offset + 2 * HEAD : offset + 3 * HEAD]
            grad_part = grad_mix[
                seq_first : seq_first + L, head_index * HEAD : (head_index + 1) * HEAD
            ]
            log_list = log_tables[seq_index * head_count + head_index]
            query_grads = []
            key_grad = jnp.zeros((L, HEAD), jnp.float32)
            value_grad = jnp.zeros((L, HEAD), jnp.float32)
            for block_index, block_first in enumerate(range(0, L, block_rows)):
                query_blk = query_seq[block_first : block_first + block_rows]
                grad_blk = grad_part[block_first : block_first + block_rows]
                visible = visible_mask(
                    token_pos[block_first : block_first + block_rows], token_pos, seq_bounds
                )
                scores = jnp.where(
                    visible, contract_last(query_blk, key_seq) * score_scale, -jnp.inf
                )
                prob_full = jnp.exp(scores - log_list[block_index][:, None])
                grad_probs = contract_last(grad_blk, value_seq)
                delta_sum = jnp.sum(grad_probs * prob_full, axis=1, keepdims=True)
                grad_scores = (prob_full * (grad_probs - delta_sum)).astype(jnp.bfloat16)
                query_grads.append(
                    jnp.dot(grad_scores, key_seq, preferred_element_type=jnp.float32) * score_scale
                )
                key_grad = key_grad + contract_first(grad_scores, query_blk) * score_scale
                value_grad = value_grad + contract_first(prob_full.astype(jnp.bfloat16), grad_blk)
            head_grads.extend([jnp.concatenate(query_grads, axis=0), key_grad, value_grad])
        grad_segments = jnp.concatenate(head_grads, axis=1)
        grad_merged = jax.vjp(rotate_local, merged_pre)[1](grad_segments)[0].astype(jnp.bfloat16)
        merged_all, expand_all = (
            lax.all_gather(grad_merged, "col", axis=0, tiled=True),
            lax.all_gather(grad_expand, "col", axis=0, tiled=True),
        )
        merged_w_acc = merged_w_acc + contract_first(attend_in, merged_all)
        expand_w_acc = expand_w_acc + contract_first(expand_in, expand_all)
        merged_b_acc = merged_b_acc + jnp.sum(merged_all.astype(jnp.float32), axis=0)
        expand_b_acc = expand_b_acc + jnp.sum(expand_all.astype(jnp.float32), axis=0)
        part_attend = contract_last(merged_all, merged_weight)
        part_expand = contract_last(expand_all, expand_weight)
        norm_term = jnp.concatenate([part_attend, part_expand], axis=1)
        norm_back = lax.psum_scatter(
            norm_term.astype(jnp.bfloat16), "row", scatter_dimension=0, tiled=True
        ).astype(jnp.float32)
        own_normed = lax.dynamic_slice_in_dim(normed, own_start, own_tokens, 0)
        own_inverse = lax.dynamic_slice_in_dim(inverse_std, own_start, own_tokens, 0)
        grad_first = norm_back[:, :width_cols]
        grad_second = norm_back[:, width_cols:]
        first_gain_acc = first_gain_acc + jnp.sum(grad_first * own_normed, axis=0)
        first_shift_acc = first_shift_acc + jnp.sum(grad_first, axis=0)
        second_gain_acc = second_gain_acc + jnp.sum(grad_second * own_normed, axis=0)
        second_shift_acc = second_shift_acc + jnp.sum(grad_second, axis=0)
        grad_hat = grad_first * first_gain + grad_second * second_gain
        moments = lax.psum(
            (jnp.sum(grad_hat, axis=1), jnp.sum(grad_hat * own_normed, axis=1)), "col"
        )
        norm_part = grad_hat - moments[0][:, None] / D - own_normed * (moments[1][:, None] / D)
        input_grads.append(grad_local.astype(jnp.float32) + own_inverse[:, None] * norm_part)
    gain_totals = lax.psum(
        (first_gain_acc, first_shift_acc, second_gain_acc, second_shift_acc), "row"
    )
    return (
        jnp.stack(results),
        jnp.stack(input_grads),
        gain_totals[0],
        gain_totals[1],
        gain_totals[2],
        gain_totals[3],
        merged_w_acc,
        merged_b_acc,
        output_w_acc,
        shift_out_acc,
        expand_w_acc,
        expand_b_acc,
        reduce_w_acc,
        shift_out_acc,
    )


def solution(mesh):
    in_specs = (
        P(None, "row", "col"),
        P(None, "col", None),
        P("col"),
        P("col"),
        P("col"),
        P("col"),
        P("col", "row"),
        P("row"),
        P("row", "col"),
        P("col"),
        P("col", "row"),
        P("row"),
        P("row", "col"),
        P("col"),
        P(None, "row", "col"),
    )
    out_specs = (
        P(None, "row", "col"),
        P(None, "row", "col"),
        P("col"),
        P("col"),
        P("col"),
        P("col"),
        P("col", "row"),
        P("row"),
        P("row", "col"),
        P("col"),
        P("col", "row"),
        P("row"),
        P("row", "col"),
        P("col"),
    )
    return jax.shard_map(body, mesh=mesh, in_specs=in_specs, out_specs=out_specs, check_vma=False)
```

profile of v0, /device:TPU:0, one launch (start us, length us, event | category | flops | bytes accessed | tf_op | source)
XLA Modules:
  0.0 3325.2 jit_solution(10594196026653127666)
XLA Ops:
  16.6 49.2 %all-gather.45.cloned.1.call-done = bf16[1,8192,256]{1,2,0:T(8,128)(2,1)} async-done(((bf16[1,2048,256]{1,2,0:T(8,128)(2,1)}), bf16[1,8192,256]{1,2,0:T(8,128)(2,1)}) %all-gather.45.cloned.1.call-update) | async-done | bytes 4194320 | tf_op jit(solution)/shard_map/all_gather | solution.py:130
  69.3 51.0 %all-gather.47.cloned.1.call-done = bf16[1,8192,256]{1,2,0:T(8,128)(2,1)} async-done(((bf16[1,2048,256]{1,2,0:T(8,128)(2,1)}), bf16[1,8192,256]{1,2,0:T(8,128)(2,1)}) %all-gather.47.cloned.1.call-update) | async-done | bytes 4194320 | tf_op jit(solution)/shard_map/all_gather | solution.py:130
  128.2 46.5 %all-gather.51.cloned.1.call-done = bf16[1,8192,256]{1,2,0:T(8,128)(2,1)} async-done(((bf16[1,2048,256]{1,2,0:T(8,128)(2,1)}), bf16[1,8192,256]{1,2,0:T(8,128)(2,1)}) %all-gather.51.cloned.1.call-update) | async-done | bytes 4194320 | tf_op jit(solution)/shard_map/all_gather | solution.py:203
  190.9 38.1 %all-gather.49.cloned.1.call-done = bf16[1,8192,256]{1,2,0:T(8,128)(2,1)} async-done(((bf16[1,2048,256]{1,2,0:T(8,128)(2,1)}), bf16[1,8192,256]{1,2,0:T(8,128)(2,1)}) %all-gather.49.cloned.1.call-update) | async-done | bytes 4194320 | tf_op jit(solution)/shard_map/all_gather | solution.py:203
  239.8 45.7 %all-to-all-done.5 = bf16[8,1024,256]{1,2,0:T(8,128)(2,1)} async-done(((bf16[8,1024,256]{1,2,0:T(8,128)(2,1)}), bf16[8,1024,256]{1,2,0:T(8,128)(2,1)}, u32[]{:S(2)}, u32[]{:S(2)}) %all-to-all-start.5) | async-done | bytes 4194336 | tf_op jit(solution)/shard_map/all_to_all | solution.py:207
  290.1 21.5 all-reduce.41.cloned.1.call-done
  324.8 96.3 %all-to-all-done.4 = bf16[8,1024,256]{1,2,0:T(8,128)(2,1)} async-done(((bf16[8,1024,256]{1,2,0:T(8,128)(2,1)}), bf16[8,1024,256]{1,2,0:T(8,128)(2,1)}, u32[]{:S(2)}, u32[]{:S(2)}) %all-to-all-start.4) | async-done | bytes 4194336 | tf_op jit(solution)/shard_map/all_to_all | solution.py:207
  458.7 145.5 %all-to-all-done.2 = bf16[8,1024,256]{1,2,0:T(8,128)(2,1)} async-done(((bf16[8,1024,256]{1,2,0:T(8,128)(2,1)}), bf16[8,1024,256]{1,2,0:T(8,128)(2,1)}, u32[]{:S(2)}, u32[]{:S(2)}) %all-to-all-start.2) | async-done | bytes 4194336 | tf_op jit(solution)/shard_map/all_to_all | solution.py:141
  635.4 134.8 %all-to-all-done = bf16[8,1024,256]{1,2,0:T(8,128)(2,1)} async-done(((bf16[8,1024,256]{1,2,0:T(8,128)(2,1)}), bf16[8,1024,256]{1,2,0:T(8,128)(2,1)}, u32[]{:S(2)}, u32[]{:S(2)}) %all-to-all-start) | async-done | bytes 4194336 | tf_op jit(solution)/shard_map/all_to_all | solution.py:141
  830.1 200.9 %all-to-all-done.1 = bf16[8,1024,256]{1,2,0:T(8,128)(2,1)} async-done(((bf16[8,1024,256]{1,2,0:T(8,128)(2,1)}), bf16[8,1024,256]{1,2,0:T(8,128)(2,1)}, u32[]{:S(2)}, u32[]{:S(2)}) %all-to-all-start.1) | async-done | bytes 4194336 | tf_op jit(solution)/shard_map/all_to_all | solution.py:142
  1050.5 149.7 %all-to-all-done.3 = bf16[8,1024,256]{1,2,0:T(8,128)(2,1)} async-done(((bf16[8,1024,256]{1,2,0:T(8,128)(2,1)}), bf16[8,1024,256]{1,2,0:T(8,128)(2,1)}, u32[]{:S(2)}, u32[]{:S(2)}) %all-to-all-start.3) | async-done | bytes 4194336 | tf_op jit(solution)/shard_map/all_to_all | solution.py:142
  1215.2 33.6 %add_convert_fusion.1 = (bf16[1024,2048]{1,0:T(8,128)(2,1)}, f32[1024,2048]{1,0:T(8,128)}) fusion(f32[1024,2048]{1,0:T(8,128)} %fusion.302, f32[2048]{0:T(1024)S(1)} %copy-done.96, bf16[1024,2048]{0,1:T(8,128)(2,1)} %bitcast.20, bf16[2048,2048]{1,0:T(8,128)(2,1)} %all-gather.37.cloned.1.call-done), kind=kOutput, calls=%fused_computation.31 | convolution fusion | flops 8743026688 | bytes 33562624 | tf_op jit(solution)/shard_map/dot_general | solution.py:18
  1248.8 33.9 %add_convert_fusion = (bf16[1024,2048]{1,0:T(8,128)(2,1)}, f32[1024,2048]{1,0:T(8,128)}, bf16[1024,2048]{1,0:T(8,128)(2,1)}) fusion(f32[1024,2048]{1,0:T(8,128)S(1)} %copy-done.38, f32[2048]{0:T(1024)S(1)} %copy-done.96, f32[1024,2048]{1,0:T(8,128)} %get-tuple-element.92, f32[1024,2048]{1,0:T(8,128)} %fusion.302, bf16[1024,2048]{0,1:T(8,128)(2,1)} %bitcast.25, ...), kind=kOutput, calls=%fused_computation.30 | convolution fusion | flops 8751415296 | bytes 54534144 | tf_op jit(solution)/shard_map/dot_general | solution.py:18
  1338.6 230.9 %all-gather.43.cloned.1.call-done = bf16[8192,2048]{1,0:T(8,128)(2,1)} async-done(((bf16[1024,2048]{1,0:T(8,128)(2,1)}), bf16[8192,2048]{1,0:T(8,128)(2,1)}) %all-gather.43.cloned.1.call-update) | async-done | bytes 33554448 | tf_op jit(solution)/shard_map/all_gather | solution.py:253
  1569.5 19.6 convolution_convert_fusion.2
  1597.1 191.9 %all-gather.35.cloned.1.call-done = bf16[8192,1536]{0,1:T(8,128)(2,1)} async-done(((bf16[1024,1536]{0,1:T(8,128)(2,1)}), bf16[8192,1536]{0,1:T(8,128)(2,1)}) %all-gather.35.cloned.1.call-update) | async-done | bytes 25165840 | tf_op jit(solution)/shard_map/all_gather | solution.py:252
  1806.4 271.0 %all-gather.39.cloned.1.call-done = bf16[8192,2048]{1,0:T(8,128)(2,1)} async-done(((bf16[1024,2048]{1,0:T(8,128)(2,1)}), bf16[8192,2048]{1,0:T(8,128)(2,1)}) %all-gather.39.cloned.1.call-update) | async-done | bytes 33554448 | tf_op jit(solution)/shard_map/all_gather | solution.py:253
  2103.9 55.8 %all-gather.23.cloned.1.call-done = bf16[8192,512]{1,0:T(8,128)(2,1)} async-done(((bf16[1024,512]{1,0:T(8,128)(2,1)}), bf16[8192,512]{1,0:T(8,128)(2,1)}) %all-gather.23.cloned.1.call-update) | async-done | bytes 8388624 | tf_op jit(solution)/shard_map/all_gather | solution.py:191
  2169.7 278.5 %all-gather.27.cloned.1.call-done = bf16[8192,2048]{1,0:T(8,128)(2,1)} async-done(((bf16[1024,2048]{1,0:T(8,128)(2,1)}), bf16[8192,2048]{1,0:T(8,128)(2,1)}) %all-gather.27.cloned.1.call-update) | async-done | bytes 33554448 | tf_op jit(solution)/shard_map/all_gather | solution.py:192
  2479.6 51.0 %all-gather.29.cloned.1.call-done = bf16[8192,512]{1,0:T(8,128)(2,1)} async-done(((bf16[1024,512]{1,0:T(8,128)(2,1)}), bf16[8192,512]{1,0:T(8,128)(2,1)}) %all-gather.29.cloned.1.call-update) | async-done | bytes 8388624 | tf_op jit(solution)/shard_map/all_gather | solution.py:191
  2540.6 278.5 %all-gather.31.cloned.1.call-done = bf16[8192,2048]{1,0:T(8,128)(2,1)} async-done(((bf16[1024,2048]{1,0:T(8,128)(2,1)}), bf16[8192,2048]{1,0:T(8,128)(2,1)}) %all-gather.31.cloned.1.call-update) | async-done | bytes 33554448 | tf_op jit(solution)/shard_map/all_gather | solution.py:192
  3038.0 26.3 all-reduce.36
  3088.9 64.0 %reduce-scatter.5.cloned.1.call-done = f32[2048,512]{0,1:T(8,128)} async-done(((f32[8192,512]{0,1:T(8,128)}), f32[2048,512]{0,1:T(8,128)}) %reduce-scatter.5.cloned.1.call-update) | async-done | bytes 4194320 | tf_op jit(solution)/shard_map/reduce_scatter | solution.py:196
  3152.9 156.9 %reduce-scatter.7.cloned.1.call-done = f32[2048,512]{0,1:T(8,128)} async-done(((f32[8192,512]{0,1:T(8,128)}), f32[2048,512]{0,1:T(8,128)}) %reduce-scatter.7.cloned.1.call-update) | async-done | bytes 4194320 | tf_op jit(solution)/shard_map/reduce_scatter | solution.py:196
  (545 shorter events, 634.5 us)
Async XLA Ops:
  11.9 162.8 %all-gather.51.cloned.1.call-start = ((), (), s32[]{:S(2)}) async-start(), calls=%async_computation.29 | async-start | bytes 5242880 | tf_op jit(solution)/shard_map/all_gather | solution.py:203
  15.1 213.9 %all-gather.49.cloned.1.call-start = ((), (), s32[]{:S(2)}) async-start(), calls=%async_computation.28 | async-start | bytes 5242880 | tf_op jit(solution)/shard_map/all_gather | solution.py:203
  16.6 295.1 %all-reduce.41.cloned.1.call-start = ((), (), s32[]{:S(2)}) async-start(), calls=%async_computation.30 | async-start | bytes 262144 | tf_op jit(solution)/shard_map/psum | solution.py:132
  126.9 320.4 %all-gather.33.cloned.1.call-start = ((), (), s32[]{:S(2)}) async-start(), calls=%async_computation.18 | async-start | bytes 2359296 | tf_op jit(solution)/shard_map/all_gather | solution.py:112
  127.5 481.5 %all-gather.21.cloned.1.call-start = ((), (), s32[]{:S(2)}) async-start(), calls=%async_computation.10 | async-start | bytes 7077888 | tf_op jit(solution)/shard_map/all_gather | solution.py:110
  190.2 845.5 %all-gather.25.cloned.1.call-start = ((), (), s32[]{:S(2)}) async-start(), calls=%async_computation.12 | async-start | bytes 9437184 | tf_op jit(solution)/shard_map/all_gather | solution.py:111
  285.6 135.5 %all-to-all-start.4 = ((bf16[8,1024,256]{1,2,0:T(8,128)(2,1)}), bf16[8,1024,256]{1,2,0:T(8,128)(2,1)}, u32[]{:S(2)}, u32[]{:S(2)}) async-start(bf16[8,1024,256]{1,2,0:T(8,128)(2,1)} %copy.72), calls=%async_computation.6 | async-start | bytes 8388608 | tf_op jit(solution)/shard_map/all_to_all | solution.py:207
  421.1 183.1 %all-to-all-start.2 = ((bf16[8,1024,256]{1,2,0:T(8,128)(2,1)}), bf16[8,1024,256]{1,2,0:T(8,128)(2,1)}, u32[]{:S(2)}, u32[]{:S(2)}) async-start(bf16[8,1024,256]{1,2,0:T(8,128)(2,1)} %bitcast.193), calls=%async_computation.3 | async-start | bytes 8388608 | tf_op jit(solution)/shard_map/all_to_all | solution.py:141
  425.9 789.2 %all-gather.37.cloned.1.call-start = ((), (), s32[]{:S(2)}) async-start(), calls=%async_computation.20 | async-start | bytes 9437184 | tf_op jit(solution)/shard_map/all_gather | solution.py:113
  604.1 166.1 %all-to-all-start = ((bf16[8,1024,256]{1,2,0:T(8,128)(2,1)}), bf16[8,1024,256]{1,2,0:T(8,128)(2,1)}, u32[]{:S(2)}, u32[]{:S(2)}) async-start(bf16[8,1024,256]{1,2,0:T(8,128)(2,1)} %bitcast.192), calls=%async_computation | async-start | bytes 8388608 | tf_op jit(solution)/shard_map/all_to_all | solution.py:141
  608.9 712.5 %all-gather.41.cloned.1.call-start = ((), (), s32[]{:S(2)}) async-start(), calls=%async_computation.23 | async-start | bytes 28311552 | tf_op jit(solution)/shard_map/all_gather | solution.py:252
  819.9 211.1 %all-to-all-start.1 = ((bf16[8,1024,256]{1,2,0:T(8,128)(2,1)}), bf16[8,1024,256]{1,2,0:T(8,128)(2,1)}, u32[]{:S(2)}, u32[]{:S(2)}) async-start(bf16[8,1024,256]{1,2,0:T(8,128)(2,1)} %bitcast.195), calls=%async_computation.1 | async-start | bytes 8388608 | tf_op jit(solution)/shard_map/all_to_all | solution.py:142
  1031.0 169.2 %all-to-all-start.3 = ((bf16[8,1024,256]{1,2,0:T(8,128)(2,1)}), bf16[8,1024,256]{1,2,0:T(8,128)(2,1)}, u32[]{:S(2)}, u32[]{:S(2)}) async-start(bf16[8,1024,256]{1,2,0:T(8,128)(2,1)} %bitcast.194), calls=%async_computation.4 | async-start | bytes 8388608 | tf_op jit(solution)/shard_map/all_to_all | solution.py:142
  1035.6 533.9 %all-gather.43.cloned.1.call-start = ((), (), s32[]{:S(2)}) async-start(), calls=%async_computation.24 | async-start | bytes 37748736 | tf_op jit(solution)/shard_map/all_gather | solution.py:253
  1282.8 506.2 %all-gather.35.cloned.1.call-start = ((), (), s32[]{:S(2)}) async-start(), calls=%async_computation.19 | async-start | bytes 28311552 | tf_op jit(solution)/shard_map/all_gather | solution.py:252
  1291.9 785.5 %all-gather.39.cloned.1.call-start = ((), (), s32[]{:S(2)}) async-start(), calls=%async_computation.21 | async-start | bytes 37748736 | tf_op jit(solution)/shard_map/all_gather | solution.py:253
  1292.7 867.0 %all-gather.23.cloned.1.call-start = ((), (), s32[]{:S(2)}) async-start(), calls=%async_computation.11 | async-start | bytes 9437184 | tf_op jit(solution)/shard_map/all_gather | solution.py:191
  1302.1 1146.1 %all-gather.27.cloned.1.call-start = ((), (), s32[]{:S(2)}) async-start(), calls=%async_computation.13 | async-start | bytes 37748736 | tf_op jit(solution)/shard_map/all_gather | solution.py:192
  1302.8 1227.8 %all-gather.29.cloned.1.call-start = ((), (), s32[]{:S(2)}) async-start(), calls=%async_computation.15 | async-start | bytes 9437184 | tf_op jit(solution)/shard_map/all_gather | solution.py:191
  1310.7 1508.4 %all-gather.31.cloned.1.call-start = ((), (), s32[]{:S(2)}) async-start(), calls=%async_computation.16 | async-start | bytes 37748736 | tf_op jit(solution)/shard_map/all_gather | solution.py:192
  1320.9 1704.2 %reduce-scatter.11.cloned.1.call-start = ((), (), s32[]{:S(2)}) async-start(), calls=%async_computation.25 | async-start | bytes 10485760 | tf_op jit(solution)/shard_map/reduce_scatter | solution.py:262
  1596.9 1432.6 %reduce-scatter.9.cloned.1.call-start = ((), (), s32[]{:S(2)}) async-start(), calls=%async_computation.22 | async-start | bytes 10485760 | tf_op jit(solution)/shard_map/reduce_scatter | solution.py:262
  2103.8 1049.1 %reduce-scatter.5.cloned.1.call-start = ((), (), s32[]{:S(2)}) async-start(), calls=%async_computation.14 | async-start | bytes 20971520 | tf_op jit(solution)/shard_map/reduce_scatter | solution.py:196
  2479.1 830.6 %reduce-scatter.7.cloned.1.call-start = ((), (), s32[]{:S(2)}) async-start(), calls=%async_computation.17 | async-start | bytes 20971520 | tf_op jit(solution)/shard_map/reduce_scatter | solution.py:196
  (151 other events, 3392.3 us)
Sparse Core Ops, SparseCore 0:
  10.5 55.2 all-gather.44
  67.6 52.5 all-gather.46
  122.1 52.5 all-gather.50
  176.4 52.5 all-gather.48
  232.5 79.0 all-reduce.40
  313.1 71.1 all-gather.32
  385.9 101.5 all-gather.20
  489.1 122.0 all-gather.24
  612.8 155.3 all-gather.36
  815.2 397.1 all-gather.40
  1282.9 286.5 all-gather.42
  1570.9 218.0 all-gather.34
  1790.6 286.7 all-gather.38
  2079.4 80.2 all-gather.22
  2161.1 287.0 all-gather.26
  2450.3 80.2 all-gather.28
  2532.0 287.0 all-gather.30
  2822.0 84.4 reduce-scatter.10
  2909.6 86.3 reduce-scatter.8
  2998.9 153.9 reduce-scatter.4
  3156.0 153.7 reduce-scatter.6
where the time goes:
time: 3330 us
  waiting for transfers between devices  2560 us (77%)
  matrix products  405 us (12%)
  other arithmetic  189 us (6%)
  local copies, waits for them, and re-layouts  82.4 us (2%)
  blocking collectives  37 us (1%)
    all_gather x2, waiting for transfers between devices, body(): lax.all_gather(activated, 'col', axis=0, tiled=True)  557 us
    all_gather x2, waiting for transfers between devices, body(): lax.all_gather(grad_expand, 'col', axis=0, tiled=True)  502 us
    all_to_all x2, waiting for transfers between devices, body(): lax.all_to_all(expand_in, 'col', split_axis=0, concat_axis=1, tiled=True)  351 us
    all_to_all x2, waiting for transfers between devices, body(): lax.all_to_all(attend_in, 'col', split_axis=0, concat_axis=1, tiled=True)  280 us
    reduce_scatter x2, waiting for transfers between devices, body(): lax.psum_scatter(jnp.concatenate([attn_part, act_part], axis=1), 'row', s...  221 us
    all_gather x2, waiting for transfers between devices, body(): lax.all_gather(grad_merged, 'col', axis=0, tiled=True)  192 us
    dot_general x24, matrix products, contract_last(): lax.dot_general(left, right, (((1,), (1,)), ((), ())), preferred_element_...  165 us
    all_to_all x2, waiting for transfers between devices, body(): lax.all_to_all(grad_all, 'col', split_axis=0, concat_axis=1, tiled=True)  142 us
  transfers between devices with their start and end apart: 27, of which 20 were waited for; matrix products, arithmetic and copies ran while one was open for 19% of the time, Pallas kernels for 0%

commit v1 on v0

v1 whole, which is shorter than its diff:
```python
import jax
import jax.numpy as jnp
from jax import lax
from jax.sharding import PartitionSpec as P

D = 2048
HEAD = 256
ROT = 64
L = 1024
PIECE = 256
HALF_SEQ = 512

norm_eps = 1e-05
theta_base = 10000.0
BF = jnp.bfloat16
F32 = jnp.float32


def mm(left, right):
    return jnp.dot(left, right, preferred_element_type=F32)


def contract_last(left, right):
    return lax.dot_general(left, right, (((1,), (1,)), ((), ())), preferred_element_type=F32)


def contract_first(left, right):
    return lax.dot_general(left, right, (((0,), (0,)), ((), ())), preferred_element_type=F32)


def rotary_tables():
    half_dims = ROT // 2
    freq_steps = jnp.arange(half_dims, dtype=F32)
    inverse = jnp.power(theta_base, -(2.0 * freq_steps) / ROT)
    angles = jnp.arange(L, dtype=jnp.int32).astype(F32)[:, None] * inverse[None, :]
    return jnp.cos(angles), jnp.sin(angles)


def turn(segment, cosine, sine):
    half_dims = ROT // 2
    leading = segment[:, :half_dims]
    trailing = segment[:, half_dims:ROT]
    return jnp.concatenate(
        [leading * cosine - trailing * sine, trailing * cosine + leading * sine, segment[:, ROT:]],
        axis=1,
    )


def visible_mask(query_pos, key_pos, seq_bounds):
    allowed = key_pos[None, :] <= query_pos[:, None]
    for piece_index in range(seq_bounds.shape[0]):
        lower = seq_bounds[piece_index]
        inside_query = (query_pos >= lower) & (query_pos < lower + PIECE)
        inside_key = (key_pos >= lower) & (key_pos < lower + PIECE)
        allowed = allowed | inside_query[:, None] & inside_key[None, :]
    return allowed


def body(
    inputs,
    piece_starts,
    first_gain,
    first_shift,
    second_gain,
    second_shift,
    merged_weight,
    merged_bias,
    output_weight,
    output_bias,
    expand_weight,
    expand_bias,
    reduce_weight,
    reduce_bias,
    cotangent,
):
    rows = lax.axis_size("row")
    cols = lax.axis_size("col")
    micro, own_tokens, width = inputs.shape
    per_row = own_tokens // L
    part = L // rows
    heads = merged_weight.shape[1] // (3 * HEAD)
    scale = HEAD ** (-0.5)
    cosine, sine = rotary_tables()

    def to_rows(block):
        b = block.reshape(micro, per_row, rows, part, width).transpose(2, 1, 0, 3, 4)
        b = lax.all_to_all(b, "row", split_axis=0, concat_axis=0, tiled=True)
        b = b.reshape(rows * per_row, micro, part, width)
        b = lax.all_to_all(b, "col", split_axis=0, concat_axis=0, tiled=True)
        return b.transpose(1, 2, 0, 3).reshape(micro, part, cols * width)

    def from_rows(block):
        b = block.reshape(micro, part, cols, width).transpose(2, 0, 1, 3)
        b = lax.all_to_all(b, "col", split_axis=0, concat_axis=0, tiled=True)
        b = b.reshape(rows, per_row, micro, part, width)
        b = lax.all_to_all(b, "row", split_axis=0, concat_axis=0, tiled=True)
        return b.transpose(2, 1, 0, 3, 4).reshape(micro, own_tokens, width)

    def whole_seq(part_rows):
        return lax.all_gather(part_rows, "row", axis=1, tiled=True).reshape(micro * L, D)

    def norm(block):
        block = block.astype(F32)
        center = jnp.mean(block, axis=-1, keepdims=True)
        spread = jnp.mean((block - center) ** 2, axis=-1, keepdims=True)
        inverse_std = lax.rsqrt(spread + norm_eps)
        return (block - center) * inverse_std, inverse_std

    gains = lax.all_gather(
        jnp.stack([first_gain, first_shift, second_gain, second_shift]), "col", axis=1, tiled=True
    )
    x_part = to_rows(inputs)
    x_seq = whole_seq(x_part)
    merged_w = lax.all_gather(merged_weight, "col", axis=0, tiled=True)
    expand_w = lax.all_gather(expand_weight, "col", axis=0, tiled=True)
    cot_part = to_rows(cotangent)
    cot_seq = whole_seq(cot_part)
    reduce_w = lax.all_gather(reduce_weight, "col", axis=1, tiled=True)
    output_w = lax.all_gather(output_weight, "col", axis=1, tiled=True)

    normed, _ = norm(x_seq)
    attend_in = (normed * gains[0] + gains[1]).astype(BF)
    expand_in = (normed * gains[2] + gains[3]).astype(BF)

    expand_pre = mm(expand_in, expand_w) + expand_bias
    activated = jax.nn.gelu(expand_pre, approximate=False).astype(BF)
    grad_act = contract_last(cot_seq, reduce_w)
    gelu = lambda v: jax.nn.gelu(v, approximate=False)
    grad_pre = jax.vjp(gelu, expand_pre)[1](grad_act)[0].astype(BF)

    def scatter_weight(grad):
        return lax.psum_scatter(grad.astype(BF), "col", scatter_dimension=0, tiled=True).astype(F32)

    reduce_grad = scatter_weight(contract_first(cot_seq, activated)).T
    expand_grad = scatter_weight(contract_first(expand_in, grad_pre))

    merged_pre = mm(attend_in, merged_w) + merged_bias
    grad_mix = contract_last(cot_seq, output_w).astype(BF)
    token_pos = jnp.arange(L, dtype=jnp.int32)
    mixes = []
    grads = []
    for m in range(micro):
        bounds = piece_starts[m, 0]
        seq_mix = []
        seq_grads = []
        for h in range(heads):
            rows_m = slice(m * L, (m + 1) * L)
            base = 3 * h * HEAD
            query = turn(merged_pre[rows_m, base : base + HEAD], cosine, sine).astype(BF)
            key = turn(merged_pre[rows_m, base + HEAD : base + 2 * HEAD], cosine, sine).astype(BF)
            value = merged_pre[rows_m, base + 2 * HEAD : base + 3 * HEAD].astype(BF)
            gm = grad_mix[rows_m, h * HEAD : (h + 1) * HEAD]
            outs = []
            gq = []
            gk = jnp.zeros((L, HEAD), F32)
            gv = jnp.zeros((L, HEAD), F32)
            for first in range(0, L, HALF_SEQ):
                last = first + HALF_SEQ
                q, k, v, g = query[first:last], key[:last], value[:last], gm[first:last]
                mask = visible_mask(token_pos[first:last], token_pos[:last], bounds)
                scores = jnp.where(mask, contract_last(q, k) * scale, -jnp.inf)
                top = jnp.max(scores, axis=1, keepdims=True)
                es = jnp.exp(scores - top)
                probs = es / jnp.sum(es, axis=1, keepdims=True)
                pb = probs.astype(BF)
                outs.append(mm(pb, v).astype(BF))
                gp = contract_last(g, v)
                delta = jnp.sum(gp * probs, axis=1, keepdims=True)
                gs = (probs * (gp - delta)).astype(BF)
                gq.append(mm(gs, k) * scale)
                pad = ((0, L - last), (0, 0))
                gk = gk + jnp.pad(contract_first(gs, q) * scale, pad)
                gv = gv + jnp.pad(contract_first(pb, g), pad)
            seq_mix.append(jnp.concatenate(outs, axis=0))
            gq = jnp.concatenate(gq, axis=0)
            seq_grads += [turn(gq, cosine, -sine), turn(gk, cosine, -sine), gv]
        mixes.append(jnp.concatenate(seq_mix, axis=1))
        grads.append(jnp.concatenate(seq_grads, axis=1).astype(BF))
    mix = jnp.concatenate(mixes, axis=0)
    grad_merged = jnp.concatenate(grads, axis=0)

    branch = mm(mix, output_w) + mm(activated, reduce_w)
    branch = branch.astype(BF).reshape(micro, L, D)
    branch = lax.psum_scatter(branch, "row", scatter_dimension=1, tiled=True)
    branch = from_rows(branch)
    result = inputs.astype(F32) + branch.astype(F32) + output_bias + reduce_bias
    result = result.astype(BF)

    output_grad = scatter_weight(contract_first(cot_seq, mix)).T
    merged_grad = scatter_weight(contract_first(attend_in, grad_merged))

    grad_first = contract_last(grad_merged, merged_w)
    grad_second = contract_last(grad_pre, expand_w)
    norm_sums = jnp.stack(
        [
            jnp.sum(grad_first * normed, axis=0),
            jnp.sum(grad_first, axis=0),
            jnp.sum(grad_second * normed, axis=0),
            jnp.sum(grad_second, axis=0),
        ]
    )
    grad_hat = (grad_first * gains[0] + grad_second * gains[2]).astype(BF).reshape(micro, L, D)
    grad_hat = lax.psum_scatter(grad_hat, "row", scatter_dimension=1, tiled=True).astype(F32)
    part_normed, part_inverse = norm(x_part)
    norm_part = part_inverse * (
        grad_hat
        - jnp.mean(grad_hat, axis=-1, keepdims=True)
        - part_normed * jnp.mean(grad_hat * part_normed, axis=-1, keepdims=True)
    )
    input_grad = cotangent.astype(F32) + from_rows(norm_part.astype(BF)).astype(F32)

    norm_sums = lax.psum(lax.psum_scatter(norm_sums, "col", scatter_dimension=1, tiled=True), "row")
    merged_b = lax.psum(jnp.sum(grad_merged.astype(F32), axis=0), "col")
    expand_b = lax.psum(jnp.sum(grad_pre.astype(F32), axis=0), "col")
    shift_b = lax.psum(jnp.sum(cotangent.astype(F32), axis=(0, 1)), "row")
    return (
        result,
        input_grad,
        norm_sums[0],
        norm_sums[1],
        norm_sums[2],
        norm_sums[3],
        merged_grad,
        merged_b,
        output_grad,
        shift_b,
        expand_grad,
        expand_b,
        reduce_grad,
        shift_b,
    )


def solution(mesh):
    in_specs = (
        P(None, "row", "col"),
        P(None, "col", None),
        P("col"),
        P("col"),
        P("col"),
        P("col"),
        P("col", "row"),
        P("row"),
        P("row", "col"),
        P("col"),
        P("col", "row"),
        P("row"),
        P("row", "col"),
        P("col"),
        P(None, "row", "col"),
    )
    out_specs = (
        P(None, "row", "col"),
        P(None, "row", "col"),
        P("col"),
        P("col"),
        P("col"),
        P("col"),
        P("col", "row"),
        P("row"),
        P("row", "col"),
        P("col"),
        P("col", "row"),
        P("row"),
        P("row", "col"),
        P("col"),
    )
    return jax.shard_map(body, mesh=mesh, in_specs=in_specs, out_specs=out_specs, check_vma=False)
```

time: 3330 us -> 1260 us (0.38)
  waiting for transfers between devices: 2560 us -> 463 us
  blocking collectives: 37 us -> 240 us
  other arithmetic: 189 us -> 90.1 us
  matrix products: 405 us -> 340 us
    all_gather x16 -> x6, waiting for transfers between devices: 1540 us -> 154 us  [the longest x1 58.2 us: body(): reduce_w = lax.all_gather(reduce_weight, 'col', axis=1, tiled=True)]
    all_to_all x6 -> x4, waiting for transfers between devices: 773 us -> 115 us  [the longest x2 115 us: from_rows(): b = lax.all_to_all(b, 'col', split_axis=0, concat_axis=0, tiled=True)]
    all_to_all x0 -> x4, blocking collectives: none -> 185 us  [the longest x2 105 us: to_rows(): b = lax.all_to_all(b, 'col', split_axis=0, concat_axis=0, tiled=True)]
    reduce_sum x19 -> x15, other arithmetic: 78.8 us -> 25.4 us  [the longest x2 7.37 us: norm(): center = jnp.mean(block, axis=-1, keepdims=True)]
    concatenate x18 -> x4, other arithmetic: 42.2 us -> 0.15 us  [turn(): jnp.concatenate([leading * cosine - trailing * sine, trailing * cosine +...]
    unnamed x297 -> x285, local copies, waits for them, and re-layouts: 50.5 us -> 14.7 us
    dot_general x24 -> x20, matrix products: 120 us -> 86.9 us  [contract_first(): lax.dot_general(left, right, (((0,), (0,)), ((), ())), preferred_element_...]
    reduce_scatter x4 -> x6, waiting for transfers between devices: 221 us -> 191 us  [the longest x4 191 us: scatter_weight(): lax.psum_scatter(grad.astype(BF), 'col', scatter_dimension=0, tiled=True)]
  transfers between devices with their start and end apart: 27 -> 17, of which waited for: 20 -> 10; matrix products, arithmetic and copies ran while one was open for 19% -> 30% of each run, Pallas kernels for 0% -> 0%
where the time goes in v1:
time: 1260 us; the launch traced here: 1250 us
  waiting for transfers between devices  463 us (37%)
  matrix products  340 us (27%)
  blocking collectives  240 us (19%)
  other arithmetic  90.1 us (7%)
  local copies, waits for them, and re-layouts  86.9 us (7%)
  between operations  18.9 us (1%)
  starting transfers between devices  16.5 us (1%)
    reduce_scatter x4, waiting for transfers between devices, scatter_weight(): lax.psum_scatter(grad.astype(BF), 'col', scatter_dimension=0, tiled=True)  191 us
    dot_general x20, matrix products, contract_last(): lax.dot_general(left, right, (((1,), (1,)), ((), ())), preferred_element_...  148 us
    all_to_all x2, waiting for transfers between devices, from_rows(): b = lax.all_to_all(b, 'col', split_axis=0, concat_axis=0, tiled=True)  115 us
    all_to_all x2, blocking collectives, to_rows(): b = lax.all_to_all(b, 'col', split_axis=0, concat_axis=0, tiled=True)  105 us
    dot_general x20, matrix products, mm(): return jnp.dot(left, right, preferred_element_type=F32)  104 us
    dot_general x20, matrix products, contract_first(): lax.dot_general(left, right, (((0,), (0,)), ((), ())), preferred_element_...  86.9 us
    all_to_all x2, blocking collectives, to_rows(): b = lax.all_to_all(b, 'row', split_axis=0, concat_axis=0, tiled=True)  79.5 us
    all_gather x1, waiting for transfers between devices, body(): reduce_w = lax.all_gather(reduce_weight, 'col', axis=1, tiled=True)  58.2 us
  transfers between devices with their start and end apart: 17, of which 10 were waited for; matrix products, arithmetic and copies ran while one was open for 30% of the time, Pallas kernels for 0%

profile of v1, /device:TPU:0, one launch (start us, length us, event | category | flops | bytes accessed | tf_op | source)
XLA Modules:
  0.0 1254.6 jit_solution(38191921361162565)
XLA Ops:
  9.0 30.4 %all_to_all.40 = bf16[4,2,2,256,256]{4,3,1,2,0:T(8,128)(2,1)S(1)} all-to-all(bf16[4,2,2,256,256]{4,3,1,2,0:T(8,128)(2,1)S(1)} %copy.66), channel_id=1, replica_groups=mesh['row'=4,'col'=8] {'row'}, dimensions={0} | all-to-all | bytes 4194304 | tf_op jit(solution)/shard_map/all_to_all | solution.py:87
  39.5 53.7 %all_to_all.41 = bf16[8,2,256,256]{3,2,1,0:T(8,128)(2,1)S(1)} all-to-all(bf16[8,2,256,256]{3,2,1,0:T(8,128)(2,1)S(1)} %bitcast.142), channel_id=1, replica_groups=mesh['row'=4,'col'=8] {'col'}, dimensions={0} | all-to-all | bytes 4194304 | tf_op jit(solution)/shard_map/all_to_all | solution.py:89
  98.4 49.2 %all_to_all.42 = bf16[4,2,2,256,256]{4,3,1,2,0:T(8,128)(2,1)S(1)} all-to-all(bf16[4,2,2,256,256]{4,3,1,2,0:T(8,128)(2,1)S(1)} %copy.74), channel_id=1, replica_groups=mesh['row'=4,'col'=8] {'row'}, dimensions={0} | all-to-all | bytes 4194304 | tf_op jit(solution)/shard_map/all_to_all | solution.py:87
  147.8 51.5 %all_to_all.43 = bf16[8,2,256,256]{3,2,1,0:T(8,128)(2,1)S(1)} all-to-all(bf16[8,2,256,256]{3,2,1,0:T(8,128)(2,1)S(1)} %bitcast.143), channel_id=1, replica_groups=mesh['row'=4,'col'=8] {'col'}, dimensions={0} | all-to-all | bytes 4194304 | tf_op jit(solution)/shard_map/all_to_all | solution.py:89
  266.0 19.3 %fusion.334 = (bf16[2048,1536]{0,1:T(8,128)(2,1)S(1)}, f32[2048,1536]{0,1:T(8,128)}) fusion(f32[1536]{0:T(1024)S(1)} %copy-done.127, bf16[2048,2048]{1,0:T(8,128)(2,1)} %get-tuple-element.29, bf16[2048,1536]{1,0:T(8,128)(2,1)} %all-gather.9.cloned.1.call-done), kind=kOutput, calls=%fused_computation.489 | convolution fusion | flops 12891193344 | bytes 33560576 | tf_op jit(solution)/shard_map/dot_general | solution.py:20
  308.1 46.2 %all-gather.17.cloned.1.call-done = bf16[2,1024,2048]{1,2,0:T(8,128)(2,1)} async-done(((bf16[2,256,2048]{1,2,0:T(8,128)(2,1)}), bf16[2,1024,2048]{1,2,0:T(8,128)(2,1)}) %all-gather.17.cloned.1.call-update) | async-done | bytes 8388624 | tf_op jit(solution)/shard_map/all_gather | solution.py:100
  366.5 20.0 %all-gather.11.cloned.1.call-done = bf16[512,2048]{1,0:T(8,128)(2,1)} async-done(((bf16[512,256]{1,0:T(8,128)(2,1)}), bf16[512,2048]{1,0:T(8,128)(2,1)}) %all-gather.11.cloned.1.call-update) | async-done | bytes 2097168 | tf_op jit(solution)/shard_map/all_gather | solution.py:119
  442.3 26.7 %all-gather.13.cloned.1.call-done = bf16[2048,2048]{1,0:T(8,128)(2,1)} async-done(((bf16[256,2048]{1,0:T(8,128)(2,1)}), bf16[2048,2048]{1,0:T(8,128)(2,1)}) %all-gather.13.cloned.1.call-update) | async-done | bytes 8388624 | tf_op jit(solution)/shard_map/all_gather | solution.py:115
  469.0 24.2 %fusion.343 = f32[2048,2048]{1,0:T(8,128)} fusion(bf16[2048,2048]{1,0:T(8,128)(2,1)} %get-tuple-element.28, bf16[2048,2048]{1,0:T(8,128)(2,1)} %all-gather.13.cloned.1.call-done), kind=kOutput, calls=%fused_computation.498 | convolution fusion | flops 17179869184 | bytes 33554432 | tf_op jit(solution)/shard_map/dot_general | solution.py:20
  493.2 58.2 %all-gather.15.cloned.1.call-done = bf16[2048,2048]{1,0:T(8,128)(2,1)} async-done(((bf16[2048,256]{1,0:T(8,128)(2,1)}), bf16[2048,2048]{1,0:T(8,128)(2,1)}) %all-gather.15.cloned.1.call-update) | async-done | bytes 8388624 | tf_op jit(solution)/shard_map/all_gather | solution.py:118
  551.4 64.0 %convert_reduce_fusion = (f32[2048]{0:T(1024)}, bf16[2048,2048]{1,0:T(8,128)(2,1)}, f32[2048,2048]{1,0:T(8,128)}) fusion(f32[2048,2048]{1,0:T(8,128)} %fusion.343, f32[2048]{0:T(1024)S(1)} %copy-done.102, bf16[2048,2048]{1,0:T(8,128)(2,1)} %bitcast.133, bf16[2048,2048]{1,0:T(8,128)(2,1)} %all-gather.15.cloned.1.call-done), kind=kOutput, calls=%fused_computation.4 | convolution fusion | flops 17494439936 | bytes 58736640 | tf_op jit(solution)/shard_map/dot_general | solution.py:24
  615.5 22.2 %fusion.344 = f32[2048,2048]{1,0:T(8,128)} fusion(bf16[2048,2048]{1,0:T(8,128)(2,1)} %get-tuple-element.25, bf16[2048,2048]{1,0:T(8,128)(2,1)S(1)} %copy-done.125), kind=kOutput, calls=%fused_computation.499 | convolution fusion | flops 17179869184 | bytes 33554432 | tf_op jit(solution)/shard_map/dot_general | solution.py:24
  637.7 25.3 %multiply_reduce_fusion.1 = (f32[2048]{0:T(1024)S(1)}, f32[2048]{0:T(1024)S(1)}, f32[2048]{0:T(1024)S(1)}, f32[2048]{0:T(1024)S(1)}, bf16[2048,2048]{1,0:T(8,128)(2,1)}) fusion(f32[2,1024,2048]{2,1,0:T(8,128)} %copy.69, f32[2048]{0:T(1024)S(1)} %copy-done.61, f32[2048]{0:T(1024)S(1)} %copy-done.63, f32[2048,2048]{1,0:T(8,128)} %fusion.344, ...), kind=kOutput, calls=%fused_computation.6 | convolution fusion | flops 12947808256 | bytes 54591488 | tf_op jit(solution)/shard_map/dot_general | solution.py:24
  689.5 17.7 %fusion.320 = f32[2048,2048]{1,0:T(8,128)} fusion(bf16[512,2048]{1,0:T(8,128)(2,1)S(1)} %copy-done.126, bf16[512,256]{1,0:T(8,128)(2,1)S(1)} %convolution_convert_fusion.4, bf16[512,256]{1,0:T(8,128)(2,1)S(1)} %convolution_convert_fusion.5, bf16[512,256]{1,0:T(8,128)(2,1)S(1)} %convolution_convert_fusion.6, ...), kind=kOutput, calls=%fused_computation.484 | convolution fusion | flops 4311744512 | bytes 20971520 | tf_op jit(solution)/shard_map/dot_general | solution.py:20
  716.0 27.2 %add_convert_fusion.2 = bf16[2048,2048]{1,0:T(8,128)(2,1)} fusion(f32[2048,2048]{1,0:T(8,128)} %fusion.320, bf16[2048,2048]{1,0:T(8,128)(2,1)S(1)} %multiply_convert_fusion, bf16[2048,2048]{1,0:T(8,128)(2,1)} %all-gather.15.cloned.1.call-done), kind=kOutput, calls=%fused_computation.9 | convolution fusion | flops 17188257792 | bytes 41943040 | tf_op jit(solution)/shard_map/dot_general | solution.py:20
  767.1 19.6 %convolution_convert_fusion.1 = bf16[2048,1536]{1,0:T(8,128)(2,1)} fusion(bf16[2048,2048]{1,0:T(8,128)(2,1)} %get-tuple-element.29, bf16[1024,1536]{0,1:T(8,128)(2,1)} %fusion.42, bf16[1024,1536]{0,1:T(8,128)(2,1)S(1)} %copy-done.28), kind=kOutput, calls=%fused_computation.32 | convolution fusion | flops 12900630528 | bytes 20971520 | tf_op jit(solution)/shard_map/dot_general | solution.py:28
  786.8 24.0 %convolution_convert_fusion = bf16[2048,2048]{1,0:T(8,128)(2,1)} fusion(bf16[2048,2048]{1,0:T(8,128)(2,1)} %get-tuple-element.28, bf16[2048,2048]{1,0:T(8,128)(2,1)} %get-tuple-element.25), kind=kOutput, calls=%fused_computation.31 | convolution fusion | flops 17184063488 | bytes 25165824 | tf_op jit(solution)/shard_map/dot_general | solution.py:28
  811.1 23.9 %convert_bitcast_fusion = bf16[2048,2048]{0,1:T(8,128)(2,1)} fusion(bf16[2048,2048]{1,0:T(8,128)(2,1)} %copy-done.16, bf16[2048,2048]{1,0:T(8,128)(2,1)} %bitcast.135), kind=kOutput, calls=%fused_computation.30 | convolution fusion | flops 17184063488 | bytes 25165824 | tf_op jit(solution)/shard_map/dot_general | solution.py:28
  852.0 55.7 %all-to-all-done.6 = bf16[8,2,256,256]{2,3,1,0:T(8,128)(2,1)S(1)} async-done(((bf16[8,2,256,256]{2,3,1,0:T(8,128)(2,1)}), bf16[8,2,256,256]{2,3,1,0:T(8,128)(2,1)S(1)}, u32[]{:S(2)}, u32[]{:S(2)}) %all-to-all-start.6) | async-done | bytes 2097184 | tf_op jit(solution)/shard_map/all_to_all | solution.py:94
  916.5 59.8 %all-to-all-done.2 = bf16[8,2,256,256]{2,3,1,0:T(8,128)(2,1)S(1)} async-done(((bf16[8,2,256,256]{2,3,1,0:T(8,128)(2,1)}), bf16[8,2,256,256]{2,3,1,0:T(8,128)(2,1)S(1)}, u32[]{:S(2)}, u32[]{:S(2)}) %all-to-all-start.2) | async-done | bytes 2097184 | tf_op jit(solution)/shard_map/all_to_all | solution.py:94
  985.0 30.4 %all-reduce.8 = (f32[1536]{0:T(1024)}, f32[2048]{0:T(1024)}) all-reduce(f32[1536]{0:T(1024)S(1)} %convert_reduce_fusion.1, f32[2048]{0:T(1024)S(1)} %copy-done.68), channel_id=1, replica_groups=mesh['row'=4,'col'=8] {'col'}, use_global_device_ids=true, to_apply=%region_40.41 | all-reduce | flops 3584 | bytes 28672 | tf_op jit(solution)/shard_map/psum | solution.py:213
  1018.1 24.0 %reduce-scatter.14.cloned.1.call-done = bf16[256,1536]{1,0:T(8,128)(2,1)} async-done(((bf16[2048,1536]{1,0:T(8,128)(2,1)}), bf16[256,1536]{1,0:T(8,128)(2,1)}) %reduce-scatter.14.cloned.1.call-update) | async-done | bytes 786448 | tf_op jit(solution)/shard_map/reduce_scatter | solution.py:132
  1044.6 87.7 %reduce-scatter.18.cloned.1.call-done = bf16[256,2048]{1,0:T(8,128)(2,1)} async-done(((bf16[2048,2048]{1,0:T(8,128)(2,1)}), bf16[256,2048]{1,0:T(8,128)(2,1)}) %reduce-scatter.18.cloned.1.call-update) | async-done | bytes 1048592 | tf_op jit(solution)/shard_map/reduce_scatter | solution.py:132
  1143.8 78.9 %reduce-scatter.20.cloned.1.call-done = bf16[256,2048]{0,1:T(8,128)(2,1)} async-done(((bf16[2048,2048]{0,1:T(8,128)(2,1)}), bf16[256,2048]{0,1:T(8,128)(2,1)}) %reduce-scatter.20.cloned.1.call-update) | async-done | bytes 1048592 | tf_op jit(solution)/shard_map/reduce_scatter | solution.py:132
  (465 shorter events, 295.9 us)
Async XLA Ops:
  7.2 220.8 %all-gather.7.cloned.1.call-start = ((), (), s32[]{:S(2)}) async-start(), calls=%async_computation.15 | async-start | bytes 10485760 | tf_op jit(solution)/shard_map/all_gather | solution.py:100
  95.9 170.1 %all-gather.9.cloned.1.call-start = ((), (), s32[]{:S(2)}) async-start(), calls=%async_computation.16 | async-start | bytes 7077888 | tf_op jit(solution)/shard_map/all_gather | solution.py:114
  96.6 257.7 %all-gather.17.cloned.1.call-start = ((), (), s32[]{:S(2)}) async-start(), calls=%async_computation.21 | async-start | bytes 10485760 | tf_op jit(solution)/shard_map/all_gather | solution.py:100
  201.7 184.8 %all-gather.11.cloned.1.call-start = ((), (), s32[]{:S(2)}) async-start(), calls=%async_computation.17 | async-start | bytes 2359296 | tf_op jit(solution)/shard_map/all_gather | solution.py:119
  202.3 266.7 %all-gather.13.cloned.1.call-start = ((), (), s32[]{:S(2)}) async-start(), calls=%async_computation.18 | async-start | bytes 9437184 | tf_op jit(solution)/shard_map/all_gather | solution.py:115
  202.9 348.6 %all-gather.15.cloned.1.call-start = ((), (), s32[]{:S(2)}) async-start(), calls=%async_computation.19 | async-start | bytes 9437184 | tf_op jit(solution)/shard_map/all_gather | solution.py:118
  203.4 636.2 %reduce-scatter.12.cloned.1.call-start = ((), (), s32[]{:S(2)}) async-start(), calls=%async_computation.22 | async-start | bytes 10485760 | tf_op jit(solution)/shard_map/reduce_scatter | solution.py:203
  206.7 86.6 %copy-start.106 = (s32[512]{0:T(512)}, s32[512]{0:T(512)S(1)}, u32[]{:S(2)}) copy-start(s32[512]{0:T(512)S(1)} %slice.408) | copy-start | bytes 6148
  206.8 87.6 %copy-start.104 = (s32[512]{0:T(512)}, s32[512]{0:T(512)S(1)}, u32[]{:S(2)}) copy-start(s32[512]{0:T(512)S(1)} %slice.422) | copy-start | bytes 6148
  208.1 86.3 %copy-start.113 = (pred[1024]{0:T(1024)(128)(4,1)}, pred[1024]{0:T(1024)(128)(4,1)S(1)}, u32[]{:S(2)}) copy-start(pred[1024]{0:T(1024)(128)(4,1)S(1)} %get-tuple-element.136) | copy-start | bytes 3076
  294.4 143.2 %copy-start.17 = (f32[512,512]{0,1:T(8,128)}, f32[512,512]{0,1:T(8,128)S(1)}, u32[]{:S(2)}) copy-start(f32[512,512]{0,1:T(8,128)S(1)} %get-tuple-element.107) | copy-start | bytes 3145732
  296.8 131.7 %copy-start.71 = (f32[512]{0:T(512)}, f32[512]{0:T(512)S(1)}, u32[]{:S(2)}) copy-start(f32[512]{0:T(512)S(1)} %get-tuple-element.108) | copy-start | bytes 6148
  298.6 139.8 %copy-start.4 = (f32[512,1024]{1,0:T(8,128)}, f32[512,1024]{1,0:T(8,128)S(1)}, u32[]{:S(2)}) copy-start(f32[512,1024]{1,0:T(8,128)S(1)} %get-tuple-element.105) | copy-start | bytes 6291460
  298.6 139.8 %copy-start.69 = (f32[512]{0:T(512)}, f32[512]{0:T(512)S(1)}, u32[]{:S(2)}) copy-start(f32[512]{0:T(512)S(1)} %get-tuple-element.104) | copy-start | bytes 6148
  674.8 174.0 %reduce-scatter.10.cloned.1.call-start = ((), (), s32[]{:S(2)}) async-start(), calls=%async_computation.20 | async-start | bytes 10485760 | tf_op jit(solution)/shard_map/reduce_scatter | solution.py:184
  755.2 260.1 %reduce-scatter.22.cloned.1.call-start = ((), (), s32[]{:S(2)}) async-start(), calls=%async_computation.27 | async-start | bytes 1179648
  756.7 259.6 %reduce-scatter.16.cloned.1.call-start = ((), (), s32[]{:S(2)}) async-start(), calls=%async_computation.24 | async-start | bytes 2359296 | tf_op jit(solution)/shard_map/reduce_scatter | solution.py:132
  767.0 275.2 %reduce-scatter.14.cloned.1.call-start = ((), (), s32[]{:S(2)}) async-start(), calls=%async_computation.23 | async-start | bytes 7077888 | tf_op jit(solution)/shard_map/reduce_scatter | solution.py:132
  786.7 345.6 %reduce-scatter.18.cloned.1.call-start = ((), (), s32[]{:S(2)}) async-start(), calls=%async_computation.25 | async-start | bytes 9437184 | tf_op jit(solution)/shard_map/reduce_scatter | solution.py:132
  810.8 411.8 %reduce-scatter.20.cloned.1.call-start = ((), (), s32[]{:S(2)}) async-start(), calls=%async_computation.26 | async-start | bytes 9437184 | tf_op jit(solution)/shard_map/reduce_scatter | solution.py:132
  845.3 62.4 %all-to-all-start.6 = ((bf16[8,2,256,256]{2,3,1,0:T(8,128)(2,1)}), bf16[8,2,256,256]{2,3,1,0:T(8,128)(2,1)S(1)}, u32[]{:S(2)}, u32[]{:S(2)}) async-start(bf16[8,2,256,256]{2,3,1,0:T(8,128)(2,1)} %copy.87), calls=%async_computation.8 | async-start | bytes 4194304 | tf_op jit(solution)/shard_map/all_to_all | solution.py:94
  909.0 67.3 %all-to-all-start.2 = ((bf16[8,2,256,256]{2,3,1,0:T(8,128)(2,1)}), bf16[8,2,256,256]{2,3,1,0:T(8,128)(2,1)S(1)}, u32[]{:S(2)}, u32[]{:S(2)}) async-start(bf16[8,2,256,256]{2,3,1,0:T(8,128)(2,1)} %copy.71), calls=%async_computation.3 | async-start | bytes 4194304 | tf_op jit(solution)/shard_map/all_to_all | solution.py:94
  977.6 161.5 %all-to-all-start.7 = ((bf16[4,2,2,256,256]{4,3,2,1,0:T(8,128)(2,1)}), bf16[4,2,2,256,256]{4,3,2,1,0:T(8,128)(2,1)S(1)}, u32[]{:S(2)}, u32[]{:S(2)}) async-start(bf16[4,2,2,256,256]{4,3,2,1,0:T(8,128)(2,1)} %bitcast.139), calls=%async_computation.9 | async-start | bytes 4194304 | tf_op jit(solution)/shard_map/all_to_all | solution.py:96
  1139.0 102.2 %all-to-all-start.3 = ((bf16[4,2,2,256,256]{4,3,2,1,0:T(8,128)(2,1)}), bf16[4,2,2,256,256]{4,3,2,1,0:T(8,128)(2,1)}, u32[]{:S(2)}, u32[]{:S(2)}) async-start(bf16[4,2,2,256,256]{4,3,2,1,0:T(8,128)(2,1)} %bitcast.140), calls=%async_computation.4 | async-start | bytes 4194304 | tf_op jit(solution)/shard_map/all_to_all | solution.py:96
  (132 other events, 1347.9 us)
Sparse Core Ops, SparseCore 0:
  96.0 103.3 all-gather.6
  201.0 64.8 all-gather.8
  268.4 85.9 all-gather.16
  355.8 30.5 all-gather.10
  387.9 81.0 all-gather.12
  470.4 80.9 all-gather.14
  674.9 84.4 reduce-scatter.11
  762.5 86.2 reduce-scatter.9
  851.7 39.6 reduce-scatter.21
  894.1 63.9 reduce-scatter.15
  960.4 81.6 reduce-scatter.13
  1044.3 87.9 reduce-scatter.17
  1134.6 87.9 reduce-scatter.19

commit v2 on v1

v2 whole, which is shorter than its diff:
```python
import functools

import jax
import jax.numpy as jnp
from jax import lax
from jax.experimental import pallas as pl
from jax.experimental.pallas import tpu as pltpu
from jax.sharding import PartitionSpec as P

D = 2048
HEAD = 256
ROT = 64
L = 1024
PIECE = 256
SPAN = 512

norm_eps = 1e-05
theta_base = 10000.0
BF = jnp.bfloat16
F32 = jnp.float32


def mm(left, right):
    return jnp.dot(left, right, preferred_element_type=F32)


def contract_last(left, right):
    return lax.dot_general(left, right, (((1,), (1,)), ((), ())), preferred_element_type=F32)


def contract_first(left, right):
    return lax.dot_general(left, right, (((0,), (0,)), ((), ())), preferred_element_type=F32)


def rotary_tables():
    half = ROT // 2
    freq_steps = jnp.arange(half, dtype=F32)
    inverse = jnp.power(theta_base, -(2.0 * freq_steps) / ROT)
    angles = jnp.arange(L, dtype=jnp.int32).astype(F32)[:, None] * inverse[None, :]
    cosine = jnp.cos(angles)
    sine = jnp.sin(angles)
    rest = 128 - ROT
    cos_table = jnp.concatenate([cosine, cosine, jnp.ones((L, rest), F32)], axis=1)
    sin_table = jnp.concatenate([-sine, sine, jnp.zeros((L, rest), F32)], axis=1)
    return cos_table, sin_table


def turn(block, cos, sin):
    half = ROT // 2
    head = block[:, :128]
    lane = lax.broadcasted_iota(jnp.int32, head.shape, 1)
    partner = jnp.where(lane < half, pltpu.roll(head, 128 - half, 1), pltpu.roll(head, half, 1))
    return jnp.concatenate([head * cos + partner * sin, block[:, 128:]], axis=1)


def attention_kernel(
    slot_ref, starts_ref, pre_ref, gm_ref, cos_ref, sin_ref,
    mix_ref, grad_ref, q_s, k_s, v_s, g_s, gk_s, gv_s, *, parts, part,
):
    m = pl.program_id(1)
    scale = HEAD ** (-0.5)
    for a in range(parts):
        rows = slice(a * part, (a + 1) * part)
        j = slot_ref[a]
        block = pre_ref[j, 0]
        cos, sin = cos_ref[rows], sin_ref[rows]
        q_s[rows] = turn(block[:, :HEAD], cos, sin).astype(BF)
        k_s[rows] = turn(block[:, HEAD : 2 * HEAD], cos, sin).astype(BF)
        v_s[rows] = block[:, 2 * HEAD :].astype(BF)
        g_s[rows] = gm_ref[j, 0]
    for first in range(0, L, SPAN):
        last = first + SPAN
        q, g = q_s[first:last], g_s[first:last]
        k, v = k_s[:last], v_s[:last]
        row = lax.broadcasted_iota(jnp.int32, (SPAN, 1), 0) + first
        limit = row
        for piece in range(2):
            low = starts_ref[2 * m + piece]
            limit = jnp.where((row >= low) & (row < low + PIECE), low + PIECE - 1, limit)
        column = lax.broadcasted_iota(jnp.int32, (SPAN, last), 1)
        scores = jnp.where(column <= limit, contract_last(q, k) * scale, -jnp.inf)
        top = jnp.max(scores, axis=1, keepdims=True)
        powers = jnp.exp(scores - top)
        probs = powers * (1.0 / jnp.sum(powers, axis=1, keepdims=True))
        pb = probs.astype(BF)
        mix = mm(pb, v).astype(BF)
        gp = contract_last(g, v)
        delta = jnp.sum(gp * probs, axis=1, keepdims=True)
        gs = (probs * (gp - delta)).astype(BF)
        gq = mm(gs, k) * scale
        gk = contract_first(gs, q)
        gv = contract_first(pb, g)
        if first == 0:
            gk_s[:last] = gk
            gv_s[:last] = gv
            gk_s[last:] = jnp.zeros((L - last, HEAD), F32)
            gv_s[last:] = jnp.zeros((L - last, HEAD), F32)
        else:
            gk_s[:last] += gk
            gv_s[:last] += gv
        for a in range(first // part, last // part):
            rows = slice(a * part - first, (a + 1) * part - first)
            table = slice(a * part, (a + 1) * part)
            j = slot_ref[a]
            mix_ref[j, 0] = mix[rows]
            grad_ref[j, 0, :, :HEAD] = turn(gq[rows], cos_ref[table], -sin_ref[table]).astype(BF)
    for a in range(parts):
        rows = slice(a * part, (a + 1) * part)
        j = slot_ref[a]
        gk = gk_s[rows] * scale
        grad_ref[j, 0, :, HEAD : 2 * HEAD] = turn(gk, cos_ref[rows], -sin_ref[rows]).astype(BF)
        grad_ref[j, 0, :, 2 * HEAD :] = gv_s[rows].astype(BF)


def attention(slots, starts, merged_pre, grad_mix, micro, parts):
    part = L // parts
    heads = merged_pre.shape[1] // (3 * HEAD)
    cos, sin = rotary_tables()
    pre = merged_pre.reshape(parts, micro, part, heads * 3 * HEAD)
    gm = grad_mix.reshape(parts, micro, part, heads * HEAD)
    spec = lambda w: pl.BlockSpec((parts, 1, part, w), lambda h, m, *_: (0, m, 0, h))
    table = pl.BlockSpec((L, 128), lambda h, m, *_: (0, 0))
    flops = heads * micro * 2 * 5 * L * L * HEAD * 3 // 4
    mix, grads = pl.pallas_call(
        functools.partial(attention_kernel, parts=parts, part=part),
        out_shape=(
            jax.ShapeDtypeStruct(gm.shape, BF),
            jax.ShapeDtypeStruct(pre.shape, BF),
        ),
        grid_spec=pltpu.PrefetchScalarGridSpec(
            num_scalar_prefetch=2,
            grid=(heads, micro),
            in_specs=[spec(3 * HEAD), spec(HEAD), table, table],
            out_specs=[spec(HEAD), spec(3 * HEAD)],
            scratch_shapes=[pltpu.VMEM((L, HEAD), BF)] * 4 + [pltpu.VMEM((L, HEAD), F32)] * 2,
        ),
        compiler_params=pltpu.CompilerParams(
            dimension_semantics=("arbitrary", "arbitrary"), vmem_limit_bytes=60 << 20
        ),
        cost_estimate=pl.CostEstimate(
            flops=2 * flops, bytes_accessed=pre.size * 6 + gm.size * 4, transcendentals=heads * micro * L * L
        ),
        name="attention",
    )(slots, starts, pre, gm, cos, sin)
    return mix.reshape(-1, heads * HEAD), grads.reshape(-1, heads * 3 * HEAD)


def after(value, *earlier):
    return lax.optimization_barrier((value,) + earlier)[0]


def ring_order(rows):
    if rows < 4:
        return list(range(rows))
    half = rows // 2
    return list(range(half)) + list(range(rows - 1, half - 1, -1))


def body(
    inputs,
    piece_starts,
    first_gain,
    first_shift,
    second_gain,
    second_shift,
    merged_weight,
    merged_bias,
    output_weight,
    output_bias,
    expand_weight,
    expand_bias,
    reduce_weight,
    reduce_bias,
    cotangent,
):
    rows = lax.axis_size("row")
    cols = lax.axis_size("col")
    micro, own_tokens, width = inputs.shape
    per_row = own_tokens // L
    part = L // rows
    block_rows = micro * part
    order = ring_order(rows)
    spot = [order.index(r) for r in range(rows)]
    ahead = [(order[i], order[(i + 1) % rows]) for i in range(rows)]
    behind = [(b, a) for a, b in ahead]
    me = lax.axis_index("row")
    my_spot = jnp.asarray(spot, jnp.int32)[me]
    slots = (jnp.asarray(spot, jnp.int32) - my_spot) % rows
    up = lambda v: lax.ppermute(v, "row", ahead)
    down = lambda v: lax.ppermute(v, "row", behind)

    def row_swap(pair):
        b = pair.reshape(2, micro, per_row, rows, part, width).transpose(3, 0, 2, 1, 4, 5)
        b = lax.all_to_all(b, "row", split_axis=0, concat_axis=0, tiled=True)
        b = b.reshape(rows, 2, per_row, block_rows, width)
        return (b[:, i].reshape(rows * per_row, block_rows, width) for i in range(2))

    def col_swap(b):
        return lax.all_to_all(b, "col", split_axis=0, concat_axis=0, tiled=True)

    def side_by_side(b):
        return b.transpose(1, 0, 2).reshape(block_rows, cols * width)

    def from_rows(block):
        b = block.reshape(block_rows, cols, width).transpose(1, 0, 2)
        b = lax.all_to_all(b, "col", split_axis=0, concat_axis=0, tiled=True)
        b = b.reshape(rows, per_row, micro, part, width)
        b = lax.all_to_all(b, "row", split_axis=0, concat_axis=0, tiled=True)
        return b.transpose(2, 1, 0, 3, 4).reshape(micro, own_tokens, width)

    def ring_gather(own):
        pieces = [None] * rows
        pieces[0] = own
        fore, back = own, own
        far = rows // 2
        cut = block_rows // 2
        for step in range(1, far):
            fore, back = up(fore), down(back)
            pieces[rows - step], pieces[step] = fore, back
        pieces[far] = jnp.concatenate([up(fore[:cut]), down(back[cut:])], axis=0)
        return jnp.concatenate(pieces, axis=0)

    def ring_scatter(total):
        chunk = lambda j: total[j * block_rows : (j + 1) * block_rows]
        far = rows // 2
        cut = block_rows // 2
        half_up, half_down = up(chunk(far)[:cut].astype(BF)), down(chunk(far)[cut:].astype(BF))
        fore = back = None
        for step in range(far - 1, 0, -1):
            a, b = chunk(step), chunk(rows - step)
            if fore is None:
                a = jnp.concatenate([a[:cut] + half_up.astype(F32), a[cut:]], axis=0)
                b = jnp.concatenate([b[:cut], b[cut:] + half_down.astype(F32)], axis=0)
            else:
                a, b = a + fore.astype(F32), b + back.astype(F32)
            fore, back = up(a.astype(BF)), down(b.astype(BF))
        return chunk(0) + fore.astype(F32) + back.astype(F32)

    def norm(block):
        block = block.astype(F32)
        center = jnp.mean(block, axis=-1, keepdims=True)
        spread = jnp.mean((block - center) ** 2, axis=-1, keepdims=True)
        inverse_std = lax.rsqrt(spread + norm_eps)
        return (block - center) * inverse_std, inverse_std

    def broadcast(value, axis, size):
        return lax.all_to_all(
            jnp.broadcast_to(value, (size,) + value.shape), axis, split_axis=0, concat_axis=0, tiled=True
        )

    gains = jnp.stack([first_gain, first_shift, second_gain, second_shift])
    gains = broadcast(gains, "col", cols).transpose(1, 0, 2).reshape(4, cols * width)
    expand_w = lax.all_gather(expand_weight, "col", axis=0, tiled=True)
    x_half, cot_half = row_swap(jnp.stack([inputs, cotangent]))
    reduce_w = lax.all_gather(after(reduce_weight, x_half), "col", axis=1, tiled=True)
    mixed_weight = jnp.concatenate([merged_weight, output_weight.T], axis=1)
    x_part = col_swap(after(x_half, gains))
    mixed_w = lax.all_gather(after(mixed_weight, x_part), "col", axis=0, tiled=True)
    merged_cols = merged_weight.shape[1]
    merged_w, output_wt = mixed_w[:, :merged_cols], mixed_w[:, merged_cols:]
    cot_part = col_swap(after(cot_half, x_part))
    x_part = side_by_side(x_part)
    x_seq = ring_gather(x_part)
    cot_part = side_by_side(after(cot_part, x_seq))
    cot_seq = ring_gather(cot_part)

    normed, _ = norm(x_seq)
    attend_in = (normed * gains[0] + gains[1]).astype(BF)
    expand_in = (normed * gains[2] + gains[3]).astype(BF)

    expand_pre = lax.optimization_barrier(mm(expand_in, expand_w) + expand_bias)
    phi_sum = 0.5 * (1.0 + lax.erf(expand_pre * (0.5 ** 0.5)))
    density = jnp.exp(-0.5 * expand_pre * expand_pre) * 0.3989422804014327
    activated = (expand_pre * phi_sum).astype(BF)
    slope = (phi_sum + expand_pre * density).astype(BF)
    activated, slope = lax.optimization_barrier((activated, slope))

    def scatter_weight(grad):
        return lax.psum_scatter(grad, "col", scatter_dimension=0, tiled=True).astype(F32)

    reduce_dot = contract_first(cot_seq, activated).astype(BF)
    reduce_grad = scatter_weight(reduce_dot).T
    grad_act = contract_last(after(cot_seq, reduce_dot), reduce_w)
    grad_pre = (grad_act * slope.astype(F32)).astype(BF)
    expand_b = jnp.sum(grad_pre.astype(F32), axis=0)
    expand_dot = contract_first(expand_in, grad_pre).astype(BF)
    expand_grad = scatter_weight(expand_dot)

    merged_pre = mm(after(attend_in, expand_dot), merged_w) + merged_bias
    grad_mix = mm(after(cot_seq, expand_dot), output_wt).astype(BF)
    mix, grad_merged = attention(
        slots, piece_starts.reshape(-1), merged_pre, grad_mix, micro, rows
    )
    attend_late, cot_late, mix_late = lax.optimization_barrier(
        (attend_in, cot_seq, mix, reduce_grad)
    )[:3]
    mixed_dot = jnp.concatenate(
        [
            contract_first(attend_late, grad_merged).astype(BF),
            contract_first(cot_late, mix_late).astype(BF),
        ],
        axis=1,
    )
    mixed_grad = scatter_weight(mixed_dot)
    merged_grad, output_grad = mixed_grad[:, :merged_cols], mixed_grad[:, merged_cols:].T

    mix, activated = after((mix, activated), mixed_dot)
    branch = contract_last(mix, output_wt) + mm(activated, reduce_w)
    grad_pre, grad_merged, branch = lax.optimization_barrier(
        (grad_pre, grad_merged, branch, expand_grad)
    )[:3]
    branch = from_rows(ring_scatter(branch).astype(BF))
    result = inputs.astype(F32) + branch.astype(F32) + output_bias + reduce_bias
    result = result.astype(BF)

    grad_first = contract_last(grad_merged, merged_w)
    grad_second = contract_last(grad_pre, expand_w)
    norm_sums = jnp.stack(
        [
            jnp.sum(grad_first * normed, axis=0),
            jnp.sum(grad_first, axis=0),
            jnp.sum(grad_second * normed, axis=0),
            jnp.sum(grad_second, axis=0),
        ]
    )
    grad_hat = ring_scatter(grad_first * gains[0] + grad_second * gains[2])
    part_normed, part_inverse = norm(x_part)
    norm_part = part_inverse * (
        grad_hat
        - jnp.mean(grad_hat, axis=-1, keepdims=True)
        - part_normed * jnp.mean(grad_hat * part_normed, axis=-1, keepdims=True)
    )
    input_grad = cotangent.astype(F32) + from_rows(norm_part.astype(BF)).astype(F32)

    merged_b = jnp.sum(grad_merged.astype(F32), axis=0)
    shift_b = jnp.sum(cotangent.astype(F32), axis=(0, 1))
    sums = jnp.concatenate(
        [
            norm_sums.reshape(4, cols, width).transpose(1, 0, 2).reshape(cols, 4 * width),
            jnp.broadcast_to(merged_b, (cols, merged_cols)),
            jnp.broadcast_to(expand_b, (cols, expand_b.shape[0])),
        ],
        axis=1,
    ).reshape(cols, -1, 128)
    sums = lax.all_to_all(sums, "col", split_axis=0, concat_axis=0, tiled=True)
    sums = jnp.sum(sums.reshape(cols, -1), axis=0)
    merged_b = sums[4 * width : 4 * width + merged_cols]
    expand_b = sums[4 * width + merged_cols :]
    tail = jnp.concatenate([sums[: 4 * width], shift_b]).reshape(-1, 128)
    tail = jnp.sum(broadcast(tail, "row", rows), axis=0).reshape(5, width)
    norm_sums, shift_b = tail[:4], tail[4]
    return (
        result,
        input_grad,
        norm_sums[0],
        norm_sums[1],
        norm_sums[2],
        norm_sums[3],
        merged_grad,
        merged_b,
        output_grad,
        shift_b,
        expand_grad,
        expand_b,
        reduce_grad,
        shift_b,
    )


def solution(mesh):
    in_specs = (
        P(None, "row", "col"),
        P(None, "col", None),
        P("col"),
        P("col"),
        P("col"),
        P("col"),
        P("col", "row"),
        P("row"),
        P("row", "col"),
        P("col"),
        P("col", "row"),
        P("row"),
        P("row", "col"),
        P("col"),
        P(None, "row", "col"),
    )
    out_specs = (
        P(None, "row", "col"),
        P(None, "row", "col"),
        P("col"),
        P("col"),
        P("col"),
        P("col"),
        P("col", "row"),
        P("row"),
        P("row", "col"),
        P("col"),
        P("col", "row"),
        P("row"),
        P("row", "col"),
        P("col"),
    )
    return jax.shard_map(body, mesh=mesh, in_specs=in_specs, out_specs=out_specs, check_vma=False)
```

time: 1260 us -> 928 us (0.74)
  waiting for transfers between devices: 463 us -> 275 us
  matrix products: 340 us -> 232 us
  blocking collectives: 240 us -> 160 us
  starting transfers between devices: 16.5 us -> 55.5 us
  Pallas kernels: 0 us -> 21 us
  local copies, waits for them, and re-layouts: 86.9 us -> 67.7 us
    ppermute x0 -> x16, waiting for transfers between devices: none -> 191 us  [the longest x8 117 us: body(): up = lambda v: lax.ppermute(v, 'row', ahead)]
    reduce_scatter x6 -> x3, waiting for transfers between devices: 191 us -> 0.01 us  [scatter_weight(): lax.psum_scatter(grad, 'col', scatter_dimension=0, tiled=True).astype(F32)]
    all_gather x5 -> x2, waiting for transfers between devices: 128 us -> 0.02 us  [the longest x1 0.02 us: body(): lax.all_gather(after(mixed_weight, x_part), 'col', axis=0, tiled=True)]
    all_to_all x2, waiting for transfers between devices: 115 us -> 47.7 us  [from_rows(): b = lax.all_to_all(b, 'col', split_axis=0, concat_axis=0, tiled=True)]
    dot_general x20 -> x4, matrix products: 148 us -> 84 us  [contract_last(): lax.dot_general(left, right, (((1,), (1,)), ((), ())), preferred_element_...]
    psum x2 -> x0, blocking collectives: 40.3 us -> none  [the longest x1 30.4 us: body(): merged_b = lax.psum(jnp.sum(grad_merged.astype(F32), axis=0), 'col')]
    all_to_all x2, waiting for transfers between devices: 0.01 us -> 35.3 us  [from_rows(): b = lax.all_to_all(b, 'row', split_axis=0, concat_axis=0, tiled=True)]
    all_gather x1, waiting for transfers between devices: 26.7 us -> 0.01 us  [body(): expand_w = lax.all_gather(expand_weight, 'col', axis=0, tiled=True)]
  transfers between devices with their start and end apart: 17 -> 29, of which waited for: 10 -> 17; matrix products, arithmetic and copies ran while one was open for 30% -> 36% of each run, Pallas kernels for 0% -> 2%
where the time goes in v2:
time: 928 us; the launch traced here: 927 us
  waiting for transfers between devices  275 us (30%)
  matrix products  232 us (25%)
  blocking collectives  160 us (17%)
  other arithmetic  99.7 us (11%)
  local copies, waits for them, and re-layouts  67.7 us (7%)
  starting transfers between devices  55.5 us (6%)
  Pallas kernels  21 us (2%)
  between operations  15 us (2%)
    ppermute x8, waiting for transfers between devices, body(): up = lambda v: lax.ppermute(v, 'row', ahead)  117 us
    all_to_all x1, blocking collectives, col_swap(): return lax.all_to_all(b, 'col', split_axis=0, concat_axis=0, tiled=True)  98.5 us
    dot_general x4, matrix products, contract_last(): lax.dot_general(left, right, (((1,), (1,)), ((), ())), preferred_element_...  84 us
    dot_general x4, matrix products, mm(): return jnp.dot(left, right, preferred_element_type=F32)  79 us
    ppermute x8, waiting for transfers between devices, body(): down = lambda v: lax.ppermute(v, 'row', behind)  74.6 us
    dot_general x4, matrix products, contract_first(): lax.dot_general(left, right, (((0,), (0,)), ((), ())), preferred_element_...  69.3 us
    all_to_all x1, blocking collectives, row_swap(): b = lax.all_to_all(b, 'row', split_axis=0, concat_axis=0, tiled=True)  52.8 us
    all_to_all x2, waiting for transfers between devices, from_rows(): b = lax.all_to_all(b, 'col', split_axis=0, concat_axis=0, tiled=True)  47.7 us
  transfers between devices with their start and end apart: 29, of which 17 were waited for; matrix products, arithmetic and copies ran while one was open for 36% of the time, Pallas kernels for 2%

profile of v2, /device:TPU:0, one launch (start us, length us, event | category | flops | bytes accessed | tf_op | source)
XLA Modules:
  0.0 926.9 jit_solution(11885513010437478486)
XLA Ops:
  11.0 52.8 %all_to_all.50 = bf16[4,2,2,2,256,256]{5,4,2,3,1,0:T(8,128)(2,1)S(1)} all-to-all(bf16[4,2,2,2,256,256]{5,4,2,3,1,0:T(8,128)(2,1)S(1)} %copy.102), channel_id=1, replica_groups=mesh['row'=4,'col'=8] {'row'}, dimensions={0} | all-to-all | bytes 8388608 | tf_op jit(solution)/shard_map/all_to_all | solution.py:194
  68.3 98.5 %all_to_all.51 = bf16[8,512,256]{1,2,0:T(8,128)(2,1)S(1)} all-to-all(bf16[8,512,256]{1,2,0:T(8,128)(2,1)} %copy.104), channel_id=1, replica_groups=mesh['row'=4,'col'=8] {'col'}, dimensions={0} | all-to-all | bytes 4194304 | tf_op jit(solution)/shard_map/all_to_all | solution.py:199
  177.1 37.5 %collective-permute-done.1 = bf16[512,2048]{0,1:T(8,128)(2,1)} collective-permute-done((bf16[512,2048]{0,1:T(8,128)(2,1)S(1)}, bf16[512,2048]{0,1:T(8,128)(2,1)}, u32[]{:S(2)}, u32[]{:S(2)}) %collective-permute-start.1) | collective-permute-done | bytes 2097184 | tf_op jit(solution)/shard_map/ppermute | solution.py:189
  229.4 12.1 %collective-permute-done.2 = bf16[256,2048]{0,1:T(8,128)(2,1)S(1)} collective-permute-done((bf16[256,2048]{0,1:T(8,128)(2,1)}, bf16[256,2048]{0,1:T(8,128)(2,1)S(1)}, u32[]{:S(2)}, u32[]{:S(2)}) %collective-permute-start.2) | collective-permute-done | bytes 1048608 | tf_op jit(solution)/shard_map/ppermute | solution.py:189
  267.6 30.2 %collective-permute-done.5 = bf16[512,2048]{0,1:T(8,128)(2,1)S(1)} collective-permute-done((bf16[512,2048]{0,1:T(8,128)(2,1)}, bf16[512,2048]{0,1:T(8,128)(2,1)S(1)}, u32[]{:S(2)}, u32[]{:S(2)}) %collective-permute-start.5) | collective-permute-done | bytes 2097184 | tf_op jit(solution)/shard_map/ppermute | solution.py:189
  310.9 10.4 %collective-permute-done.6 = bf16[256,2048]{0,1:T(8,128)(2,1)S(1)} collective-permute-done((bf16[256,2048]{0,1:T(8,128)(2,1)S(1)}, bf16[256,2048]{0,1:T(8,128)(2,1)S(1)}, u32[]{:S(2)}, u32[]{:S(2)}) %collective-permute-start.6) | collective-permute-done | bytes 1048608 | tf_op jit(solution)/shard_map/ppermute | solution.py:189
  325.6 24.4 %convolution_add_fusion.2 = f32[2048,2048]{1,0:T(8,128)S(1)} fusion(bf16[2048,2048]{1,0:T(8,128)(2,1)} %all-gather.4.cloned.1.call-done, f32[2048]{0:T(1024)S(1)} %copy-done.24, bf16[2048,2048]{0,1:T(8,128)(2,1)} %constant_dynamic-update-slice_fusion, f32[2048]{0:T(1024)S(1)} %bitcast.133, f32[2048]{0:T(1024)S(1)} %bitcast.130, ...), kind=kOutput, calls=%fused_computation.29 | convolution fusion | flops 17209229312 | bytes 33595392 | tf_op jit(solution)/shard_map/dot_general | solution.py:24
  361.8 21.3 %convolution_convert_fusion.1 = bf16[2048,2048]{1,0:T(8,128)(2,1)} fusion(bf16[2048,2048]{0,1:T(8,128)(2,1)} %constant_dynamic-update-slice_fusion.5, bf16[2048,2048]{1,0:T(8,128)(2,1)S(1)} %get-tuple-element.48), kind=kOutput, calls=%fused_computation.32 | convolution fusion | flops 17184063488 | bytes 25165824 | tf_op jit(solution)/shard_map/dot_general | solution.py:32
  383.2 11.4 %reduce-scatter.6.cloned.1.call-start = ((), (), s32[]{:S(2)}) async-start(), calls=%async_computation.17 | async-start | bytes 9437184 | tf_op jit(solution)/shard_map/reduce_scatter | solution.py:279
  410.0 24.5 %convert_reduce_fusion.1 = (f32[2048]{0:T(1024)}, bf16[2048,2048]{1,0:T(8,128)(2,1)S(1)}) fusion(bf16[2048,2048]{1,0:T(8,128)(2,1)} %get-tuple-element.38, bf16[2048,2048]{0,1:T(8,128)(2,1)} %constant_dynamic-update-slice_fusion.5, bf16[2048,2048]{1,0:T(8,128)(2,1)} %all-gather.6.cloned.1.call-done), kind=kOutput, calls=%fused_computation.21 | convolution fusion | flops 17200838656 | bytes 33562624 | tf_op jit(solution)/shard_map/dot_general | solution.py:28
  437.8 21.6 %convolution_convert_fusion = bf16[2048,2048]{1,0:T(8,128)(2,1)} fusion(bf16[2048,2048]{1,0:T(8,128)(2,1)S(1)} %get-tuple-element.51, bf16[2048,2048]{0,1:T(8,128)(2,1)} %constant_dynamic-update-slice_fusion, f32[2048]{0:T(1024)S(1)} %bitcast.134, f32[2048]{0:T(1024)S(1)} %bitcast.131, f32[2048]{0:T(1024)S(1)} %add_rsqrt_fusion, ...), kind=kOutput, calls=%fused_computation.31 | convolution fusion | flops 17209229312 | bytes 25198592 | tf_op jit(solution)/shard_map/dot_general | solution.py:32
  469.6 18.0 %convolution_add_fusion = f32[2048,1536]{1,0:T(8,128)} fusion(bf16[2048,2048]{0,1:T(8,128)(2,1)} %fusion.9, f32[1536]{0:T(1024)S(1)} %copy-done.25, bf16[2048,2048]{1,0:T(8,128)(2,1)S(1)} %copy-done.23), kind=kOutput, calls=%fused_computation.27 | convolution fusion | flops 12888047616 | bytes 27271168 | tf_op jit(solution)/shard_map/dot_general | solution.py:24
  487.6 21.0 %attention.1 = (bf16[4,2,256,512]{3,2,1,0:T(8,128)(2,1)}, bf16[4,2,256,1536]{3,2,1,0:T(8,128)(2,1)}) custom-call(s32[4]{0:T(128)} %and_select_fusion.slot_ref, s32[4]{0:T(128)} %reshape.174.starts_ref, f32[4,2,256,1536]{3,2,1,0:T(8,128)} %bitcast.139, bf16[4,2,256,512]{3,2,1,0:T(8,128)(2,1)} %bitcast.142, f32[1024,128]{1,0:T(8,128)} %get-tuple-element.208.cos_ref, ...), custom_call_target="tpu_custom_call" | custom-call | flops 16106127360 | bytes 23068672 | tf_op jit(solution)/shard_map/attention/pallas_call | solution.py:124
  520.4 17.6 %convolution_convert_fusion.2 = bf16[2048,1536]{0,1:T(8,128)(2,1)} fusion(bf16[2048,2048]{0,1:T(8,128)(2,1)} %fusion.9, bf16[2048,1536]{1,0:T(8,128)(2,1)S(1)} %bitcast.120), kind=kOutput, calls=%fused_computation.33 | convolution fusion | flops 12888047616 | bytes 20971520 | tf_op jit(solution)/shard_map/dot_general | solution.py:32
  545.7 12.6 %fusion.29 = f32[2048,2048]{1,0:T(8,128)} fusion(bf16[2048,512]{1,0:T(8,128)(2,1)} %bitcast.141, bf16[2048,2048]{1,0:T(8,128)(2,1)} %all-gather.8.cloned.1.call-done), kind=kOutput, calls=%fused_computation.70 | convolution fusion | flops 4294967296 | bytes 20971520 | tf_op jit(solution)/shard_map/dot_general | solution.py:28
  558.3 26.6 %convolution_add_fusion.1 = f32[2048,2048]{1,0:T(8,128)} fusion(f32[2048,2048]{1,0:T(8,128)} %fusion.29, bf16[2048,2048]{1,0:T(8,128)(2,1)} %copy-done.3, bf16[2048,2048]{1,0:T(8,128)(2,1)} %all-gather.6.cloned.1.call-done), kind=kOutput, calls=%fused_computation.28 | convolution fusion | flops 17184063488 | bytes 50331648 | tf_op jit(solution)/shard_map/dot_general | solution.py:24
  587.7 24.3 %fusion.42 = f32[2048,2048]{0,1:T(8,128)} fusion(bf16[2048,2048]{1,0:T(8,128)(2,1)} %copy-done.27, bf16[2048,2048]{1,0:T(8,128)(2,1)} %all-gather.4.cloned.1.call-done), kind=kOutput, calls=%fused_computation.120 | convolution fusion | flops 17179869184 | bytes 33554432 | tf_op jit(solution)/shard_map/dot_general | solution.py:28
  612.0 22.7 %fusion.10 = (f32[2048]{0:T(1024)S(1)}, f32[2048]{0:T(1024)S(1)}, f32[2048]{0:T(1024)S(1)}, f32[2048]{0:T(1024)S(1)}, bf16[2048,2048]{0,1:T(8,128)(2,1)S(1)}, /*index=5*/f32[2048,2048]{0,1:T(8,128)}) fusion(bf16[2048,2048]{0,1:T(8,128)(2,1)} %constant_dynamic-update-slice_fusion, f32[2048]{0:T(1024)S(1)} %copy-done.9, f32[2048]{0:T(1024)S(1)} %copy-done.7, ...), kind=kOutput, calls=%fused_computation.13 | convolution fusion | flops 12939419648 | bytes 62980096 | tf_op jit(solution)/shard_map/dot_general | solution.py:28
  638.8 20.5 %collective-permute-done.12 = bf16[256,2048]{0,1:T(8,128)(2,1)S(1)} collective-permute-done((bf16[256,2048]{0,1:T(8,128)(2,1)}, bf16[256,2048]{0,1:T(8,128)(2,1)S(1)}, u32[]{:S(2)}, u32[]{:S(2)}) %collective-permute-start.12) | collective-permute-done | bytes 1048608 | tf_op jit(solution)/shard_map/ppermute | solution.py:189
  691.0 24.9 %collective-permute-done.15 = bf16[512,2048]{0,1:T(8,128)(2,1)} collective-permute-done((bf16[512,2048]{0,1:T(8,128)(2,1)}, bf16[512,2048]{0,1:T(8,128)(2,1)}, u32[]{:S(2)}, u32[]{:S(2)}) %collective-permute-start.15) | collective-permute-done | bytes 2097184 | tf_op jit(solution)/shard_map/ppermute | solution.py:190
  742.9 44.0 %collective-permute-done.11 = bf16[512,2048]{1,0:T(8,128)(2,1)S(1)} collective-permute-done((bf16[512,2048]{1,0:T(8,128)(2,1)S(1)}, bf16[512,2048]{1,0:T(8,128)(2,1)S(1)}, u32[]{:S(2)}, u32[]{:S(2)}) %collective-permute-start.11) | collective-permute-done | bytes 2097184 | tf_op jit(solution)/shard_map/ppermute | solution.py:190
  799.4 47.7 %all-to-all-done.4 = bf16[8,512,256]{2,1,0:T(8,128)(2,1)} async-done(((bf16[8,512,256]{2,1,0:T(8,128)(2,1)}), bf16[8,512,256]{2,1,0:T(8,128)(2,1)}, u32[]{:S(2)}, u32[]{:S(2)}) %all-to-all-start.4) | async-done | bytes 2097184 | tf_op jit(solution)/shard_map/all_to_all | solution.py:206
  856.7 18.8 %all-to-all-done.7 = bf16[4,2,2,256,256]{4,3,1,2,0:T(8,128)(2,1)S(1)} async-done(((bf16[4,2,2,256,256]{4,3,1,2,0:T(8,128)(2,1)}), bf16[4,2,2,256,256]{4,3,1,2,0:T(8,128)(2,1)S(1)}, u32[]{:S(2)}, u32[]{:S(2)}) %all-to-all-start.7) | async-done | bytes 2097184 | tf_op jit(solution)/shard_map/all_to_all | solution.py:208
  888.5 16.5 %all-to-all-done.5 = bf16[4,2,2,256,256]{4,3,1,2,0:T(8,128)(2,1)S(1)} async-done(((bf16[4,2,2,256,256]{4,3,1,2,0:T(8,128)(2,1)}), bf16[4,2,2,256,256]{4,3,1,2,0:T(8,128)(2,1)S(1)}, u32[]{:S(2)}, u32[]{:S(2)}) %all-to-all-start.5) | async-done | bytes 2097184 | tf_op jit(solution)/shard_map/all_to_all | solution.py:208
  (228 shorter events, 252.1 us)
Async XLA Ops:
  7.2 318.4 %all-gather.4.cloned.1.call-start = ((), (), s32[]{:S(2)}) async-start(), calls=%async_computation.13 | async-start | bytes 9437184 | tf_op jit(solution)/shard_map/all_gather | solution.py:253
  7.9 402.1 %all-gather.6.cloned.1.call-start = ((), (), s32[]{:S(2)}) async-start(), calls=%async_computation.14 | async-start | bytes 9437184 | tf_op jit(solution)/shard_map/all_gather | solution.py:255
  166.8 47.8 %collective-permute-start.1 = (bf16[512,2048]{0,1:T(8,128)(2,1)S(1)}, bf16[512,2048]{0,1:T(8,128)(2,1)}, u32[]{:S(2)}, u32[]{:S(2)}) collective-permute-start(bf16[512,2048]{0,1:T(8,128)(2,1)S(1)} %bitcast.102), channel_id=1, source_target_pairs={{0,8},{8,24},{24,16},{16,0},{1,9},{9,25},{25,17},{17,1},{2,10},{10... | collective-permute-start | bytes 6291464 | tf_op jit(solution)/shard_map/ppermute | solution.py:189
  168.3 51.2 %collective-permute-start = (bf16[512,2048]{0,1:T(8,128)(2,1)S(1)}, bf16[512,2048]{0,1:T(8,128)(2,1)}, u32[]{:S(2)}, u32[]{:S(2)}) collective-permute-start(bf16[512,2048]{0,1:T(8,128)(2,1)S(1)} %bitcast.103), channel_id=1, source_target_pairs={{8,0},{24,8},{16,24},{0,16},{9,1},{25,9},{17,25},{1,17},{10,2},{26... | collective-permute-start | bytes 6291464 | tf_op jit(solution)/shard_map/ppermute | solution.py:190
  172.7 78.9 %all-to-all-start.2 = ((bf16[8,512,256]{1,2,0:T(8,128)(2,1)}), bf16[8,512,256]{1,2,0:T(8,128)(2,1)}, u32[]{:S(2)}, u32[]{:S(2)}) async-start(bf16[8,512,256]{1,2,0:T(8,128)(2,1)} %copy.105), calls=%async_computation.2 | async-start | bytes 4194304 | tf_op jit(solution)/shard_map/all_to_all | solution.py:199
  177.1 282.4 %all-gather.8.cloned.1.call-start = ((), (), s32[]{:S(2)}) async-start(), calls=%async_computation.15 | async-start | bytes 9437184 | tf_op jit(solution)/shard_map/all_gather | solution.py:258
  216.9 24.6 %collective-permute-start.2 = (bf16[256,2048]{0,1:T(8,128)(2,1)}, bf16[256,2048]{0,1:T(8,128)(2,1)S(1)}, u32[]{:S(2)}, u32[]{:S(2)}) collective-permute-start(bf16[256,2048]{0,1:T(8,128)(2,1)} %slice.203), channel_id=1, source_target_pairs={{0,8},{8,24},{24,16},{16,0},{1,9},{9,25},{25,17},{17,1},{2,10},{10... | collective-permute-start | bytes 3145736 | tf_op jit(solution)/shard_map/ppermute | solution.py:189
  221.7 24.4 %collective-permute-start.3 = (bf16[256,2048]{0,1:T(8,128)(2,1)}, bf16[256,2048]{0,1:T(8,128)(2,1)}, u32[]{:S(2)}, u32[]{:S(2)}) collective-permute-start(bf16[256,2048]{0,1:T(8,128)(2,1)} %slice.204), channel_id=1, source_target_pairs={{8,0},{24,8},{16,24},{0,16},{9,1},{25,9},{17,25},{1,17},{10,2},{26... | collective-permute-start | bytes 3145736 | tf_op jit(solution)/shard_map/ppermute | solution.py:190
  224.6 284.0 %reduce-scatter.4.cloned.1.call-start = ((), (), s32[]{:S(2)}) async-start(), calls=%async_computation.16 | async-start | bytes 9437184 | tf_op jit(solution)/shard_map/reduce_scatter | solution.py:279
  251.7 46.2 %collective-permute-start.5 = (bf16[512,2048]{0,1:T(8,128)(2,1)}, bf16[512,2048]{0,1:T(8,128)(2,1)S(1)}, u32[]{:S(2)}, u32[]{:S(2)}) collective-permute-start(bf16[512,2048]{0,1:T(8,128)(2,1)} %bitcast.10), channel_id=1, source_target_pairs={{0,8},{8,24},{24,16},{16,0},{1,9},{9,25},{25,17},{17,1},{2,10},{10... | collective-permute-start | bytes 6291464 | tf_op jit(solution)/shard_map/ppermute | solution.py:189
  252.8 46.6 %collective-permute-start.4 = (bf16[512,2048]{0,1:T(8,128)(2,1)}, bf16[512,2048]{0,1:T(8,128)(2,1)S(1)}, u32[]{:S(2)}, u32[]{:S(2)}) collective-permute-start(bf16[512,2048]{0,1:T(8,128)(2,1)} %bitcast.10), channel_id=1, source_target_pairs={{8,0},{24,8},{16,24},{0,16},{9,1},{25,9},{17,25},{1,17},{10,2},{26... | collective-permute-start | bytes 6291464 | tf_op jit(solution)/shard_map/ppermute | solution.py:190
  383.2 201.8 %reduce-scatter.6.cloned.1.call-start = ((), (), s32[]{:S(2)}) async-start(), calls=%async_computation.17 | async-start | bytes 9437184 | tf_op jit(solution)/shard_map/reduce_scatter | solution.py:279
  459.4 454.7 %reduce-scatter.8.cloned.1.call-start = ((), (), s32[]{:S(2)}) async-start(), calls=%async_computation.18 | async-start | bytes 9437184 | tf_op jit(solution)/shard_map/reduce_scatter | solution.py:279
  667.1 48.8 %collective-permute-start.15 = (bf16[512,2048]{0,1:T(8,128)(2,1)}, bf16[512,2048]{0,1:T(8,128)(2,1)}, u32[]{:S(2)}, u32[]{:S(2)}) collective-permute-start(bf16[512,2048]{0,1:T(8,128)(2,1)} %pad_maximum_fusion.4), channel_id=1, source_target_pairs={{8,0},{24,8},{16,24},{0,16},{9,1},{25,9},{17,25},{1,17},{10,2},{26... | collective-permute-start | bytes 6291464 | tf_op jit(solution)/shard_map/ppermute | solution.py:190
  669.7 48.8 %collective-permute-start.13 = (bf16[512,2048]{0,1:T(8,128)(2,1)}, bf16[512,2048]{0,1:T(8,128)(2,1)}, u32[]{:S(2)}, u32[]{:S(2)}) collective-permute-start(bf16[512,2048]{0,1:T(8,128)(2,1)} %pad_maximum_fusion.3), channel_id=1, source_target_pairs={{0,8},{8,24},{24,16},{16,0},{1,9},{9,25},{25,17},{17,1},{2,10},{10... | collective-permute-start | bytes 6291464 | tf_op jit(solution)/shard_map/ppermute | solution.py:189
  676.2 55.2 %all-to-all-start.8 = ((f32[8,36,128]{2,1,0:T(8,128)}), f32[8,36,128]{2,1,0:T(8,128)S(1)}, u32[]{:S(2)}, u32[]{:S(2)}) async-start(f32[8,36,128]{2,1,0:T(8,128)} %copy.114), calls=%async_computation.10 | async-start | bytes 327680 | tf_op jit(solution)/shard_map/all_to_all | solution.py:345
  689.0 47.8 %collective-permute-start.8 = (bf16[256,2048]{1,0:T(8,128)(2,1)}, bf16[256,2048]{1,0:T(8,128)(2,1)}, u32[]{:S(2)}, u32[]{:S(2)}) collective-permute-start(bf16[256,2048]{1,0:T(8,128)(2,1)} %get-tuple-element.186), channel_id=1, source_target_pairs={{0,8},{8,24},{24,16},{16,0},{1,9},{9,25},{25,17},{17,1},{2,10},{10... | collective-permute-start | bytes 3145736 | tf_op jit(solution)/shard_map/ppermute | solution.py:189
  690.3 46.5 %collective-permute-start.10 = (bf16[256,2048]{1,0:T(8,128)(2,1)}, bf16[256,2048]{1,0:T(8,128)(2,1)}, u32[]{:S(2)}, u32[]{:S(2)}) collective-permute-start(bf16[256,2048]{1,0:T(8,128)(2,1)} %get-tuple-element.187), channel_id=1, source_target_pairs={{8,0},{24,8},{16,24},{0,16},{9,1},{25,9},{17,25},{1,17},{10,2},{26... | collective-permute-start | bytes 3145736 | tf_op jit(solution)/shard_map/ppermute | solution.py:190
  731.4 61.8 %all-to-all-start.6 = ((bf16[8,512,256]{2,1,0:T(8,128)(2,1)}), bf16[8,512,256]{2,1,0:T(8,128)(2,1)S(1)}, u32[]{:S(2)}, u32[]{:S(2)}) async-start(bf16[8,512,256]{2,1,0:T(8,128)(2,1)} %bitcast.111), calls=%async_computation.8 | async-start | bytes 4194304 | tf_op jit(solution)/shard_map/all_to_all | solution.py:206
  740.6 46.4 %collective-permute-start.11 = (bf16[512,2048]{1,0:T(8,128)(2,1)S(1)}, bf16[512,2048]{1,0:T(8,128)(2,1)S(1)}, u32[]{:S(2)}, u32[]{:S(2)}) collective-permute-start(bf16[512,2048]{1,0:T(8,128)(2,1)S(1)} %pad_maximum_fusion.2), channel_id=1, source_target_pairs={{8,0},{24,8},{16,24},{0,16},{9,1},{25,9},{17,25},{1,17},{10,2},{26... | collective-permute-start | bytes 6291464 | tf_op jit(solution)/shard_map/ppermute | solution.py:190
  742.3 46.1 %collective-permute-start.9 = (bf16[512,2048]{1,0:T(8,128)(2,1)S(1)}, bf16[512,2048]{1,0:T(8,128)(2,1)S(1)}, u32[]{:S(2)}, u32[]{:S(2)}) collective-permute-start(bf16[512,2048]{1,0:T(8,128)(2,1)S(1)} %pad_maximum_fusion.1), channel_id=1, source_target_pairs={{0,8},{8,24},{24,16},{16,0},{1,9},{9,25},{25,17},{17,1},{2,10},{10... | collective-permute-start | bytes 6291464 | tf_op jit(solution)/shard_map/ppermute | solution.py:189
  793.2 53.9 %all-to-all-start.4 = ((bf16[8,512,256]{2,1,0:T(8,128)(2,1)}), bf16[8,512,256]{2,1,0:T(8,128)(2,1)}, u32[]{:S(2)}, u32[]{:S(2)}) async-start(bf16[8,512,256]{2,1,0:T(8,128)(2,1)} %bitcast.112), calls=%async_computation.6 | async-start | bytes 4194304 | tf_op jit(solution)/shard_map/all_to_all | solution.py:206
  847.1 28.4 %all-to-all-start.7 = ((bf16[4,2,2,256,256]{4,3,1,2,0:T(8,128)(2,1)}), bf16[4,2,2,256,256]{4,3,1,2,0:T(8,128)(2,1)S(1)}, u32[]{:S(2)}, u32[]{:S(2)}) async-start(bf16[4,2,2,256,256]{4,3,1,2,0:T(8,128)(2,1)} %copy.112), calls=%async_computation.9 | async-start | bytes 4194304 | tf_op jit(solution)/shard_map/all_to_all | solution.py:208
  876.8 28.1 %all-to-all-start.5 = ((bf16[4,2,2,256,256]{4,3,1,2,0:T(8,128)(2,1)}), bf16[4,2,2,256,256]{4,3,1,2,0:T(8,128)(2,1)S(1)}, u32[]{:S(2)}, u32[]{:S(2)}) async-start(bf16[4,2,2,256,256]{4,3,1,2,0:T(8,128)(2,1)} %copy.109), calls=%async_computation.7 | async-start | bytes 4194304 | tf_op jit(solution)/shard_map/all_to_all | solution.py:208
  (41 other events, 1378.7 us)
Sparse Core Ops, SparseCore 0:
  9.6 107.8 all-gather.3
  119.1 125.2 all-gather.5
  246.5 82.1 all-gather.7
  383.3 87.7 reduce-scatter.3
  473.2 87.9 reduce-scatter.5
  638.9 90.4 reduce-scatter.7

commit v3 on v2

--- a/solution.py
+++ b/solution.py
@@ -112,10 +112,10 @@
         grad_ref[j, 0, :, 2 * HEAD :] = gv_s[rows].astype(BF)
 
 
-def attention(slots, starts, merged_pre, grad_mix, micro, parts):
+def attention(slots, starts, merged_pre, grad_mix, tables, micro, parts):
     part = L // parts
     heads = merged_pre.shape[1] // (3 * HEAD)
-    cos, sin = rotary_tables()
+    cos, sin = tables
     pre = merged_pre.reshape(parts, micro, part, heads * 3 * HEAD)
     gm = grad_mix.reshape(parts, micro, part, heads * HEAD)
     spec = lambda w: pl.BlockSpec((parts, 1, part, w), lambda h, m, *_: (0, m, 0, h))
@@ -189,11 +189,10 @@
     up = lambda v: lax.ppermute(v, "row", ahead)
     down = lambda v: lax.ppermute(v, "row", behind)
 
-    def row_swap(pair):
-        b = pair.reshape(2, micro, per_row, rows, part, width).transpose(3, 0, 2, 1, 4, 5)
+    def row_swap(own):
+        b = own.reshape(micro, per_row, rows, part, width).transpose(2, 1, 0, 3, 4)
         b = lax.all_to_all(b, "row", split_axis=0, concat_axis=0, tiled=True)
-        b = b.reshape(rows, 2, per_row, block_rows, width)
-        return (b[:, i].reshape(rows * per_row, block_rows, width) for i in range(2))
+        return b.reshape(rows * per_row, block_rows, width)
 
     def col_swap(b):
         return lax.all_to_all(b, "col", split_axis=0, concat_axis=0, tiled=True)
@@ -201,40 +200,60 @@
     def side_by_side(b):
         return b.transpose(1, 0, 2).reshape(block_rows, cols * width)
 
-    def from_rows(block):
+    def from_rows(block, *earlier):
         b = block.reshape(block_rows, cols, width).transpose(1, 0, 2)
-        b = lax.all_to_all(b, "col", split_axis=0, concat_axis=0, tiled=True)
-        b = b.reshape(rows, per_row, micro, part, width)
-        b = lax.all_to_all(b, "row", split_axis=0, concat_axis=0, tiled=True)
-        return b.transpose(2, 1, 0, 3, 4).reshape(micro, own_tokens, width)
-
-    def ring_gather(own):
+        b = col_swap(b).reshape(rows, per_row, micro, part, width)
+        if earlier:
+            b = lax.all_to_all(after(b, *earlier), "row", split_axis=0, concat_axis=0, tiled=True)
+            return b.transpose(2, 1, 0, 3, 4).reshape(micro, own_tokens, width)
+        b = b.transpose(0, 2, 1, 3, 4)
+        whole = jnp.zeros((micro, per_row, rows, part, width), BF)
+        for step in range(rows):
+            other = partner(me, step)
+            source = me ^ step if rows & (rows - 1) == 0 else (me - step) % rows
+            piece = lax.dynamic_index_in_dim(b, other, 0, keepdims=False)
+            if step:
+                piece = lax.ppermute(piece, "row", [(r, partner(r, step)) for r in range(rows)])
+            whole = lax.dynamic_update_slice_in_dim(whole, piece[:, :, None], source, 2)
+        return whole.reshape(micro, own_tokens, width)
+
+    def partner(r, step):
+        return r ^ step if rows & (rows - 1) == 0 else (r + step) % rows
+
+    far = rows // 2
+    cut = block_rows // 2
+
+    def ring_gather(own, *earlier):
         pieces = [None] * rows
         pieces[0] = own
         fore, back = own, own
-        far = rows // 2
-        cut = block_rows // 2
         for step in range(1, far):
             fore, back = up(fore), down(back)
             pieces[rows - step], pieces[step] = fore, back
+        if earlier:
+            fore, back = lax.optimization_barrier((fore, back) + earlier)[:2]
         pieces[far] = jnp.concatenate([up(fore[:cut]), down(back[cut:])], axis=0)
         return jnp.concatenate(pieces, axis=0)
 
-    def ring_scatter(total):
-        chunk = lambda j: total[j * block_rows : (j + 1) * block_rows]
-        far = rows // 2
-        cut = block_rows // 2
-        half_up, half_down = up(chunk(far)[:cut].astype(BF)), down(chunk(far)[cut:].astype(BF))
+    def chunk(total, j):
+        return total[j * block_rows : (j + 1) * block_rows]
+
+    def ring_open(total):
+        last = chunk(total, far)
+        return up(last[:cut]), down(last[cut:])
+
+    def ring_close(total, halves):
+        half_up, half_down = halves
         fore = back = None
         for step in range(far - 1, 0, -1):
-            a, b = chunk(step), chunk(rows - step)
+            a, b = chunk(total, step).astype(F32), chunk(total, rows - step).astype(F32)
             if fore is None:
                 a = jnp.concatenate([a[:cut] + half_up.astype(F32), a[cut:]], axis=0)
                 b = jnp.concatenate([b[:cut], b[cut:] + half_down.astype(F32)], axis=0)
             else:
                 a, b = a + fore.astype(F32), b + back.astype(F32)
             fore, back = up(a.astype(BF)), down(b.astype(BF))
-        return chunk(0) + fore.astype(F32) + back.astype(F32)
+        return chunk(total, 0).astype(F32) + fore.astype(F32) + back.astype(F32)
 
     def norm(block):
         block = block.astype(F32)
@@ -249,35 +268,41 @@
         )
 
     gains = jnp.stack([first_gain, first_shift, second_gain, second_shift])
-    gains = broadcast(gains, "col", cols).transpose(1, 0, 2).reshape(4, cols * width)
+    spread_gains = broadcast(gains, "col", cols)
+    gains = spread_gains.transpose(1, 0, 2).reshape(4, cols * width)
     expand_w = lax.all_gather(expand_weight, "col", axis=0, tiled=True)
-    x_half, cot_half = row_swap(jnp.stack([inputs, cotangent]))
-    reduce_w = lax.all_gather(after(reduce_weight, x_half), "col", axis=1, tiled=True)
+    x_half = row_swap(after(inputs, spread_gains))
+    cot_half = row_swap(after(cotangent, x_half))
+    x_part = col_swap(after(x_half, cot_half))
+    reduce_w = lax.all_gather(after(reduce_weight, x_part), "col", axis=1, tiled=True)
     mixed_weight = jnp.concatenate([merged_weight, output_weight.T], axis=1)
-    x_part = col_swap(after(x_half, gains))
-    mixed_w = lax.all_gather(after(mixed_weight, x_part), "col", axis=0, tiled=True)
+    cot_part = col_swap(after(cot_half, x_part))
     merged_cols = merged_weight.shape[1]
-    merged_w, output_wt = mixed_w[:, :merged_cols], mixed_w[:, merged_cols:]
-    cot_part = col_swap(after(cot_half, x_part))
     x_part = side_by_side(x_part)
     x_seq = ring_gather(x_part)
-    cot_part = side_by_side(after(cot_part, x_seq))
-    cot_seq = ring_gather(cot_part)
 
     normed, _ = norm(x_seq)
     attend_in = (normed * gains[0] + gains[1]).astype(BF)
     expand_in = (normed * gains[2] + gains[3]).astype(BF)
 
     expand_pre = lax.optimization_barrier(mm(expand_in, expand_w) + expand_bias)
+    cot_part = side_by_side(after(cot_part, expand_pre[:8, :128]))
+    mixed_w = lax.all_gather(after(mixed_weight, cot_part), "col", axis=0, tiled=True)
+    merged_w, output_wt = mixed_w[:, :merged_cols], mixed_w[:, merged_cols:]
     phi_sum = 0.5 * (1.0 + lax.erf(expand_pre * (0.5 ** 0.5)))
     density = jnp.exp(-0.5 * expand_pre * expand_pre) * 0.3989422804014327
     activated = (expand_pre * phi_sum).astype(BF)
     slope = (phi_sum + expand_pre * density).astype(BF)
     activated, slope = lax.optimization_barrier((activated, slope))
+    branch_ff = mm(activated, reduce_w).astype(BF)
+    cot_seq = ring_gather(cot_part, branch_ff)
 
     def scatter_weight(grad):
         return lax.psum_scatter(grad, "col", scatter_dimension=0, tiled=True).astype(F32)
 
+    cot_seq, branch_ff, attend_in, *tables = lax.optimization_barrier(
+        (cot_seq, branch_ff, attend_in) + rotary_tables()
+    )
     reduce_dot = contract_first(cot_seq, activated).astype(BF)
     reduce_grad = scatter_weight(reduce_dot).T
     grad_act = contract_last(after(cot_seq, reduce_dot), reduce_w)
@@ -289,30 +314,20 @@
     merged_pre = mm(after(attend_in, expand_dot), merged_w) + merged_bias
     grad_mix = mm(after(cot_seq, expand_dot), output_wt).astype(BF)
     mix, grad_merged = attention(
-        slots, piece_starts.reshape(-1), merged_pre, grad_mix, micro, rows
-    )
-    attend_late, cot_late, mix_late = lax.optimization_barrier(
-        (attend_in, cot_seq, mix, reduce_grad)
-    )[:3]
-    mixed_dot = jnp.concatenate(
-        [
-            contract_first(attend_late, grad_merged).astype(BF),
-            contract_first(cot_late, mix_late).astype(BF),
-        ],
-        axis=1,
-    )
-    mixed_grad = scatter_weight(mixed_dot)
-    merged_grad, output_grad = mixed_grad[:, :merged_cols], mixed_grad[:, merged_cols:].T
-
-    mix, activated = after((mix, activated), mixed_dot)
-    branch = contract_last(mix, output_wt) + mm(activated, reduce_w)
-    grad_pre, grad_merged, branch = lax.optimization_barrier(
-        (grad_pre, grad_merged, branch, expand_grad)
-    )[:3]
-    branch = from_rows(ring_scatter(branch).astype(BF))
-    result = inputs.astype(F32) + branch.astype(F32) + output_bias + reduce_bias
-    result = result.astype(BF)
-
+        slots, piece_starts.reshape(-1), merged_pre, grad_mix, tables, micro, rows
+    )
+    branch = (contract_last(mix, output_wt) + branch_ff).astype(BF)
+    halves = ring_open(branch)
+    grad_merged, attend_late = lax.optimization_barrier(
+        (grad_merged, attend_in, branch, reduce_grad)
+    )[:2]
+    merged_dot = contract_first(attend_late, grad_merged).astype(BF)
+    merged_grad = scatter_weight(merged_dot)
+
+    grad_merged, grad_pre, half_up, half_down = lax.optimization_barrier(
+        (grad_merged, grad_pre) + halves + (merged_dot,)
+    )[:4]
+    branch = ring_close(branch, (half_up, half_down))
     grad_first = contract_last(grad_merged, merged_w)
     grad_second = contract_last(grad_pre, expand_w)
     norm_sums = jnp.stack(
@@ -323,15 +338,8 @@
             jnp.sum(grad_second, axis=0),
         ]
     )
-    grad_hat = ring_scatter(grad_first * gains[0] + grad_second * gains[2])
-    part_normed, part_inverse = norm(x_part)
-    norm_part = part_inverse * (
-        grad_hat
-        - jnp.mean(grad_hat, axis=-1, keepdims=True)
-        - part_normed * jnp.mean(grad_hat * part_normed, axis=-1, keepdims=True)
-    )
-    input_grad = cotangent.astype(F32) + from_rows(norm_part.astype(BF)).astype(F32)
-
+    grad_hat = (grad_first * gains[0] + grad_second * gains[2]).astype(BF)
+    halves = ring_open(grad_hat)
     merged_b = jnp.sum(grad_merged.astype(F32), axis=0)
     shift_b = jnp.sum(cotangent.astype(F32), axis=(0, 1))
     sums = jnp.concatenate(
@@ -342,12 +350,41 @@
         ],
         axis=1,
     ).reshape(cols, -1, 128)
-    sums = lax.all_to_all(sums, "col", split_axis=0, concat_axis=0, tiled=True)
-    sums = jnp.sum(sums.reshape(cols, -1), axis=0)
+    spread_sums = lax.all_to_all(sums, "col", split_axis=0, concat_axis=0, tiled=True)
+    mix_late, cot_late = lax.optimization_barrier(
+        (mix, cot_seq, grad_hat, expand_grad, branch, spread_sums)
+    )[:2]
+    output_dot = contract_first(cot_late, mix_late).astype(BF)
+    output_grad = scatter_weight(after(output_dot, merged_grad)).T
+    halves = lax.optimization_barrier(halves + (output_dot,))[:2]
+    grad_hat = ring_close(grad_hat, halves)
+    sums = jnp.sum(spread_sums.reshape(cols, -1), axis=0)
     merged_b = sums[4 * width : 4 * width + merged_cols]
     expand_b = sums[4 * width + merged_cols :]
     tail = jnp.concatenate([sums[: 4 * width], shift_b]).reshape(-1, 128)
-    tail = jnp.sum(broadcast(tail, "row", rows), axis=0).reshape(5, width)
+    if rows & (rows - 1) == 0:
+        step = 1
+        while step < rows:
+            far_tail = lax.ppermute(tail, "row", [(r, r ^ step) for r in range(rows)])
+            tail = tail + far_tail
+            step *= 2
+    else:
+        far_tail = broadcast(tail, "row", rows)
+        tail = jnp.sum(far_tail, axis=0)
+    tail = tail.reshape(5, width)
+    branch = from_rows(branch.astype(BF))
+    result = inputs.astype(F32) + branch.astype(F32) + output_bias + reduce_bias
+    result = result.astype(BF)
+
+    part_normed, part_inverse = norm(x_part)
+    norm_part = part_inverse * (
+        grad_hat
+        - jnp.mean(grad_hat, axis=-1, keepdims=True)
+        - part_normed * jnp.mean(grad_hat * part_normed, axis=-1, keepdims=True)
+    )
+
+    norm_part = after(norm_part.astype(BF), output_grad, merged_grad)
+    input_grad = cotangent.astype(F32) + from_rows(norm_part, result, far_tail).astype(F32)
     norm_sums, shift_b = tail[:4], tail[4]
     return (
         result,

time: 928 us -> 797 us (0.86)
  waiting for transfers between devices: 275 us -> 206 us
  blocking collectives: 160 us -> 125 us
  other arithmetic: 99.7 us -> 88.4 us
  starting transfers between devices: 55.5 us -> 44.4 us
    all_to_all x6 -> x2, waiting for transfers between devices: 83.4 us -> 19.2 us  [the longest x1 19.2 us: from_rows(): lax.all_to_all(after(b, *earlier), 'row', split_axis=0, concat_axis=0, ti...]
    all_to_all x1 -> x3, waiting for transfers between devices: 0.01 us -> 50.9 us  [col_swap(): return lax.all_to_all(b, 'col', split_axis=0, concat_axis=0, tiled=True)]
    ppermute x8, waiting for transfers between devices: 117 us -> 72.6 us  [body(): up = lambda v: lax.ppermute(v, 'row', ahead)]
    all_to_all x1, blocking collectives: 98.5 us -> 57.9 us  [col_swap(): return lax.all_to_all(b, 'col', split_axis=0, concat_axis=0, tiled=True)]
    ppermute x8, waiting for transfers between devices: 74.6 us -> 35.7 us  [body(): down = lambda v: lax.ppermute(v, 'row', behind)]
    ppermute x0 -> x5, waiting for transfers between devices: none -> 23.1 us  [the longest x3 11.7 us: from_rows(): lax.ppermute(piece, 'row', [(r, partner(r, step)) for r in range(rows)])]
    all_to_all x6 -> x2, starting transfers between devices: 22.4 us -> 7.82 us  [the longest x1 4.43 us: from_rows(): lax.all_to_all(after(b, *earlier), 'row', split_axis=0, concat_axis=0, ti...]
    reduce_scatter x3 -> x4, starting transfers between devices: 11.4 us -> 0.92 us  [scatter_weight(): lax.psum_scatter(grad, 'col', scatter_dimension=0, tiled=True).astype(F32)]
  transfers between devices with their start and end apart: 29 -> 33, of which waited for: 17 -> 16; matrix products, arithmetic and copies ran while one was open for 36% -> 45% of each run, Pallas kernels for 2% -> 3%
where the time goes in v3:
time: 797 us; the launch traced here: 788 us
  matrix products  225 us (28%)
  waiting for transfers between devices  206 us (26%)
  blocking collectives  125 us (16%)
  other arithmetic  88.4 us (11%)
  local copies, waits for them, and re-layouts  62.5 us (8%)
  starting transfers between devices  44.4 us (6%)
  Pallas kernels  21 us (3%)
  between operations  15.1 us (2%)
    dot_general x4, matrix products, contract_last(): lax.dot_general(left, right, (((1,), (1,)), ((), ())), preferred_element_...  81.7 us
    dot_general x4, matrix products, mm(): return jnp.dot(left, right, preferred_element_type=F32)  73.2 us
    ppermute x8, waiting for transfers between devices, body(): up = lambda v: lax.ppermute(v, 'row', ahead)  72.6 us
    dot_general x4, matrix products, contract_first(): lax.dot_general(left, right, (((0,), (0,)), ((), ())), preferred_element_...  70.6 us
    all_to_all x1, blocking collectives, col_swap(): return lax.all_to_all(b, 'col', split_axis=0, concat_axis=0, tiled=True)  57.9 us
    all_to_all x2, blocking collectives, row_swap(): b = lax.all_to_all(b, 'row', split_axis=0, concat_axis=0, tiled=True)  55.5 us
    all_to_all x3, waiting for transfers between devices, col_swap(): return lax.all_to_all(b, 'col', split_axis=0, concat_axis=0, tiled=True)  50.9 us
    ppermute x8, waiting for transfers between devices, body(): down = lambda v: lax.ppermute(v, 'row', behind)  35.7 us
  transfers between devices with their start and end apart: 33, of which 16 were waited for; matrix products, arithmetic and copies ran while one was open for 45% of the time, Pallas kernels for 3%

profile of v3, /device:TPU:0, one launch (start us, length us, event | category | flops | bytes accessed | tf_op | source)
XLA Modules:
  0.0 788.5 jit_solution(17236474558796878742)
XLA Ops:
  8.7 11.9 %all_to_all.45 = f32[8,4,256]{2,1,0:T(4,128)S(1)} all-to-all(f32[8,4,256]{2,1,0:T(4,128)S(1)} %broadcast_in_dim.21), channel_id=1, replica_groups=mesh['row'=4,'col'=8] {'col'}, dimensions={0} | all-to-all | bytes 65536 | tf_op jit(solution)/shard_map/all_to_all | solution.py:266
  22.6 28.8 %all_to_all.46 = bf16[4,2,2,256,256]{4,3,1,2,0:T(8,128)(2,1)S(1)} all-to-all(bf16[4,2,2,256,256]{4,3,1,2,0:T(8,128)(2,1)S(1)} %copy.98), channel_id=1, replica_groups=mesh['row'=4,'col'=8] {'row'}, dimensions={0} | all-to-all | bytes 4194304 | tf_op jit(solution)/shard_map/all_to_all | solution.py:194
  51.7 26.7 %all_to_all.47 = bf16[4,2,2,256,256]{4,3,1,2,0:T(8,128)(2,1)S(1)} all-to-all(bf16[4,2,2,256,256]{4,3,1,2,0:T(8,128)(2,1)S(1)} %copy.100), channel_id=1, replica_groups=mesh['row'=4,'col'=8] {'row'}, dimensions={0} | all-to-all | bytes 4194304 | tf_op jit(solution)/shard_map/all_to_all | solution.py:194
  79.9 57.9 %all_to_all.48 = bf16[8,512,256]{2,1,0:T(8,128)(2,1)} all-to-all(bf16[8,512,256]{2,1,0:T(8,128)(2,1)S(1)} %bitcast.141), channel_id=1, replica_groups=mesh['row'=4,'col'=8] {'col'}, dimensions={0} | all-to-all | bytes 4194304 | tf_op jit(solution)/shard_map/all_to_all | solution.py:198
  149.4 38.1 %collective-permute-done.3 = bf16[512,2048]{1,0:T(8,128)(2,1)} collective-permute-done((bf16[512,2048]{1,0:T(8,128)(2,1)S(1)}, bf16[512,2048]{1,0:T(8,128)(2,1)}, u32[]{:S(2)}, u32[]{:S(2)}) %collective-permute-start.3) | collective-permute-done | bytes 2097184 | tf_op jit(solution)/shard_map/ppermute | solution.py:189
  202.0 12.4 %collective-permute-done.4 = bf16[256,2048]{1,0:T(8,128)(2,1)} collective-permute-done((bf16[256,2048]{1,0:T(8,128)(2,1)}, bf16[256,2048]{1,0:T(8,128)(2,1)}, u32[]{:S(2)}, u32[]{:S(2)}) %collective-permute-start.4) | collective-permute-done | bytes 1048608 | tf_op jit(solution)/shard_map/ppermute | solution.py:189
  226.6 23.9 %all-to-all-done.4 = bf16[8,512,256]{2,1,0:T(8,128)(2,1)} async-done(((bf16[8,512,256]{2,1,0:T(8,128)(2,1)}), bf16[8,512,256]{2,1,0:T(8,128)(2,1)}, u32[]{:S(2)}, u32[]{:S(2)}) %all-to-all-start.4) | async-done | bytes 2097184 | tf_op jit(solution)/shard_map/all_to_all | solution.py:198
  256.0 21.8 %convolution_add_fusion.1 = f32[2048,2048]{1,0:T(8,128)S(1)} fusion(bf16[2048,2048]{1,0:T(8,128)(2,1)} %all-gather.4.cloned.1.call-done, f32[2048]{0:T(1024)S(1)} %copy-done.24, bf16[2048,2048]{1,0:T(8,128)(2,1)} %copy-done, f32[2048]{0:T(1024)S(1)} %bitcast.158, f32[2048]{0:T(1024)S(1)} %bitcast.155, f32[2048]{0:T(1024)S(1)} %add_rsqrt_fusion, ...), kind=kOutput, calls=%fused_computation.29 | convolution fusion | flops 17209229312 | bytes 33595392 | tf_op jit(solution)/shard_map/dot_general | solution.py:24
  286.5 23.6 %convolution_convert_fusion.2 = bf16[2048,2048]{1,0:T(8,128)(2,1)} fusion(bf16[2048,2048]{1,0:T(8,128)(2,1)} %get-tuple-element.51, bf16[2048,2048]{1,0:T(8,128)(2,1)} %all-gather.6.cloned.1.call-done), kind=kOutput, calls=%fused_computation.32 | convolution fusion | flops 17184063488 | bytes 25165824 | tf_op jit(solution)/shard_map/dot_general | solution.py:24
  325.9 12.4 %collective-permute-done.6 = bf16[256,2048]{0,1:T(8,128)(2,1)S(1)} collective-permute-done((bf16[256,2048]{0,1:T(8,128)(2,1)S(1)}, bf16[256,2048]{0,1:T(8,128)(2,1)S(1)}, u32[]{:S(2)}, u32[]{:S(2)}) %collective-permute-start.6) | collective-permute-done | bytes 1048608 | tf_op jit(solution)/shard_map/ppermute | solution.py:189
  343.8 19.5 %convolution_convert_fusion.1 = bf16[2048,2048]{1,0:T(8,128)(2,1)} fusion(bf16[2048,2048]{0,1:T(8,128)(2,1)S(1)} %constant_dynamic-update-slice_fusion.5, bf16[2048,2048]{1,0:T(8,128)(2,1)S(1)} %bitcast.145), kind=kOutput, calls=%fused_computation.31 | convolution fusion | flops 17184063488 | bytes 25165824 | tf_op jit(solution)/shard_map/dot_general | solution.py:32
  363.8 24.6 %convert_reduce_fusion.1 = (f32[2048]{0:T(1024)S(1)}, bf16[2048,2048]{1,0:T(8,128)(2,1)S(1)}) fusion(bf16[2048,2048]{1,0:T(8,128)(2,1)} %get-tuple-element.58, bf16[2048,2048]{0,1:T(8,128)(2,1)} %copy-done.7, bf16[2048,2048]{1,0:T(8,128)(2,1)} %all-gather.6.cloned.1.call-done), kind=kOutput, calls=%fused_computation.21 | convolution fusion | flops 17200838656 | bytes 33562624 | tf_op jit(solution)/shard_map/dot_general | solution.py:28
  391.7 22.6 %convolution_convert_fusion = bf16[2048,2048]{1,0:T(8,128)(2,1)} fusion(bf16[2048,2048]{1,0:T(8,128)(2,1)S(1)} %get-tuple-element.72, bf16[2048,2048]{1,0:T(8,128)(2,1)} %copy-done, f32[2048]{0:T(1024)S(1)} %bitcast.159, f32[2048]{0:T(1024)S(1)} %bitcast.156, f32[2048]{0:T(1024)S(1)} %add_rsqrt_fusion, f32[2048]{0:T(1024)S(1)} %broadcast_multiply_fusion), kind=kOutput, calls=%fused_computation.30 | convolution fusion | flops 17209229312 | bytes 25198592 | tf_op jit(solution)/shard_map/dot_general | solution.py:32
  428.2 17.7 %convolution_add_fusion = f32[2048,1536]{1,0:T(8,128)} fusion(bf16[2048,2048]{1,0:T(8,128)(2,1)} %fusion.9, f32[1536]{0:T(1024)S(1)} %copy-done.25, bf16[2048,2048]{1,0:T(8,128)(2,1)S(1)} %copy-done.23), kind=kOutput, calls=%fused_computation.28 | convolution fusion | flops 12888047616 | bytes 27271168 | tf_op jit(solution)/shard_map/dot_general | solution.py:24
  445.9 21.0 %attention.1 = (bf16[4,2,256,512]{3,2,1,0:T(8,128)(2,1)}, bf16[4,2,256,1536]{3,2,1,0:T(8,128)(2,1)}) custom-call(s32[4]{0:T(128)} %and_select_fusion.slot_ref, s32[4]{0:T(128)} %reshape.176.starts_ref, f32[4,2,256,1536]{3,2,1,0:T(8,128)} %bitcast.164, bf16[4,2,256,512]{3,2,1,0:T(8,128)(2,1)} %bitcast.167, f32[1024,128]{1,0:T(8,128)} %get-tuple-element.62.cos_ref, ...), custom_call_target="tpu_custom_call" | custom-call | flops 16106127360 | bytes 23068672 | tf_op jit(solution)/shard_map/attention/pallas_call | solution.py:124
  489.8 19.3 %convolution_convert_fusion.3 = bf16[2048,1536]{1,0:T(8,128)(2,1)} fusion(bf16[2048,2048]{1,0:T(8,128)(2,1)} %fusion.9, bf16[2048,1536]{1,0:T(8,128)(2,1)} %bitcast.146), kind=kOutput, calls=%fused_computation.33 | convolution fusion | flops 12888047616 | bytes 20971520 | tf_op jit(solution)/shard_map/dot_general | solution.py:32
  515.9 24.8 %fusion.38 = f32[2048,2048]{1,0:T(8,128)} fusion(bf16[2048,2048]{1,0:T(8,128)(2,1)} %copy-done.28, bf16[2048,2048]{1,0:T(8,128)(2,1)} %all-gather.4.cloned.1.call-done), kind=kOutput, calls=%fused_computation.123 | convolution fusion | flops 17179869184 | bytes 33554432 | tf_op jit(solution)/shard_map/dot_general | solution.py:28
  540.7 25.2 %fusion.10 = (f32[2048]{0:T(1024)S(1)}, f32[2048]{0:T(1024)S(1)}, f32[2048]{0:T(1024)S(1)}, f32[2048]{0:T(1024)S(1)}, bf16[2048,2048]{1,0:T(8,128)(2,1)}) fusion(bf16[2048,2048]{1,0:T(8,128)(2,1)} %copy-done, f32[2048]{0:T(1024)S(1)} %copy-done.11, f32[2048]{0:T(1024)S(1)} %copy-done.9, f32[2048,2048]{1,0:T(8,128)} %fusion.38, f32[2048]{0:T(1024)S(1)} %bitcast.157, ...), kind=kOutput, calls=%fused_computation.13 | convolution fusion | flops 12939419648 | bytes 46202880 | tf_op jit(solution)/shard_map/dot_general | solution.py:28
  632.4 24.3 %collective-permute-done.18 = bf16[512,2048]{1,0:T(8,128)(2,1)} collective-permute-done((bf16[512,2048]{1,0:T(8,128)(2,1)}, bf16[512,2048]{1,0:T(8,128)(2,1)}, u32[]{:S(2)}, u32[]{:S(2)}) %collective-permute-start.18) | collective-permute-done | bytes 2097184 | tf_op jit(solution)/shard_map/ppermute | solution.py:190
  678.0 12.2 %all-to-all-done.5 = bf16[8,512,256]{2,1,0:T(8,128)(2,1)} async-done(((bf16[8,512,256]{2,1,0:T(8,128)(2,1)}), bf16[8,512,256]{2,1,0:T(8,128)(2,1)}, u32[]{:S(2)}, u32[]{:S(2)}) %all-to-all-start.5) | async-done | bytes 2097184 | tf_op jit(solution)/shard_map/all_to_all | solution.py:198
  700.1 11.4 %collective-permute-done.19 = f32[10,128]{1,0:T(8,128)S(1)} collective-permute-done((f32[10,128]{1,0:T(8,128)S(1)}, f32[10,128]{1,0:T(8,128)S(1)}, u32[]{:S(2)}, u32[]{:S(2)}) %collective-permute-start.19) | collective-permute-done | bytes 5152 | tf_op jit(solution)/shard_map/ppermute | solution.py:368
  714.8 11.7 %collective-permute-done.14 = bf16[2,2,256,256]{3,2,0,1:T(8,128)(2,1)S(1)} collective-permute-done((bf16[2,2,256,256]{3,2,0,1:T(8,128)(2,1)S(1)}, bf16[2,2,256,256]{3,2,0,1:T(8,128)(2,1)S(1)}, u32[]{:S(2)}, u32[]{:S(2)}) %collective-permute-start.14) | collective-permute-done | bytes 524320 | tf_op jit(solution)/shard_map/ppermute | solution.py:216
  728.8 14.9 %all-to-all-done.7 = bf16[8,512,256]{2,1,0:T(8,128)(2,1)} async-done(((bf16[8,512,256]{2,1,0:T(8,128)(2,1)}), bf16[8,512,256]{2,1,0:T(8,128)(2,1)}, u32[]{:S(2)}, u32[]{:S(2)}) %all-to-all-start.7) | async-done | bytes 2097184 | tf_op jit(solution)/shard_map/all_to_all | solution.py:198
  756.9 19.2 %all-to-all-done.8 = bf16[4,2,2,256,256]{4,3,1,2,0:T(8,128)(2,1)} async-done(((bf16[4,2,2,256,256]{4,3,1,2,0:T(8,128)(2,1)}), bf16[4,2,2,256,256]{4,3,1,2,0:T(8,128)(2,1)}, u32[]{:S(2)}, u32[]{:S(2)}) %all-to-all-start.8) | async-done | bytes 2097184 | tf_op jit(solution)/shard_map/all_to_all | solution.py:207
  (229 shorter events, 247.6 us)
Async XLA Ops:
  7.2 248.7 %all-gather.4.cloned.1.call-start = ((), (), s32[]{:S(2)}) async-start(), calls=%async_computation.13 | async-start | bytes 9437184 | tf_op jit(solution)/shard_map/all_gather | solution.py:273
  7.9 278.6 %all-gather.6.cloned.1.call-start = ((), (), s32[]{:S(2)}) async-start(), calls=%async_computation.14 | async-start | bytes 9437184 | tf_op jit(solution)/shard_map/all_gather | solution.py:277
  139.7 47.8 %collective-permute-start.3 = (bf16[512,2048]{1,0:T(8,128)(2,1)S(1)}, bf16[512,2048]{1,0:T(8,128)(2,1)}, u32[]{:S(2)}, u32[]{:S(2)}) collective-permute-start(bf16[512,2048]{1,0:T(8,128)(2,1)S(1)} %bitcast.127), channel_id=1, source_target_pairs={{0,8},{8,24},{24,16},{16,0},{1,9},{9,25},{25,17},{17,1},{2,10},{10... | collective-permute-start | bytes 6291464 | tf_op jit(solution)/shard_map/ppermute | solution.py:189
  141.3 53.6 %collective-permute-start.2 = (bf16[512,2048]{1,0:T(8,128)(2,1)S(1)}, bf16[512,2048]{1,0:T(8,128)(2,1)}, u32[]{:S(2)}, u32[]{:S(2)}) collective-permute-start(bf16[512,2048]{1,0:T(8,128)(2,1)S(1)} %bitcast.128), channel_id=1, source_target_pairs={{8,0},{24,8},{16,24},{0,16},{9,1},{25,9},{17,25},{1,17},{10,2},{26... | collective-permute-start | bytes 6291464 | tf_op jit(solution)/shard_map/ppermute | solution.py:190
  145.0 105.5 %all-to-all-start.4 = ((bf16[8,512,256]{2,1,0:T(8,128)(2,1)}), bf16[8,512,256]{2,1,0:T(8,128)(2,1)}, u32[]{:S(2)}, u32[]{:S(2)}) async-start(bf16[8,512,256]{2,1,0:T(8,128)(2,1)} %bitcast.136), calls=%async_computation.4 | async-start | bytes 4194304 | tf_op jit(solution)/shard_map/all_to_all | solution.py:198
  149.4 268.7 %all-gather.8.cloned.1.call-start = ((), (), s32[]{:S(2)}) async-start(), calls=%async_computation.15 | async-start | bytes 9437184 | tf_op jit(solution)/shard_map/all_gather | solution.py:290
  189.8 24.6 %collective-permute-start.4 = (bf16[256,2048]{1,0:T(8,128)(2,1)}, bf16[256,2048]{1,0:T(8,128)(2,1)}, u32[]{:S(2)}, u32[]{:S(2)}) collective-permute-start(bf16[256,2048]{1,0:T(8,128)(2,1)} %slice.196), channel_id=1, source_target_pairs={{0,8},{8,24},{24,16},{16,0},{1,9},{9,25},{25,17},{17,1},{2,10},{10... | collective-permute-start | bytes 3145736 | tf_op jit(solution)/shard_map/ppermute | solution.py:189
  253.6 56.5 %collective-permute-start.1 = (bf16[512,2048]{0,1:T(8,128)(2,1)S(1)}, bf16[512,2048]{0,1:T(8,128)(2,1)}, u32[]{:S(2)}, u32[]{:S(2)}) collective-permute-start(bf16[512,2048]{0,1:T(8,128)(2,1)S(1)} %bitcast.137), channel_id=1, source_target_pairs={{0,8},{8,24},{24,16},{16,0},{1,9},{9,25},{25,17},{17,1},{2,10},{10... | collective-permute-start | bytes 6291464 | tf_op jit(solution)/shard_map/ppermute | solution.py:189
  255.1 55.0 %collective-permute-start = (bf16[512,2048]{0,1:T(8,128)(2,1)S(1)}, bf16[512,2048]{0,1:T(8,128)(2,1)}, u32[]{:S(2)}, u32[]{:S(2)}) collective-permute-start(bf16[512,2048]{0,1:T(8,128)(2,1)S(1)} %bitcast.138), channel_id=1, source_target_pairs={{8,0},{24,8},{16,24},{0,16},{9,1},{25,9},{17,25},{1,17},{10,2},{26... | collective-permute-start | bytes 6291464 | tf_op jit(solution)/shard_map/ppermute | solution.py:190
  255.7 231.3 %reduce-scatter.5.cloned.1.call-start = ((), (), s32[]{:S(2)}) async-start(), calls=%async_computation.16 | async-start | bytes 9437184 | tf_op jit(solution)/shard_map/reduce_scatter | solution.py:301
  312.7 25.8 %collective-permute-start.7 = (bf16[256,2048]{0,1:T(8,128)(2,1)S(1)}, bf16[256,2048]{0,1:T(8,128)(2,1)S(1)}, u32[]{:S(2)}, u32[]{:S(2)}) collective-permute-start(bf16[256,2048]{0,1:T(8,128)(2,1)S(1)} %slice.162), channel_id=1, source_target_pairs={{8,0},{24,8},{16,24},{0,16},{9,1},{25,9},{17,25},{1,17},{10,2},{26... | collective-permute-start | bytes 3145736 | tf_op jit(solution)/shard_map/ppermute | solution.py:190
  363.3 216.8 %reduce-scatter.7.cloned.1.call-start = ((), (), s32[]{:S(2)}) async-start(), calls=%async_computation.17 | async-start | bytes 9437184 | tf_op jit(solution)/shard_map/reduce_scatter | solution.py:301
  414.3 199.4 %reduce-scatter.9.cloned.1.call-start = ((), (), s32[]{:S(2)}) async-start(), calls=%async_computation.18 | async-start | bytes 7077888 | tf_op jit(solution)/shard_map/reduce_scatter | solution.py:301
  485.0 24.2 %collective-permute-start.9 = (bf16[256,2048]{1,0:T(8,128)(2,1)}, bf16[256,2048]{1,0:T(8,128)(2,1)S(1)}, u32[]{:S(2)}, u32[]{:S(2)}) collective-permute-start(bf16[256,2048]{1,0:T(8,128)(2,1)} %get-tuple-element.185), channel_id=1, source_target_pairs={{8,0},{24,8},{16,24},{0,16},{9,1},{25,9},{17,25},{1,17},{10,2},{26... | collective-permute-start | bytes 3145736 | tf_op jit(solution)/shard_map/ppermute | solution.py:190
  513.5 69.4 %collective-permute-start.11 = (bf16[512,2048]{1,0:T(8,128)(2,1)}, bf16[512,2048]{1,0:T(8,128)(2,1)}, u32[]{:S(2)}, u32[]{:S(2)}) collective-permute-start(bf16[512,2048]{1,0:T(8,128)(2,1)} %pad_maximum_fusion.1), channel_id=1, source_target_pairs={{8,0},{24,8},{16,24},{0,16},{9,1},{25,9},{17,25},{1,17},{10,2},{26... | collective-permute-start | bytes 6291464 | tf_op jit(solution)/shard_map/ppermute | solution.py:190
  515.2 67.7 %collective-permute-start.10 = (bf16[512,2048]{1,0:T(8,128)(2,1)S(1)}, bf16[512,2048]{1,0:T(8,128)(2,1)}, u32[]{:S(2)}, u32[]{:S(2)}) collective-permute-start(bf16[512,2048]{1,0:T(8,128)(2,1)S(1)} %pad_maximum_fusion), channel_id=1, source_target_pairs={{0,8},{8,24},{24,16},{16,0},{1,9},{9,25},{25,17},{17,1},{2,10},{10... | collective-permute-start | bytes 6291464 | tf_op jit(solution)/shard_map/ppermute | solution.py:189
  573.9 99.9 %reduce-scatter.11.cloned.1.call-start = ((), (), s32[]{:S(2)}) async-start(), calls=%async_computation.19 | async-start | bytes 2359296 | tf_op jit(solution)/shard_map/reduce_scatter | solution.py:301
  577.9 25.7 %collective-permute-start.16 = (bf16[256,2048]{1,0:T(8,128)(2,1)}, bf16[256,2048]{1,0:T(8,128)(2,1)}, u32[]{:S(2)}, u32[]{:S(2)}) collective-permute-start(bf16[256,2048]{1,0:T(8,128)(2,1)} %get-tuple-element.179), channel_id=1, source_target_pairs={{8,0},{24,8},{16,24},{0,16},{9,1},{25,9},{17,25},{1,17},{10,2},{26... | collective-permute-start | bytes 3145736 | tf_op jit(solution)/shard_map/ppermute | solution.py:190
  579.4 25.6 %collective-permute-start.15 = (bf16[256,2048]{1,0:T(8,128)(2,1)}, bf16[256,2048]{1,0:T(8,128)(2,1)}, u32[]{:S(2)}, u32[]{:S(2)}) collective-permute-start(bf16[256,2048]{1,0:T(8,128)(2,1)} %get-tuple-element.180), channel_id=1, source_target_pairs={{0,8},{8,24},{24,16},{16,0},{1,9},{9,25},{25,17},{17,1},{2,10},{10... | collective-permute-start | bytes 3145736 | tf_op jit(solution)/shard_map/ppermute | solution.py:189
  609.6 47.1 %collective-permute-start.18 = (bf16[512,2048]{1,0:T(8,128)(2,1)}, bf16[512,2048]{1,0:T(8,128)(2,1)}, u32[]{:S(2)}, u32[]{:S(2)}) collective-permute-start(bf16[512,2048]{1,0:T(8,128)(2,1)} %pad_maximum_fusion.3), channel_id=1, source_target_pairs={{8,0},{24,8},{16,24},{0,16},{9,1},{25,9},{17,25},{1,17},{10,2},{26... | collective-permute-start | bytes 6291464 | tf_op jit(solution)/shard_map/ppermute | solution.py:190
  619.2 45.8 %collective-permute-start.17 = (bf16[512,2048]{1,0:T(8,128)(2,1)}, bf16[512,2048]{1,0:T(8,128)(2,1)}, u32[]{:S(2)}, u32[]{:S(2)}) collective-permute-start(bf16[512,2048]{1,0:T(8,128)(2,1)} %pad_maximum_fusion.2), channel_id=1, source_target_pairs={{0,8},{8,24},{24,16},{16,0},{1,9},{9,25},{25,17},{17,1},{2,10},{10... | collective-permute-start | bytes 6291464 | tf_op jit(solution)/shard_map/ppermute | solution.py:189
  623.8 66.4 %all-to-all-start.5 = ((bf16[8,512,256]{2,1,0:T(8,128)(2,1)}), bf16[8,512,256]{2,1,0:T(8,128)(2,1)}, u32[]{:S(2)}, u32[]{:S(2)}) async-start(bf16[8,512,256]{2,1,0:T(8,128)(2,1)} %bitcast.140), calls=%async_computation.6 | async-start | bytes 4194304 | tf_op jit(solution)/shard_map/all_to_all | solution.py:198
  690.1 53.5 %all-to-all-start.7 = ((bf16[8,512,256]{2,1,0:T(8,128)(2,1)}), bf16[8,512,256]{2,1,0:T(8,128)(2,1)}, u32[]{:S(2)}, u32[]{:S(2)}) async-start(bf16[8,512,256]{2,1,0:T(8,128)(2,1)} %bitcast.135), calls=%async_computation.11 | async-start | bytes 4194304 | tf_op jit(solution)/shard_map/all_to_all | solution.py:198
  746.8 29.4 %all-to-all-start.8 = ((bf16[4,2,2,256,256]{4,3,1,2,0:T(8,128)(2,1)}), bf16[4,2,2,256,256]{4,3,1,2,0:T(8,128)(2,1)}, u32[]{:S(2)}, u32[]{:S(2)}) async-start(bf16[4,2,2,256,256]{4,3,1,2,0:T(8,128)(2,1)} %copy.114), calls=%async_computation.12 | async-start | bytes 4194304 | tf_op jit(solution)/shard_map/all_to_all | solution.py:207
  (40 other events, 1293.6 us)
Sparse Core Ops, SparseCore 0:
  9.6 91.6 all-gather.3
  138.0 125.3 all-gather.5
  265.6 81.9 all-gather.7
  363.4 87.1 reduce-scatter.4
  452.7 87.9 reduce-scatter.6
  542.9 70.8 reduce-scatter.8
  616.4 48.8 reduce-scatter.10

commit v4 on v3

--- a/solution.py
+++ b/solution.py
@@ -233,7 +233,7 @@
         if earlier:
             fore, back = lax.optimization_barrier((fore, back) + earlier)[:2]
         pieces[far] = jnp.concatenate([up(fore[:cut]), down(back[cut:])], axis=0)
-        return jnp.concatenate(pieces, axis=0)
+        return pieces
 
     def chunk(total, j):
         return total[j * block_rows : (j + 1) * block_rows]
@@ -268,65 +268,106 @@
         )
 
     gains = jnp.stack([first_gain, first_shift, second_gain, second_shift])
+    def add_up(value, axis, size):
+        if size & (size - 1):
+            spread = broadcast(value, axis, size)
+            return jnp.sum(spread, axis=0), spread
+        step = 1
+        while step < size:
+            taken = lax.ppermute(value, axis, [(r, r ^ step) for r in range(size)])
+            value = value + taken
+            step *= 2
+        return value, taken
+
     spread_gains = broadcast(gains, "col", cols)
     gains = spread_gains.transpose(1, 0, 2).reshape(4, cols * width)
     expand_w = lax.all_gather(expand_weight, "col", axis=0, tiled=True)
     x_half = row_swap(after(inputs, spread_gains))
     cot_half = row_swap(after(cotangent, x_half))
     x_part = col_swap(after(x_half, cot_half))
-    reduce_w = lax.all_gather(after(reduce_weight, x_part), "col", axis=1, tiled=True)
+    cot_part = col_swap(after(cot_half, x_part))
+    x_part = side_by_side(x_part)
+    x_pieces = ring_gather(x_part)
+    x_seq = jnp.concatenate(x_pieces, axis=0)
+    reduce_weight = after(reduce_weight, x_pieces[1], x_pieces[-1], cot_part)
+    reduce_w = lax.all_gather(reduce_weight, "col", axis=1, tiled=True)
+    merged_cols = merged_weight.shape[1]
     mixed_weight = jnp.concatenate([merged_weight, output_weight.T], axis=1)
-    cot_part = col_swap(after(cot_half, x_part))
-    merged_cols = merged_weight.shape[1]
-    x_part = side_by_side(x_part)
-    x_seq = ring_gather(x_part)
+    mixed_w = lax.all_gather(after(mixed_weight, cot_part), "col", axis=0, tiled=True)
+    merged_w, output_wt = mixed_w[:, :merged_cols], mixed_w[:, merged_cols:]
 
     normed, _ = norm(x_seq)
     attend_in = (normed * gains[0] + gains[1]).astype(BF)
     expand_in = (normed * gains[2] + gains[3]).astype(BF)
 
     expand_pre = lax.optimization_barrier(mm(expand_in, expand_w) + expand_bias)
-    cot_part = side_by_side(after(cot_part, expand_pre[:8, :128]))
-    mixed_w = lax.all_gather(after(mixed_weight, cot_part), "col", axis=0, tiled=True)
-    merged_w, output_wt = mixed_w[:, :merged_cols], mixed_w[:, merged_cols:]
+    cot_part = side_by_side(after(cot_part, x_seq))
     phi_sum = 0.5 * (1.0 + lax.erf(expand_pre * (0.5 ** 0.5)))
     density = jnp.exp(-0.5 * expand_pre * expand_pre) * 0.3989422804014327
     activated = (expand_pre * phi_sum).astype(BF)
     slope = (phi_sum + expand_pre * density).astype(BF)
     activated, slope = lax.optimization_barrier((activated, slope))
-    branch_ff = mm(activated, reduce_w).astype(BF)
-    cot_seq = ring_gather(cot_part, branch_ff)
+    core = lax.axis_index("col") % 2
+    other_core = [(c, c ^ 1) for c in range(cols)]
+    chips = [list(range(k, cols, 2)) for k in range(2)]
+
+    def own_and_other(value):
+        blocks = [value[:, c * width : (c + 1) * width] for c in range(cols)]
+        even, odd = blocks[::2], blocks[1::2]
+        own = [jnp.where(core == 0, a, b) for a, b in zip(even, odd)]
+        other = [jnp.where(core == 0, b, a) for a, b in zip(even, odd)]
+        return jnp.concatenate(own, axis=1), jnp.concatenate(other, axis=1)
+
+    cot_pieces = ring_gather(cot_part, activated)
+    cot_seq = jnp.concatenate(cot_pieces, axis=0)
+    cot_own, cot_other = (
+        jnp.concatenate(part, axis=0) for part in zip(*[own_and_other(p) for p in cot_pieces])
+    )
+    ready = (attend_in,) + own_and_other(expand_in) + own_and_other(attend_in) + rotary_tables()
+    cot_other, attend_in, expand_own, expand_other, attend_own, attend_other, *tables = (
+        lax.optimization_barrier((cot_other,) + ready)
+    )
+
+    def give(other, grad):
+        sent = contract_first(other, grad).astype(BF)
+        return sent, lax.ppermute(sent, "col", other_core)
+
+    def keep(own, grad, taken):
+        return (contract_first(own, grad) + taken.astype(F32)).astype(BF)
 
     def scatter_weight(grad):
-        return lax.psum_scatter(grad, "col", scatter_dimension=0, tiled=True).astype(F32)
-
-    cot_seq, branch_ff, attend_in, *tables = lax.optimization_barrier(
-        (cot_seq, branch_ff, attend_in) + rotary_tables()
-    )
-    reduce_dot = contract_first(cot_seq, activated).astype(BF)
+        grad = lax.psum_scatter(
+            grad, "col", scatter_dimension=0, tiled=True, axis_index_groups=chips
+        )
+        return grad.astype(F32)
+
+    reduce_sent, reduce_taken = give(cot_other, activated)
+    branch_ff = mm(after(activated, reduce_sent), reduce_w).astype(BF)
+    reduce_dot = keep(after(cot_own, branch_ff), activated, reduce_taken)
     reduce_grad = scatter_weight(reduce_dot).T
     grad_act = contract_last(after(cot_seq, reduce_dot), reduce_w)
     grad_pre = (grad_act * slope.astype(F32)).astype(BF)
     expand_b = jnp.sum(grad_pre.astype(F32), axis=0)
-    expand_dot = contract_first(expand_in, grad_pre).astype(BF)
-    expand_grad = scatter_weight(expand_dot)
-
-    merged_pre = mm(after(attend_in, expand_dot), merged_w) + merged_bias
-    grad_mix = mm(after(cot_seq, expand_dot), output_wt).astype(BF)
+    expand_sent, expand_taken = give(expand_other, grad_pre)
+    grad_mix = mm(after(cot_seq, expand_sent), output_wt).astype(BF)
+    merged_pre = mm(after(attend_in, grad_mix), merged_w) + merged_bias
     mix, grad_merged = attention(
         slots, piece_starts.reshape(-1), merged_pre, grad_mix, tables, micro, rows
     )
+    mix = after(mix, reduce_grad)
     branch = (contract_last(mix, output_wt) + branch_ff).astype(BF)
     halves = ring_open(branch)
-    grad_merged, attend_late = lax.optimization_barrier(
-        (grad_merged, attend_in, branch, reduce_grad)
+    expand_dot = keep(after(expand_own, branch), grad_pre, expand_taken)
+    expand_grad = scatter_weight(expand_dot)
+    grad_merged, attend_other = lax.optimization_barrier(
+        (grad_merged, attend_other, branch)
     )[:2]
-    merged_dot = contract_first(attend_late, grad_merged).astype(BF)
+    merged_sent, merged_taken = give(attend_other, grad_merged)
+    grad_merged, grad_pre, half_up, half_down = lax.optimization_barrier(
+        (grad_merged, grad_pre) + halves + (merged_sent,)
+    )[:4]
+    merged_dot = keep(attend_own, grad_merged, merged_taken)
     merged_grad = scatter_weight(merged_dot)
-
-    grad_merged, grad_pre, half_up, half_down = lax.optimization_barrier(
-        (grad_merged, grad_pre) + halves + (merged_dot,)
-    )[:4]
     branch = ring_close(branch, (half_up, half_down))
     grad_first = contract_last(grad_merged, merged_w)
     grad_second = contract_last(grad_pre, expand_w)
@@ -342,35 +383,23 @@
     halves = ring_open(grad_hat)
     merged_b = jnp.sum(grad_merged.astype(F32), axis=0)
     shift_b = jnp.sum(cotangent.astype(F32), axis=(0, 1))
-    sums = jnp.concatenate(
-        [
-            norm_sums.reshape(4, cols, width).transpose(1, 0, 2).reshape(cols, 4 * width),
-            jnp.broadcast_to(merged_b, (cols, merged_cols)),
-            jnp.broadcast_to(expand_b, (cols, expand_b.shape[0])),
-        ],
-        axis=1,
-    ).reshape(cols, -1, 128)
-    spread_sums = lax.all_to_all(sums, "col", split_axis=0, concat_axis=0, tiled=True)
-    mix_late, cot_late = lax.optimization_barrier(
-        (mix, cot_seq, grad_hat, expand_grad, branch, spread_sums)
-    )[:2]
-    output_dot = contract_first(cot_late, mix_late).astype(BF)
+    sums, far_sums = add_up(
+        jnp.concatenate([norm_sums.reshape(-1), merged_b, expand_b]).reshape(-1, 128), "col", cols
+    )
+    mix = lax.optimization_barrier((mix, grad_hat, expand_grad, branch, merged_dot))[0]
+    output_sent, output_taken = give(cot_other, mix)
+    output_dot = keep(cot_own, mix, output_taken)
     output_grad = scatter_weight(after(output_dot, merged_grad)).T
-    halves = lax.optimization_barrier(halves + (output_dot,))[:2]
+    halves = lax.optimization_barrier(halves + (output_sent,))[:2]
     grad_hat = ring_close(grad_hat, halves)
-    sums = jnp.sum(spread_sums.reshape(cols, -1), axis=0)
-    merged_b = sums[4 * width : 4 * width + merged_cols]
-    expand_b = sums[4 * width + merged_cols :]
-    tail = jnp.concatenate([sums[: 4 * width], shift_b]).reshape(-1, 128)
-    if rows & (rows - 1) == 0:
-        step = 1
-        while step < rows:
-            far_tail = lax.ppermute(tail, "row", [(r, r ^ step) for r in range(rows)])
-            tail = tail + far_tail
-            step *= 2
-    else:
-        far_tail = broadcast(tail, "row", rows)
-        tail = jnp.sum(far_tail, axis=0)
+    own_sums = lax.dynamic_index_in_dim(
+        sums[: 4 * cols * width // 128].reshape(4, cols, -1, 128), lax.axis_index("col"), 1, keepdims=False
+    )
+    biases = sums[4 * cols * width // 128 :].reshape(-1)
+    merged_b, expand_b = biases[:merged_cols], biases[merged_cols:]
+    tail, far_tail = add_up(
+        jnp.concatenate([own_sums.reshape(-1, 128), shift_b.reshape(-1, 128)]), "row", rows
+    )
     tail = tail.reshape(5, width)
     branch = from_rows(branch.astype(BF))
     result = inputs.astype(F32) + branch.astype(F32) + output_bias + reduce_bias

time: 797 us -> 976 us (1.22)
  other arithmetic: 88.4 us -> 205 us
  waiting for transfers between devices: 206 us -> 238 us
  local copies, waits for them, and re-layouts: 62.5 us -> 77.4 us
  matrix products: 225 us -> 239 us
    concatenate x0 -> x5, other arithmetic: none -> 123 us  [the longest x2 115 us: body(): jnp.concatenate(part, axis=0)]
    reduce_scatter x4, waiting for transfers between devices: 3.94 us -> 60.5 us  [scatter_weight(): lax.psum_scatter(grad, 'col', scatter_dimension=0, tiled=True, axis_index...]
    all_to_all x3, waiting for transfers between devices: 50.9 us -> 0.01 us  [col_swap(): return lax.all_to_all(b, 'col', split_axis=0, concat_axis=0, tiled=True)]
    ppermute x2 -> x9, waiting for transfers between devices: 11.4 us -> 48.9 us  [the longest x5 48.9 us: add_up(): taken = lax.ppermute(value, axis, [(r, r ^ step) for r in range(size)])]
    ppermute x8, waiting for transfers between devices: 72.6 us -> 44.4 us  [body(): up = lambda v: lax.ppermute(v, 'row', ahead)]
    ppermute x8, waiting for transfers between devices: 35.7 us -> 56.1 us  [body(): down = lambda v: lax.ppermute(v, 'row', behind)]
    unnamed x74 -> x101, local copies, waits for them, and re-layouts: 20.8 us -> 31.4 us
    dot_general x4 -> x8, matrix products: 70.6 us -> 80 us  [contract_first(): lax.dot_general(left, right, (((0,), (0,)), ((), ())), preferred_element_...]
  transfers between devices with their start and end apart: 33 -> 39, of which waited for: 16 -> 17; matrix products, arithmetic and copies ran while one was open for 45% -> 52% of each run, Pallas kernels for 3% -> 2%
where the time goes in v4:
time: 976 us; the launch traced here: 969 us
  matrix products  239 us (24%)
  waiting for transfers between devices  238 us (24%)
  other arithmetic  205 us (21%)
  blocking collectives  125 us (13%)
  local copies, waits for them, and re-layouts  77.4 us (8%)
  starting transfers between devices  49 us (5%)
  Pallas kernels  21.1 us (2%)
  between operations  15.3 us (2%)
    concatenate x2, other arithmetic, body(): jnp.concatenate(part, axis=0)  115 us
    dot_general x4, matrix products, contract_last(): lax.dot_general(left, right, (((1,), (1,)), ((), ())), preferred_element_...  85.1 us
    dot_general x8, matrix products, contract_first(): lax.dot_general(left, right, (((0,), (0,)), ((), ())), preferred_element_...  80 us
    dot_general x4, matrix products, mm(): return jnp.dot(left, right, preferred_element_type=F32)  73.5 us
    reduce_scatter x4, waiting for transfers between devices, scatter_weight(): lax.psum_scatter(grad, 'col', scatter_dimension=0, tiled=True, axis_index...  60.5 us
    all_to_all x1, blocking collectives, col_swap(): return lax.all_to_all(b, 'col', split_axis=0, concat_axis=0, tiled=True)  57.5 us
    ppermute x8, waiting for transfers between devices, body(): down = lambda v: lax.ppermute(v, 'row', behind)  56.1 us
    all_to_all x2, blocking collectives, row_swap(): b = lax.all_to_all(b, 'row', split_axis=0, concat_axis=0, tiled=True)  55.9 us
  transfers between devices with their start and end apart: 39, of which 17 were waited for; matrix products, arithmetic and copies ran while one was open for 52% of the time, Pallas kernels for 2%

profile of v4, /device:TPU:0, one launch (start us, length us, event | category | flops | bytes accessed | tf_op | source)
XLA Modules:
  0.0 969.5 jit_solution(10322861322577964173)
XLA Ops:
  8.7 11.9 %all_to_all.40 = f32[8,4,256]{2,1,0:T(4,128)S(1)} all-to-all(f32[8,4,256]{2,1,0:T(4,128)S(1)} %broadcast_in_dim.17), channel_id=1, replica_groups=mesh['row'=4,'col'=8] {'col'}, dimensions={0} | all-to-all | bytes 65536 | tf_op jit(solution)/shard_map/all_to_all | solution.py:266
  22.6 29.0 %all_to_all.41 = bf16[4,2,2,256,256]{4,3,1,2,0:T(8,128)(2,1)S(1)} all-to-all(bf16[4,2,2,256,256]{4,3,1,2,0:T(8,128)(2,1)S(1)} %copy.89), channel_id=1, replica_groups=mesh['row'=4,'col'=8] {'row'}, dimensions={0} | all-to-all | bytes 4194304 | tf_op jit(solution)/shard_map/all_to_all | solution.py:194
  52.0 26.9 %all_to_all.42 = bf16[4,2,2,256,256]{4,3,1,2,0:T(8,128)(2,1)S(1)} all-to-all(bf16[4,2,2,256,256]{4,3,1,2,0:T(8,128)(2,1)S(1)} %copy.91), channel_id=1, replica_groups=mesh['row'=4,'col'=8] {'row'}, dimensions={0} | all-to-all | bytes 4194304 | tf_op jit(solution)/shard_map/all_to_all | solution.py:194
  80.3 57.5 %all_to_all.43 = bf16[8,512,256]{2,1,0:T(8,128)(2,1)} all-to-all(bf16[8,512,256]{2,1,0:T(8,128)(2,1)S(1)} %bitcast.143), channel_id=1, replica_groups=mesh['row'=4,'col'=8] {'col'}, dimensions={0} | all-to-all | bytes 4194304 | tf_op jit(solution)/shard_map/all_to_all | solution.py:198
  146.3 45.8 %collective-permute-done = bf16[512,2048]{1,0:T(8,128)(2,1)S(1)} collective-permute-done((bf16[512,2048]{1,0:T(8,128)(2,1)S(1)}, bf16[512,2048]{1,0:T(8,128)(2,1)S(1)}, u32[]{:S(2)}, u32[]{:S(2)}) %collective-permute-start) | collective-permute-done | bytes 2097184 | tf_op jit(solution)/shard_map/ppermute | solution.py:190
  211.7 12.6 %collective-permute-done.2 = bf16[256,2048]{1,0:T(8,128)(2,1)S(1)} collective-permute-done((bf16[256,2048]{1,0:T(8,128)(2,1)}, bf16[256,2048]{1,0:T(8,128)(2,1)S(1)}, u32[]{:S(2)}, u32[]{:S(2)}) %collective-permute-start.2) | collective-permute-done | bytes 1048608 | tf_op jit(solution)/shard_map/ppermute | solution.py:189
  265.4 21.7 %convolution_add_fusion.1 = f32[2048,2048]{1,0:T(8,128)S(1)} fusion(bf16[2048,2048]{1,0:T(8,128)(2,1)} %copy-done.2, bf16[2048,2048]{1,0:T(8,128)(2,1)} %all-gather.4.cloned.1.call-done, f32[2048]{0:T(1024)S(1)} %copy-done.36), kind=kOutput, calls=%fused_computation.29 | convolution fusion | flops 17184063488 | bytes 33562624 | tf_op jit(solution)/shard_map/dot_general | solution.py:24
  295.6 12.4 %collective-permute-done.5 = bf16[512,2048]{0,1:T(8,128)(2,1)} collective-permute-done((bf16[512,2048]{0,1:T(8,128)(2,1)S(1)}, bf16[512,2048]{0,1:T(8,128)(2,1)}, u32[]{:S(2)}, u32[]{:S(2)}) %collective-permute-start.5) | collective-permute-done | bytes 2097184 | tf_op jit(solution)/shard_map/ppermute | solution.py:189
  321.6 10.9 %collective-permute-done.6 = bf16[256,2048]{0,1:T(8,128)(2,1)S(1)} collective-permute-done((bf16[256,2048]{0,1:T(8,128)(2,1)S(1)}, bf16[256,2048]{0,1:T(8,128)(2,1)S(1)}, u32[]{:S(2)}, u32[]{:S(2)}) %collective-permute-start.6) | collective-permute-done | bytes 1048608 | tf_op jit(solution)/shard_map/ppermute | solution.py:189
  337.8 57.1 %maximum_maximum_fusion = bf16[2048,1024]{0,1:T(8,128)(2,1)S(1)} fusion(bf16[512,256]{0,1:T(8,128)(2,1)S(1)} %get-tuple-element.251, bf16[512,256]{0,1:T(8,128)(2,1)S(1)} %get-tuple-element.250, bf16[512,256]{0,1:T(8,128)(2,1)S(1)} %get-tuple-element.249, bf16[512,256]{0,1:T(8,128)(2,1)S(1)} %get-tuple-element.248, ...), kind=kLoop, calls=%fused_computation.43 | loop fusion | flops 67108864 | bytes 8388608 | tf_op jit(solution)/shard_map/concatenate | solution.py:324
  405.3 58.0 %maximum_maximum_fusion.1 = bf16[2048,1024]{0,1:T(8,128)(2,1)} fusion(bf16[512,256]{0,1:T(8,128)(2,1)S(1)} %get-tuple-element.254, bf16[512,256]{0,1:T(8,128)(2,1)S(1)} %get-tuple-element.253, bf16[512,256]{0,1:T(8,128)(2,1)S(1)} %get-tuple-element.252, bf16[512,256]{0,1:T(8,128)(2,1)S(1)} %get-tuple-element.247, ...), kind=kLoop, calls=%fused_computation.48 | loop fusion | flops 67108864 | bytes 8388608 | tf_op jit(solution)/shard_map/concatenate | solution.py:324
  466.5 24.0 %convolution_convert_fusion = bf16[2048,2048]{0,1:T(8,128)(2,1)} fusion(bf16[2048,2048]{1,0:T(8,128)(2,1)} %copy-done.10, bf16[2048,2048]{1,0:T(8,128)(2,1)} %all-gather.6.cloned.1.call-done), kind=kOutput, calls=%fused_computation.32 | convolution fusion | flops 17184063488 | bytes 25165824 | tf_op jit(solution)/shard_map/dot_general | solution.py:24
  490.5 13.2 %add_convert_fusion.3 = bf16[1024,2048]{1,0:T(8,128)(2,1)} fusion(bf16[1024,2048]{1,0:T(8,128)(2,1)} %collective-permute-done.8, bf16[2048,1024]{0,1:T(8,128)(2,1)S(1)} %copy-done.13, bf16[2048,2048]{1,0:T(8,128)(2,1)} %copy-done.10), kind=kOutput, calls=%fused_computation.31 | convolution fusion | flops 8596226048 | bytes 20971520 | tf_op jit(solution)/shard_map/dot_general | solution.py:32
  503.8 25.3 %convert_reduce_fusion.1 = (f32[2048]{0:T(1024)}, bf16[2048,2048]{1,0:T(8,128)(2,1)S(1)}) fusion(bf16[2048,2048]{1,0:T(8,128)(2,1)} %get-tuple-element.69, bf16[2048,2048]{0,1:T(8,128)(2,1)} %constant_dynamic-update-slice_fusion.7, bf16[2048,2048]{1,0:T(8,128)(2,1)} %all-gather.6.cloned.1.call-done), kind=kOutput, calls=%fused_computation.21 | convolution fusion | flops 17200838656 | bytes 33562624 | tf_op jit(solution)/shard_map/dot_general | solution.py:28
  529.1 10.8 %convolution_convert_fusion.2 = bf16[1024,2048]{1,0:T(8,128)(2,1)} fusion(bf16[2048,1024]{1,0:T(8,128)(2,1)S(1)} %copy-done.17, bf16[2048,2048]{1,0:T(8,128)(2,1)S(1)} %get-tuple-element.84), kind=kOutput, calls=%fused_computation.59 | convolution fusion | flops 8592031744 | bytes 16777216 | tf_op jit(solution)/shard_map/dot_general | solution.py:32
  550.7 17.7 %convolution_add_fusion = f32[2048,1536]{1,0:T(8,128)} fusion(bf16[2048,2048]{1,0:T(8,128)(2,1)} %copy-done.1, f32[1536]{0:T(1024)S(1)} %copy-done.37, bf16[2048,2048]{1,0:T(8,128)(2,1)S(1)} %copy-done.35), kind=kOutput, calls=%fused_computation.28 | convolution fusion | flops 12888047616 | bytes 27271168 | tf_op jit(solution)/shard_map/dot_general | solution.py:24
  568.4 21.1 %attention.1 = (bf16[4,2,256,512]{3,2,1,0:T(8,128)(2,1)}, bf16[4,2,256,1536]{3,2,1,0:T(8,128)(2,1)}) custom-call(s32[4]{0:T(128)} %and_select_fusion.slot_ref, s32[4]{0:T(128)} %reshape.172.starts_ref, f32[4,2,256,1536]{3,2,1,0:T(8,128)} %bitcast.179, bf16[4,2,256,512]{3,2,1,0:T(8,128)(2,1)} %bitcast.183, f32[1024,128]{1,0:T(8,128)} %get-tuple-element.73.cos_ref, ...), custom_call_target="tpu_custom_call" | custom-call | flops 16106127360 | bytes 23068672 | tf_op jit(solution)/shard_map/attention/pallas_call | solution.py:124
  608.6 13.8 %add_convert_fusion.2 = bf16[1024,2048]{1,0:T(8,128)(2,1)} fusion(bf16[1024,2048]{1,0:T(8,128)(2,1)} %collective-permute-done.18, bf16[2048,1024]{1,0:T(8,128)(2,1)S(1)} %copy-done.16, bf16[2048,2048]{1,0:T(8,128)(2,1)} %copy-done.39), kind=kOutput, calls=%fused_computation.30 | convolution fusion | flops 8596226048 | bytes 20971520 | tf_op jit(solution)/shard_map/dot_general | solution.py:32
  640.7 25.2 %fusion.36 = f32[2048,2048]{1,0:T(8,128)} fusion(bf16[2048,2048]{1,0:T(8,128)(2,1)} %copy-done.39, bf16[2048,2048]{1,0:T(8,128)(2,1)} %all-gather.4.cloned.1.call-done), kind=kOutput, calls=%fused_computation.182 | convolution fusion | flops 17179869184 | bytes 33554432 | tf_op jit(solution)/shard_map/dot_general | solution.py:28
  674.6 25.4 %fusion.10 = (f32[2048]{0:T(1024)S(1)}, f32[2048]{0:T(1024)S(1)}, f32[2048]{0:T(1024)S(1)}, f32[2048]{0:T(1024)S(1)}, bf16[2048,2048]{1,0:T(8,128)(2,1)}) fusion(bf16[2048,2048]{1,0:T(8,128)(2,1)} %copy-done, f32[2048]{0:T(1024)S(1)} %copy-done.26, f32[2048]{0:T(1024)S(1)} %copy-done.24, f32[2048,2048]{1,0:T(8,128)} %fusion.36, f32[2048]{0:T(1024)S(1)} %bitcast.166, ...), kind=kOutput, calls=%fused_computation.13 | convolution fusion | flops 12939419648 | bytes 46202880 | tf_op jit(solution)/shard_map/dot_general | solution.py:28
  741.8 33.0 %reduce-scatter.9.cloned.1.call-done = bf16[256,1536]{1,0:T(8,128)(2,1)} async-done(((bf16[1024,1536]{1,0:T(8,128)(2,1)}), bf16[256,1536]{1,0:T(8,128)(2,1)}) %reduce-scatter.9.cloned.1.call-update) | async-done | bytes 786448 | tf_op jit(solution)/shard_map/reduce_scatter | solution.py:339
  795.1 27.5 %reduce-scatter.11.cloned.1.call-done = bf16[256,512]{1,0:T(8,128)(2,1)} async-done(((bf16[1024,512]{1,0:T(8,128)(2,1)}), bf16[256,512]{1,0:T(8,128)(2,1)}) %reduce-scatter.11.cloned.1.call-update) | async-done | bytes 262160 | tf_op jit(solution)/shard_map/reduce_scatter | solution.py:339
  838.2 28.6 %collective-permute-done.24 = f32[92,128]{1,0:T(8,128)S(1)} collective-permute-done((f32[92,128]{1,0:T(8,128)S(1)}, f32[92,128]{1,0:T(8,128)S(1)}, u32[]{:S(2)}, u32[]{:S(2)}) %collective-permute-start.24) | collective-permute-done | bytes 47136 | tf_op jit(solution)/shard_map/ppermute | solution.py:277
  939.6 17.5 %all-to-all-done.7 = bf16[4,2,2,256,256]{4,3,1,2,0:T(8,128)(2,1)} async-done(((bf16[4,2,2,256,256]{4,3,1,2,0:T(8,128)(2,1)}), bf16[4,2,2,256,256]{4,3,1,2,0:T(8,128)(2,1)}, u32[]{:S(2)}, u32[]{:S(2)}) %all-to-all-start.7) | async-done | bytes 2097184 | tf_op jit(solution)/shard_map/all_to_all | solution.py:207
  (277 shorter events, 327.4 us)
Async XLA Ops:
  7.2 258.2 %all-gather.4.cloned.1.call-start = ((), (), s32[]{:S(2)}) async-start(), calls=%async_computation.12 | async-start | bytes 9437184 | tf_op jit(solution)/shard_map/all_gather | solution.py:284
  137.8 55.7 %all-to-all-start.4 = ((bf16[8,512,256]{2,1,0:T(8,128)(2,1)}), bf16[8,512,256]{2,1,0:T(8,128)(2,1)}, u32[]{:S(2)}, u32[]{:S(2)}) async-start(bf16[8,512,256]{2,1,0:T(8,128)(2,1)} %bitcast.10), calls=%async_computation.4 | async-start | bytes 4194304 | tf_op jit(solution)/shard_map/all_to_all | solution.py:198
  142.3 324.1 %all-gather.6.cloned.1.call-start = ((), (), s32[]{:S(2)}) async-start(), calls=%async_computation.13 | async-start | bytes 9437184 | tf_op jit(solution)/shard_map/all_gather | solution.py:293
  144.2 47.9 %collective-permute-start = (bf16[512,2048]{1,0:T(8,128)(2,1)S(1)}, bf16[512,2048]{1,0:T(8,128)(2,1)S(1)}, u32[]{:S(2)}, u32[]{:S(2)}) collective-permute-start(bf16[512,2048]{1,0:T(8,128)(2,1)S(1)} %bitcast.131), channel_id=1, source_target_pairs={{8,0},{24,8},{16,24},{0,16},{9,1},{25,9},{17,25},{1,17},{10,2},{26... | collective-permute-start | bytes 6291464 | tf_op jit(solution)/shard_map/ppermute | solution.py:190
  145.8 47.7 %collective-permute-start.1 = (bf16[512,2048]{1,0:T(8,128)(2,1)S(1)}, bf16[512,2048]{1,0:T(8,128)(2,1)}, u32[]{:S(2)}, u32[]{:S(2)}) collective-permute-start(bf16[512,2048]{1,0:T(8,128)(2,1)S(1)} %bitcast.132), channel_id=1, source_target_pairs={{0,8},{8,24},{24,16},{16,0},{1,9},{9,25},{25,17},{17,1},{2,10},{10... | collective-permute-start | bytes 6291464 | tf_op jit(solution)/shard_map/ppermute | solution.py:189
  193.5 347.1 %all-gather.8.cloned.1.call-start = ((), (), s32[]{:S(2)}) async-start(), calls=%async_computation.14 | async-start | bytes 9437184 | tf_op jit(solution)/shard_map/all_gather | solution.py:296
  261.9 46.2 %collective-permute-start.5 = (bf16[512,2048]{0,1:T(8,128)(2,1)S(1)}, bf16[512,2048]{0,1:T(8,128)(2,1)}, u32[]{:S(2)}, u32[]{:S(2)}) collective-permute-start(bf16[512,2048]{0,1:T(8,128)(2,1)S(1)} %bitcast.138), channel_id=1, source_target_pairs={{0,8},{8,24},{24,16},{16,0},{1,9},{9,25},{25,17},{17,1},{2,10},{10... | collective-permute-start | bytes 6291464 | tf_op jit(solution)/shard_map/ppermute | solution.py:189
  263.1 45.7 %collective-permute-start.4 = (bf16[512,2048]{0,1:T(8,128)(2,1)S(1)}, bf16[512,2048]{0,1:T(8,128)(2,1)}, u32[]{:S(2)}, u32[]{:S(2)}) collective-permute-start(bf16[512,2048]{0,1:T(8,128)(2,1)S(1)} %bitcast.139), channel_id=1, source_target_pairs={{8,0},{24,8},{16,24},{0,16},{9,1},{25,9},{17,25},{1,17},{10,2},{26... | collective-permute-start | bytes 6291464 | tf_op jit(solution)/shard_map/ppermute | solution.py:190
  264.9 324.6 %reduce-scatter.5.cloned.1.call-start = ((), (), s32[]{:S(2)}) async-start(), calls=%async_computation.15 | async-start | bytes 5242880 | tf_op jit(solution)/shard_map/reduce_scatter | solution.py:339
  405.3 85.1 %collective-permute-start.8 = (bf16[1024,2048]{1,0:T(8,128)(2,1)}, bf16[1024,2048]{1,0:T(8,128)(2,1)}, u32[]{:S(2)}, u32[]{:S(2)}) collective-permute-start(bf16[1024,2048]{1,0:T(8,128)(2,1)} %convolution_convert_fusion.3), channel_id=1, source_target_pairs={{0,1},{1,0},{2,3},{3,2},{4,5},{5,4},{6,7},{7,6},{8,9},{9,8},{10,11... | collective-permute-start | bytes 12582920 | tf_op jit(solution)/shard_map/ppermute | solution.py:333
  503.7 207.8 %reduce-scatter.7.cloned.1.call-start = ((), (), s32[]{:S(2)}) async-start(), calls=%async_computation.16 | async-start | bytes 5242880 | tf_op jit(solution)/shard_map/reduce_scatter | solution.py:339
  539.9 68.7 %collective-permute-start.18 = (bf16[1024,2048]{1,0:T(8,128)(2,1)}, bf16[1024,2048]{1,0:T(8,128)(2,1)}, u32[]{:S(2)}, u32[]{:S(2)}) collective-permute-start(bf16[1024,2048]{1,0:T(8,128)(2,1)} %convolution_convert_fusion.2), channel_id=1, source_target_pairs={{0,1},{1,0},{2,3},{3,2},{4,5},{5,4},{6,7},{7,6},{8,9},{9,8},{10,11... | collective-permute-start | bytes 12582920 | tf_op jit(solution)/shard_map/ppermute | solution.py:333
  622.5 152.3 %reduce-scatter.9.cloned.1.call-start = ((), (), s32[]{:S(2)}) async-start(), calls=%async_computation.17 | async-start | bytes 3932160 | tf_op jit(solution)/shard_map/reduce_scatter | solution.py:339
  633.2 32.8 %collective-permute-start.19 = (bf16[1024,1536]{1,0:T(8,128)(2,1)S(1)}, bf16[1024,1536]{1,0:T(8,128)(2,1)S(1)}, u32[]{:S(2)}, u32[]{:S(2)}) collective-permute-start(bf16[1024,1536]{1,0:T(8,128)(2,1)S(1)} %convolution_convert_fusion.1), channel_id=1, source_target_pairs={{0,1},{1,0},{2,3},{3,2},{4,5},{5,4},{6,7},{7,6},{8,9},{9,8},{10,11... | collective-permute-start | bytes 9437192 | tf_op jit(solution)/shard_map/ppermute | solution.py:333
  637.2 68.7 %collective-permute-start.12 = (bf16[512,2048]{0,1:T(8,128)(2,1)}, bf16[512,2048]{0,1:T(8,128)(2,1)}, u32[]{:S(2)}, u32[]{:S(2)}) collective-permute-start(bf16[512,2048]{0,1:T(8,128)(2,1)} %pad_maximum_fusion.5), channel_id=1, source_target_pairs={{8,0},{24,8},{16,24},{0,16},{9,1},{25,9},{17,25},{1,17},{10,2},{26... | collective-permute-start | bytes 6291464 | tf_op jit(solution)/shard_map/ppermute | solution.py:190
  639.1 66.8 %collective-permute-start.11 = (bf16[512,2048]{0,1:T(8,128)(2,1)}, bf16[512,2048]{0,1:T(8,128)(2,1)}, u32[]{:S(2)}, u32[]{:S(2)}) collective-permute-start(bf16[512,2048]{0,1:T(8,128)(2,1)} %pad_maximum_fusion.4), channel_id=1, source_target_pairs={{0,8},{8,24},{24,16},{16,0},{1,9},{9,25},{25,17},{17,1},{2,10},{10... | collective-permute-start | bytes 6291464 | tf_op jit(solution)/shard_map/ppermute | solution.py:189
  720.6 56.7 %collective-permute-start.22 = (bf16[1024,512]{1,0:T(8,128)(2,1)}, bf16[1024,512]{1,0:T(8,128)(2,1)}, u32[]{:S(2)}, u32[]{:S(2)}) collective-permute-start(bf16[1024,512]{1,0:T(8,128)(2,1)} %convolution_convert_fusion.5), channel_id=1, source_target_pairs={{0,1},{1,0},{2,3},{3,2},{4,5},{5,4},{6,7},{7,6},{8,9},{9,8},{10,11... | collective-permute-start | bytes 3145736 | tf_op jit(solution)/shard_map/ppermute | solution.py:333
  733.5 52.6 %collective-permute-start.21 = (bf16[512,2048]{1,0:T(8,128)(2,1)}, bf16[512,2048]{1,0:T(8,128)(2,1)}, u32[]{:S(2)}, u32[]{:S(2)}) collective-permute-start(bf16[512,2048]{1,0:T(8,128)(2,1)} %pad_maximum_fusion.7), channel_id=1, source_target_pairs={{8,0},{24,8},{16,24},{0,16},{9,1},{25,9},{17,25},{1,17},{10,2},{26... | collective-permute-start | bytes 6291464 | tf_op jit(solution)/shard_map/ppermute | solution.py:190
  736.7 49.4 %collective-permute-start.20 = (bf16[512,2048]{1,0:T(8,128)(2,1)}, bf16[512,2048]{1,0:T(8,128)(2,1)}, u32[]{:S(2)}, u32[]{:S(2)}) collective-permute-start(bf16[512,2048]{1,0:T(8,128)(2,1)} %pad_maximum_fusion.6), channel_id=1, source_target_pairs={{0,8},{8,24},{24,16},{16,0},{1,9},{9,25},{25,17},{17,1},{2,10},{10... | collective-permute-start | bytes 6291464 | tf_op jit(solution)/shard_map/ppermute | solution.py:189
  737.0 89.6 %all-to-all-start.5 = ((bf16[8,512,256]{1,2,0:T(8,128)(2,1)}), bf16[8,512,256]{1,2,0:T(8,128)(2,1)}, u32[]{:S(2)}, u32[]{:S(2)}) async-start(bf16[8,512,256]{1,2,0:T(8,128)(2,1)} %bitcast.144), calls=%async_computation.6 | async-start | bytes 4194304 | tf_op jit(solution)/shard_map/all_to_all | solution.py:198
  741.4 81.2 %reduce-scatter.11.cloned.1.call-start = ((), (), s32[]{:S(2)}) async-start(), calls=%async_computation.18 | async-start | bytes 1310720 | tf_op jit(solution)/shard_map/reduce_scatter | solution.py:339
  826.6 99.8 %all-to-all-start.6 = ((bf16[8,512,256]{2,1,0:T(8,128)(2,1)}), bf16[8,512,256]{2,1,0:T(8,128)(2,1)}, u32[]{:S(2)}, u32[]{:S(2)}) async-start(bf16[8,512,256]{2,1,0:T(8,128)(2,1)} %bitcast.130), calls=%async_computation.10 | async-start | bytes 4194304 | tf_op jit(solution)/shard_map/all_to_all | solution.py:198
  836.2 30.6 %collective-permute-start.24 = (f32[92,128]{1,0:T(8,128)S(1)}, f32[92,128]{1,0:T(8,128)S(1)}, u32[]{:S(2)}, u32[]{:S(2)}) collective-permute-start(f32[92,128]{1,0:T(8,128)S(1)} %fusion.32), channel_id=1, source_target_pairs={{0,2},{1,3},{2,0},{3,1},{4,6},{5,7},{6,4},{7,5},{8,10},{9,11},{10,... | collective-permute-start | bytes 141320 | tf_op jit(solution)/shard_map/ppermute | solution.py:277
  929.5 27.6 %all-to-all-start.7 = ((bf16[4,2,2,256,256]{4,3,1,2,0:T(8,128)(2,1)}), bf16[4,2,2,256,256]{4,3,1,2,0:T(8,128)(2,1)}, u32[]{:S(2)}, u32[]{:S(2)}) async-start(bf16[4,2,2,256,256]{4,3,1,2,0:T(8,128)(2,1)} %copy.102), calls=%async_computation.11 | async-start | bytes 4194304 | tf_op jit(solution)/shard_map/all_to_all | solution.py:207
  (57 other events, 1014.3 us)
Sparse Core Ops, SparseCore 0:
  9.6 91.3 all-gather.3
  193.6 83.5 all-gather.5
  279.4 80.2 all-gather.7
  503.8 75.7 reduce-scatter.4
  622.6 75.1 reduce-scatter.6
  700.5 74.2 reduce-scatter.8
  783.8 38.7 reduce-scatter.10

commit v5 on v4

--- a/solution.py
+++ b/solution.py
@@ -201,8 +201,7 @@
         return b.transpose(1, 0, 2).reshape(block_rows, cols * width)
 
     def from_rows(block, *earlier):
-        b = block.reshape(block_rows, cols, width).transpose(1, 0, 2)
-        b = col_swap(b).reshape(rows, per_row, micro, part, width)
+        b = block.reshape(rows, per_row, micro, part, width)
         if earlier:
             b = lax.all_to_all(after(b, *earlier), "row", split_axis=0, concat_axis=0, tiled=True)
             return b.transpose(2, 1, 0, 3, 4).reshape(micro, own_tokens, width)
@@ -253,7 +252,7 @@
             else:
                 a, b = a + fore.astype(F32), b + back.astype(F32)
             fore, back = up(a.astype(BF)), down(b.astype(BF))
-        return chunk(total, 0).astype(F32) + fore.astype(F32) + back.astype(F32)
+        return chunk(total, 0), fore, back
 
     def norm(block):
         block = block.astype(F32)
@@ -318,11 +317,9 @@
         other = [jnp.where(core == 0, b, a) for a, b in zip(even, odd)]
         return jnp.concatenate(own, axis=1), jnp.concatenate(other, axis=1)
 
-    cot_pieces = ring_gather(cot_part, activated)
-    cot_seq = jnp.concatenate(cot_pieces, axis=0)
-    cot_own, cot_other = (
-        jnp.concatenate(part, axis=0) for part in zip(*[own_and_other(p) for p in cot_pieces])
-    )
+    branch_ff = mm(activated, reduce_w).astype(BF)
+    cot_seq = jnp.concatenate(ring_gather(cot_part, branch_ff), axis=0)
+    cot_own, cot_other = own_and_other(cot_seq)
     ready = (attend_in,) + own_and_other(expand_in) + own_and_other(attend_in) + rotary_tables()
     cot_other, attend_in, expand_own, expand_other, attend_own, attend_other, *tables = (
         lax.optimization_barrier((cot_other,) + ready)
@@ -342,23 +339,22 @@
         return grad.astype(F32)
 
     reduce_sent, reduce_taken = give(cot_other, activated)
-    branch_ff = mm(after(activated, reduce_sent), reduce_w).astype(BF)
-    reduce_dot = keep(after(cot_own, branch_ff), activated, reduce_taken)
+    reduce_dot = keep(after(cot_own, reduce_sent), activated, reduce_taken)
     reduce_grad = scatter_weight(reduce_dot).T
-    grad_act = contract_last(after(cot_seq, reduce_dot), reduce_w)
+    grad_act = contract_last(after(cot_seq, reduce_dot, mixed_w), reduce_w)
     grad_pre = (grad_act * slope.astype(F32)).astype(BF)
     expand_b = jnp.sum(grad_pre.astype(F32), axis=0)
     expand_sent, expand_taken = give(expand_other, grad_pre)
     grad_mix = mm(after(cot_seq, expand_sent), output_wt).astype(BF)
-    merged_pre = mm(after(attend_in, grad_mix), merged_w) + merged_bias
+    expand_dot = keep(after(expand_own, grad_mix), grad_pre, expand_taken)
+    expand_grad = scatter_weight(expand_dot)
+    merged_pre = mm(after(attend_in, expand_dot), merged_w) + merged_bias
+    grad_mix = after(grad_mix, reduce_grad)
     mix, grad_merged = attention(
         slots, piece_starts.reshape(-1), merged_pre, grad_mix, tables, micro, rows
     )
-    mix = after(mix, reduce_grad)
     branch = (contract_last(mix, output_wt) + branch_ff).astype(BF)
     halves = ring_open(branch)
-    expand_dot = keep(after(expand_own, branch), grad_pre, expand_taken)
-    expand_grad = scatter_weight(expand_dot)
     grad_merged, attend_other = lax.optimization_barrier(
         (grad_merged, attend_other, branch)
     )[:2]
@@ -366,42 +362,73 @@
     grad_merged, grad_pre, half_up, half_down = lax.optimization_barrier(
         (grad_merged, grad_pre) + halves + (merged_sent,)
     )[:4]
+    branch_parts = ring_close(branch, (half_up, half_down))
     merged_dot = keep(attend_own, grad_merged, merged_taken)
     merged_grad = scatter_weight(merged_dot)
-    branch = ring_close(branch, (half_up, half_down))
-    grad_first = contract_last(grad_merged, merged_w)
-    grad_second = contract_last(grad_pre, expand_w)
-    norm_sums = jnp.stack(
-        [
-            jnp.sum(grad_first * normed, axis=0),
-            jnp.sum(grad_first, axis=0),
-            jnp.sum(grad_second * normed, axis=0),
-            jnp.sum(grad_second, axis=0),
-        ]
-    )
-    grad_hat = (grad_first * gains[0] + grad_second * gains[2]).astype(BF)
-    halves = ring_open(grad_hat)
+    grad_merged, grad_pre = lax.optimization_barrier(
+        (grad_merged, grad_pre, merged_dot, expand_grad)
+    )[:2]
+
+    def grads(j, *earlier):
+        first = contract_last(after(chunk(grad_merged, j), *earlier), merged_w)
+        second = contract_last(after(chunk(grad_pre, j), *earlier), expand_w)
+        normal = chunk(normed, j)
+        sums = (
+            jnp.sum(first * normal, axis=0),
+            jnp.sum(first, axis=0),
+            jnp.sum(second * normal, axis=0),
+            jnp.sum(second, axis=0),
+        )
+        hat = (first * gains[0] + second * gains[2]).astype(BF)
+        return lax.optimization_barrier((hat, sums))
+
+    hat, sums = grads(far)
+    chunk_sums = [sums]
+    wide = lambda v: v.astype(F32)
+    branch_parts = lax.optimization_barrier(branch_parts + (hat,))[:3]
+    branch = wide(branch_parts[0]) + wide(branch_parts[1]) + wide(branch_parts[2])
+    grad_up, grad_down = up(hat[:cut]), down(hat[cut:])
+    for step in range(far - 1, 0, -1):
+        a, sums_a = grads(step, hat)
+        hat, sums_b = grads(rows - step, a)
+        b = hat
+        chunk_sums += [sums_a, sums_b]
+        if step == far - 1:
+            a = jnp.concatenate([wide(a[:cut]) + wide(grad_up), wide(a[cut:])], axis=0)
+            b = jnp.concatenate([wide(b[:cut]), wide(b[cut:]) + wide(grad_down)], axis=0)
+        else:
+            a, b = wide(a) + wide(grad_up), wide(b) + wide(grad_down)
+        grad_up, grad_down = up(a.astype(BF)), down(b.astype(BF))
+    hat, sums = grads(0, hat)
+    chunk_sums.append(sums)
+    norm_sums = jnp.stack([sum(parts) for parts in zip(*chunk_sums)])
     merged_b = jnp.sum(grad_merged.astype(F32), axis=0)
     shift_b = jnp.sum(cotangent.astype(F32), axis=(0, 1))
-    sums, far_sums = add_up(
-        jnp.concatenate([norm_sums.reshape(-1), merged_b, expand_b]).reshape(-1, 128), "col", cols
-    )
-    mix = lax.optimization_barrier((mix, grad_hat, expand_grad, branch, merged_dot))[0]
+    sums = jnp.concatenate(
+        [
+            norm_sums.reshape(4, cols, width).transpose(1, 0, 2).reshape(cols, 4 * width),
+            jnp.broadcast_to(merged_b, (cols, merged_cols)),
+            jnp.broadcast_to(expand_b, (cols, expand_b.shape[0])),
+        ],
+        axis=1,
+    ).reshape(cols, -1, 128)
+    branch = col_swap(branch.astype(BF).reshape(block_rows, cols, width).transpose(1, 0, 2))
+    spread_sums = lax.all_to_all(
+        after(sums, branch), "col", split_axis=0, concat_axis=0, tiled=True
+    )
+    mix = lax.optimization_barrier((mix, hat))[0]
     output_sent, output_taken = give(cot_other, mix)
     output_dot = keep(cot_own, mix, output_taken)
     output_grad = scatter_weight(after(output_dot, merged_grad)).T
-    halves = lax.optimization_barrier(halves + (output_sent,))[:2]
-    grad_hat = ring_close(grad_hat, halves)
-    own_sums = lax.dynamic_index_in_dim(
-        sums[: 4 * cols * width // 128].reshape(4, cols, -1, 128), lax.axis_index("col"), 1, keepdims=False
-    )
-    biases = sums[4 * cols * width // 128 :].reshape(-1)
-    merged_b, expand_b = biases[:merged_cols], biases[merged_cols:]
+    grad_hat = wide(hat) + wide(grad_up) + wide(grad_down)
+    sums = jnp.sum(spread_sums.reshape(cols, -1), axis=0)
+    merged_b = sums[4 * width : 4 * width + merged_cols]
+    expand_b = sums[4 * width + merged_cols :]
     tail, far_tail = add_up(
-        jnp.concatenate([own_sums.reshape(-1, 128), shift_b.reshape(-1, 128)]), "row", rows
+        jnp.concatenate([sums[: 4 * width], shift_b]).reshape(-1, 128), "row", rows
     )
     tail = tail.reshape(5, width)
-    branch = from_rows(branch.astype(BF))
+    branch = from_rows(branch)
     result = inputs.astype(F32) + branch.astype(F32) + output_bias + reduce_bias
     result = result.astype(BF)
 
@@ -412,8 +439,10 @@
         - part_normed * jnp.mean(grad_hat * part_normed, axis=-1, keepdims=True)
     )
 
-    norm_part = after(norm_part.astype(BF), output_grad, merged_grad)
-    input_grad = cotangent.astype(F32) + from_rows(norm_part, result, far_tail).astype(F32)
+    norm_part = after(norm_part.astype(BF), merged_grad, spread_sums)
+    norm_part = col_swap(norm_part.reshape(block_rows, cols, width).transpose(1, 0, 2))
+    norm_part = from_rows(norm_part, result, far_tail, output_grad)
+    input_grad = cotangent.astype(F32) + norm_part.astype(F32)
     norm_sums, shift_b = tail[:4], tail[4]
     return (
         result,

time: 976 us -> 844 us (0.86)
  other arithmetic: 205 us -> 85.9 us
  waiting for transfers between devices: 238 us -> 212 us
  matrix products: 239 us -> 263 us
    concatenate x3 -> x2, other arithmetic: 115 us -> 3.04 us  [the longest x1 1.52 us: body(): jnp.concatenate([wide(b[:cut]), wide(b[cut:]) + wide(grad_down)], axis=0)]
    reduce_scatter x4, waiting for transfers between devices: 60.5 us -> 19.3 us  [scatter_weight(): lax.psum_scatter(grad, 'col', scatter_dimension=0, tiled=True, axis_index...]
    ppermute x8, waiting for transfers between devices: 44.4 us -> 83.8 us  [body(): up = lambda v: lax.ppermute(v, 'row', ahead)]
    dot_general x4 -> x10, matrix products: 85.1 us -> 115 us  [contract_last(): lax.dot_general(left, right, (((1,), (1,)), ((), ())), preferred_element_...]
    ppermute x5 -> x2, waiting for transfers between devices: 48.9 us -> 20.4 us  [add_up(): taken = lax.ppermute(value, axis, [(r, r ^ step) for r in range(size)])]
    unnamed x101 -> x110, local copies, waits for them, and re-layouts: 31.4 us -> 22.2 us
  transfers between devices with their start and end apart: 39 -> 37, of which waited for: 17 -> 14; matrix products, arithmetic and copies ran while one was open for 52% -> 47% of each run, Pallas kernels for 2% -> 2%
where the time goes in v5:
time: 844 us; the launch traced here: 839 us
  matrix products  263 us (31%)
  waiting for transfers between devices  212 us (25%)
  blocking collectives  125 us (15%)
  other arithmetic  85.9 us (10%)
  local copies, waits for them, and re-layouts  68 us (8%)
  starting transfers between devices  48.7 us (6%)
  Pallas kernels  20.9 us (2%)
  between operations  15.4 us (2%)
    dot_general x10, matrix products, contract_last(): lax.dot_general(left, right, (((1,), (1,)), ((), ())), preferred_element_...  115 us
    ppermute x8, waiting for transfers between devices, body(): up = lambda v: lax.ppermute(v, 'row', ahead)  83.8 us
    dot_general x4, matrix products, mm(): return jnp.dot(left, right, preferred_element_type=F32)  74.7 us
    dot_general x8, matrix products, contract_first(): lax.dot_general(left, right, (((0,), (0,)), ((), ())), preferred_element_...  73.6 us
    all_to_all x1, blocking collectives, col_swap(): return lax.all_to_all(b, 'col', split_axis=0, concat_axis=0, tiled=True)  57.5 us
    ppermute x8, waiting for transfers between devices, body(): down = lambda v: lax.ppermute(v, 'row', behind)  57 us
    all_to_all x2, blocking collectives, row_swap(): b = lax.all_to_all(b, 'row', split_axis=0, concat_axis=0, tiled=True)  55.9 us
    unnamed x110, local copies, waits for them, and re-layouts  22.2 us
  transfers between devices with their start and end apart: 37, of which 14 were waited for; matrix products, arithmetic and copies ran while one was open for 47% of the time, Pallas kernels for 2%

profile of v5, /device:TPU:0, one launch (start us, length us, event | category | flops | bytes accessed | tf_op | source)
XLA Modules:
  0.0 838.7 jit_solution(1118415502233020654)
XLA Ops:
  8.7 11.9 %all_to_all.45 = f32[8,4,256]{2,1,0:T(4,128)S(1)} all-to-all(f32[8,4,256]{2,1,0:T(4,128)S(1)} %broadcast_in_dim.21), channel_id=1, replica_groups=mesh['row'=4,'col'=8] {'col'}, dimensions={0} | all-to-all | bytes 65536 | tf_op jit(solution)/shard_map/all_to_all | solution.py:265
  22.6 29.0 %all_to_all.46 = bf16[4,2,2,256,256]{4,3,1,2,0:T(8,128)(2,1)S(1)} all-to-all(bf16[4,2,2,256,256]{4,3,1,2,0:T(8,128)(2,1)S(1)} %copy.71), channel_id=1, replica_groups=mesh['row'=4,'col'=8] {'row'}, dimensions={0} | all-to-all | bytes 4194304 | tf_op jit(solution)/shard_map/all_to_all | solution.py:194
  52.0 26.9 %all_to_all.47 = bf16[4,2,2,256,256]{4,3,1,2,0:T(8,128)(2,1)S(1)} all-to-all(bf16[4,2,2,256,256]{4,3,1,2,0:T(8,128)(2,1)S(1)} %copy.73), channel_id=1, replica_groups=mesh['row'=4,'col'=8] {'row'}, dimensions={0} | all-to-all | bytes 4194304 | tf_op jit(solution)/shard_map/all_to_all | solution.py:194
  80.3 57.5 %all_to_all.48 = bf16[8,512,256]{2,1,0:T(8,128)(2,1)} all-to-all(bf16[8,512,256]{2,1,0:T(8,128)(2,1)S(1)} %bitcast.165), channel_id=1, replica_groups=mesh['row'=4,'col'=8] {'col'}, dimensions={0} | all-to-all | bytes 4194304 | tf_op jit(solution)/shard_map/all_to_all | solution.py:198
  146.2 45.8 %collective-permute-done = bf16[512,2048]{1,0:T(8,128)(2,1)S(1)} collective-permute-done((bf16[512,2048]{1,0:T(8,128)(2,1)S(1)}, bf16[512,2048]{1,0:T(8,128)(2,1)S(1)}, u32[]{:S(2)}, u32[]{:S(2)}) %collective-permute-start) | collective-permute-done | bytes 2097184 | tf_op jit(solution)/shard_map/ppermute | solution.py:190
  209.4 13.3 %collective-permute-done.2 = bf16[256,2048]{1,0:T(8,128)(2,1)S(1)} collective-permute-done((bf16[256,2048]{1,0:T(8,128)(2,1)}, bf16[256,2048]{1,0:T(8,128)(2,1)S(1)}, u32[]{:S(2)}, u32[]{:S(2)}) %collective-permute-start.2) | collective-permute-done | bytes 1048608 | tf_op jit(solution)/shard_map/ppermute | solution.py:189
  262.1 21.5 %convolution_add_fusion.1 = f32[2048,2048]{1,0:T(8,128)S(1)} fusion(bf16[2048,2048]{1,0:T(8,128)(2,1)} %copy-done.1, bf16[2048,2048]{1,0:T(8,128)(2,1)} %all-gather.4.cloned.1.call-done, f32[2048]{0:T(1024)S(1)} %copy-done.42), kind=kOutput, calls=%fused_computation.20 | convolution fusion | flops 17184063488 | bytes 33562624 | tf_op jit(solution)/shard_map/dot_general | solution.py:24
  292.3 23.8 %convolution_convert_fusion = bf16[2048,2048]{1,0:T(8,128)(2,1)} fusion(bf16[2048,2048]{1,0:T(8,128)(2,1)} %get-tuple-element.88, bf16[2048,2048]{1,0:T(8,128)(2,1)} %all-gather.6.cloned.1.call-done), kind=kOutput, calls=%fused_computation.23 | convolution fusion | flops 17184063488 | bytes 25165824 | tf_op jit(solution)/shard_map/dot_general | solution.py:24
  327.2 13.4 %collective-permute-done.6 = bf16[256,2048]{1,0:T(8,128)(2,1)S(1)} collective-permute-done((bf16[256,2048]{1,0:T(8,128)(2,1)S(1)}, bf16[256,2048]{1,0:T(8,128)(2,1)S(1)}, u32[]{:S(2)}, u32[]{:S(2)}) %collective-permute-start.6) | collective-permute-done | bytes 1048608 | tf_op jit(solution)/shard_map/ppermute | solution.py:189
  368.8 11.1 %add_convert_fusion.4 = bf16[1024,2048]{1,0:T(8,128)(2,1)} fusion(bf16[1024,2048]{1,0:T(8,128)(2,1)S(1)} %collective-permute-done.8, bf16[2048,1024]{1,0:T(8,128)(2,1)S(1)} %get-tuple-element.96, bf16[2048,2048]{1,0:T(8,128)(2,1)S(1)} %bitcast.169), kind=kOutput, calls=%fused_computation.22 | convolution fusion | flops 8596226048 | bytes 20971520 | tf_op jit(solution)/shard_map/dot_general | solution.py:32
  380.4 25.3 %convert_reduce_fusion.1 = (f32[2048]{0:T(1024)S(1)}, bf16[2048,2048]{1,0:T(8,128)(2,1)}) fusion(bf16[2048,2048]{1,0:T(8,128)(2,1)} %get-tuple-element.99, bf16[2048,2048]{1,0:T(8,128)(2,1)} %copy-done.8, bf16[2048,2048]{1,0:T(8,128)(2,1)} %all-gather.6.cloned.1.call-done), kind=kOutput, calls=%fused_computation.11 | convolution fusion | flops 17200838656 | bytes 33562624 | tf_op jit(solution)/shard_map/dot_general | solution.py:28
  405.7 13.1 %convolution_convert_fusion.2 = bf16[1024,2048]{1,0:T(8,128)(2,1)} fusion(bf16[2048,1024]{1,0:T(8,128)(2,1)S(1)} %copy-done.28, bf16[2048,2048]{1,0:T(8,128)(2,1)} %get-tuple-element.117), kind=kOutput, calls=%fused_computation.59 | convolution fusion | flops 8592031744 | bytes 16777216 | tf_op jit(solution)/shard_map/dot_general | solution.py:32
  432.4 11.9 %add_convert_fusion.3 = bf16[1024,2048]{1,0:T(8,128)(2,1)} fusion(bf16[1024,2048]{1,0:T(8,128)(2,1)} %collective-permute-done.9, bf16[2048,1024]{1,0:T(8,128)(2,1)S(1)} %copy-done.27, bf16[2048,2048]{1,0:T(8,128)(2,1)S(1)} %copy-done.10), kind=kOutput, calls=%fused_computation.21 | convolution fusion | flops 8596226048 | bytes 20971520 | tf_op jit(solution)/shard_map/dot_general | solution.py:32
  445.0 19.4 %convolution_add_fusion = f32[2048,1536]{1,0:T(8,128)} fusion(bf16[2048,2048]{1,0:T(8,128)(2,1)} %copy-done, f32[1536]{0:T(1024)S(1)} %copy-done.43, bf16[2048,2048]{1,0:T(8,128)(2,1)} %all-gather.8.cloned.1.call-done), kind=kOutput, calls=%fused_computation.19 | convolution fusion | flops 12888047616 | bytes 27269120 | tf_op jit(solution)/shard_map/dot_general | solution.py:24
  467.5 20.9 %attention.1 = (bf16[4,2,256,512]{3,2,1,0:T(8,128)(2,1)}, bf16[4,2,256,1536]{3,2,1,0:T(8,128)(2,1)}) custom-call(s32[4]{0:T(128)} %and_select_fusion.slot_ref, s32[4]{0:T(128)} %reshape.176.starts_ref, f32[4,2,256,1536]{3,2,1,0:T(8,128)} %bitcast.189, bf16[4,2,256,512]{3,2,1,0:T(8,128)(2,1)} %bitcast.193, f32[1024,128]{1,0:T(8,128)} %get-tuple-element.104.cos_ref, ...), custom_call_target="tpu_custom_call" | custom-call | flops 16106127360 | bytes 23068672 | tf_op jit(solution)/shard_map/attention/pallas_call | solution.py:124
  488.4 12.6 %add_convert_fusion = bf16[2048,2048]{1,0:T(8,128)(2,1)} fusion(bf16[2048,2048]{1,0:T(8,128)(2,1)} %convolution_convert_fusion, bf16[2048,512]{1,0:T(8,128)(2,1)} %bitcast.190, bf16[2048,2048]{1,0:T(8,128)(2,1)} %all-gather.8.cloned.1.call-done), kind=kOutput, calls=%fused_computation.12 | convolution fusion | flops 4307550208 | bytes 20971520 | tf_op jit(solution)/shard_map/dot_general | solution.py:28
  512.8 22.0 %collective-permute-done.10 = bf16[256,2048]{1,0:T(8,128)(2,1)S(1)} collective-permute-done((bf16[256,2048]{1,0:T(8,128)(2,1)S(1)}, bf16[256,2048]{1,0:T(8,128)(2,1)S(1)}, u32[]{:S(2)}, u32[]{:S(2)}) %collective-permute-start.10) | collective-permute-done | bytes 1048608 | tf_op jit(solution)/shard_map/ppermute | solution.py:189
  586.6 10.5 %multiply_reduce_fusion.5 = (f32[2048]{0:T(1024)S(1)}, f32[2048]{0:T(1024)S(1)}, f32[2048]{0:T(1024)S(1)}, f32[2048]{0:T(1024)S(1)}, bf16[512,2048]{1,0:T(8,128)(2,1)S(1)}) fusion(f32[2048,2048]{1,0:T(8,128)} %get-tuple-element.228, f32[512,2048]{1,0:T(8,128)} %fusion.17, f32[2048]{0:T(1024)S(1)} %bitcast.180, f32[2048]{0:T(1024)S(1)} %bitcast.175, ...), kind=kOutput, calls=%fused_computation.51 | convolution fusion | flops 4305444864 | bytes 21020672 | tf_op jit(solution)/shard_map/dot_general | solution.py:28
  606.7 10.4 %multiply_reduce_fusion.3 = (f32[2048]{0:T(1024)S(1)}, f32[2048]{0:T(1024)S(1)}, f32[2048]{0:T(1024)S(1)}, f32[2048]{0:T(1024)S(1)}, bf16[512,2048]{1,0:T(8,128)(2,1)S(1)}) fusion(f32[2048,2048]{1,0:T(8,128)} %get-tuple-element.228, f32[512,2048]{1,0:T(8,128)} %fusion.15, f32[2048]{0:T(1024)S(1)} %bitcast.181, f32[2048]{0:T(1024)S(1)} %bitcast.176, ...), kind=kOutput, calls=%fused_computation.48 | convolution fusion | flops 4305444864 | bytes 21020672 | tf_op jit(solution)/shard_map/dot_general | solution.py:28
  627.9 11.6 %multiply_reduce_fusion.1 = (f32[2048]{0:T(1024)S(1)}, f32[2048]{0:T(1024)S(1)}, f32[2048]{0:T(1024)S(1)}, f32[2048]{0:T(1024)S(1)}, bf16[512,2048]{1,0:T(8,128)(2,1)}) fusion(f32[2048,2048]{1,0:T(8,128)} %get-tuple-element.228, f32[512,2048]{1,0:T(8,128)} %fusion.13, f32[2048]{0:T(1024)S(1)} %bitcast.182, f32[2048]{0:T(1024)S(1)} %bitcast.177, ...), kind=kOutput, calls=%fused_computation.45 | convolution fusion | flops 4305444864 | bytes 21020672 | tf_op jit(solution)/shard_map/dot_general | solution.py:28
  665.9 35.1 %collective-permute-done.19 = bf16[512,2048]{1,0:T(8,128)(2,1)} collective-permute-done((bf16[512,2048]{1,0:T(8,128)(2,1)}, bf16[512,2048]{1,0:T(8,128)(2,1)}, u32[]{:S(2)}, u32[]{:S(2)}) %collective-permute-start.19) | collective-permute-done | bytes 2097184 | tf_op jit(solution)/shard_map/ppermute | solution.py:189
  743.2 20.4 %collective-permute-done.22 = f32[10,128]{1,0:T(8,128)S(1)} collective-permute-done((f32[10,128]{1,0:T(8,128)S(1)}, f32[10,128]{1,0:T(8,128)S(1)}, u32[]{:S(2)}, u32[]{:S(2)}) %collective-permute-start.22) | collective-permute-done | bytes 5152 | tf_op jit(solution)/shard_map/ppermute | solution.py:276
  769.7 19.3 %reduce-scatter.11.cloned.1.call-done = bf16[256,512]{1,0:T(8,128)(2,1)} async-done(((bf16[1024,512]{1,0:T(8,128)(2,1)}), bf16[256,512]{1,0:T(8,128)(2,1)}) %reduce-scatter.11.cloned.1.call-update) | async-done | bytes 262160 | tf_op jit(solution)/shard_map/reduce_scatter | solution.py:336
  807.1 19.2 %all-to-all-done.8 = bf16[4,2,2,256,256]{4,3,1,2,0:T(8,128)(2,1)} async-done(((bf16[4,2,2,256,256]{4,3,1,2,0:T(8,128)(2,1)}), bf16[4,2,2,256,256]{4,3,1,2,0:T(8,128)(2,1)}, u32[]{:S(2)}, u32[]{:S(2)}) %all-to-all-start.8) | async-done | bytes 2097184 | tf_op jit(solution)/shard_map/all_to_all | solution.py:206
  (300 shorter events, 317.4 us)
Async XLA Ops:
  7.2 254.9 %all-gather.4.cloned.1.call-start = ((), (), s32[]{:S(2)}) async-start(), calls=%async_computation.13 | async-start | bytes 9437184 | tf_op jit(solution)/shard_map/all_gather | solution.py:283
  137.8 55.5 %all-to-all-start.4 = ((bf16[8,512,256]{2,1,0:T(8,128)(2,1)}), bf16[8,512,256]{2,1,0:T(8,128)(2,1)}, u32[]{:S(2)}, u32[]{:S(2)}) async-start(bf16[8,512,256]{2,1,0:T(8,128)(2,1)} %bitcast.10), calls=%async_computation.4 | async-start | bytes 4194304 | tf_op jit(solution)/shard_map/all_to_all | solution.py:198
  142.2 150.0 %all-gather.6.cloned.1.call-start = ((), (), s32[]{:S(2)}) async-start(), calls=%async_computation.14 | async-start | bytes 9437184 | tf_op jit(solution)/shard_map/all_gather | solution.py:292
  144.1 47.9 %collective-permute-start = (bf16[512,2048]{1,0:T(8,128)(2,1)S(1)}, bf16[512,2048]{1,0:T(8,128)(2,1)S(1)}, u32[]{:S(2)}, u32[]{:S(2)}) collective-permute-start(bf16[512,2048]{1,0:T(8,128)(2,1)S(1)} %bitcast.147), channel_id=1, source_target_pairs={{8,0},{24,8},{16,24},{0,16},{9,1},{25,9},{17,25},{1,17},{10,2},{26... | collective-permute-start | bytes 6291464 | tf_op jit(solution)/shard_map/ppermute | solution.py:190
  145.7 47.7 %collective-permute-start.1 = (bf16[512,2048]{1,0:T(8,128)(2,1)S(1)}, bf16[512,2048]{1,0:T(8,128)(2,1)}, u32[]{:S(2)}, u32[]{:S(2)}) collective-permute-start(bf16[512,2048]{1,0:T(8,128)(2,1)S(1)} %bitcast.148), channel_id=1, source_target_pairs={{0,8},{8,24},{24,16},{16,0},{1,9},{9,25},{25,17},{17,1},{2,10},{10... | collective-permute-start | bytes 6291464 | tf_op jit(solution)/shard_map/ppermute | solution.py:189
  193.4 187.0 %all-gather.8.cloned.1.call-start = ((), (), s32[]{:S(2)}) async-start(), calls=%async_computation.15 | async-start | bytes 9437184 | tf_op jit(solution)/shard_map/all_gather | solution.py:295
  259.7 56.3 %collective-permute-start.4 = (bf16[512,2048]{1,0:T(8,128)(2,1)S(1)}, bf16[512,2048]{1,0:T(8,128)(2,1)}, u32[]{:S(2)}, u32[]{:S(2)}) collective-permute-start(bf16[512,2048]{1,0:T(8,128)(2,1)S(1)} %bitcast.162), channel_id=1, source_target_pairs={{8,0},{24,8},{16,24},{0,16},{9,1},{25,9},{17,25},{1,17},{10,2},{26... | collective-permute-start | bytes 6291464 | tf_op jit(solution)/shard_map/ppermute | solution.py:190
  260.2 55.9 %collective-permute-start.5 = (bf16[512,2048]{1,0:T(8,128)(2,1)S(1)}, bf16[512,2048]{1,0:T(8,128)(2,1)}, u32[]{:S(2)}, u32[]{:S(2)}) collective-permute-start(bf16[512,2048]{1,0:T(8,128)(2,1)S(1)} %bitcast.163), channel_id=1, source_target_pairs={{0,8},{8,24},{24,16},{16,0},{1,9},{9,25},{25,17},{17,1},{2,10},{10... | collective-permute-start | bytes 6291464 | tf_op jit(solution)/shard_map/ppermute | solution.py:189
  261.8 202.6 %reduce-scatter.5.cloned.1.call-start = ((), (), s32[]{:S(2)}) async-start(), calls=%async_computation.16 | async-start | bytes 5242880 | tf_op jit(solution)/shard_map/reduce_scatter | solution.py:336
  380.0 168.5 %reduce-scatter.7.cloned.1.call-start = ((), (), s32[]{:S(2)}) async-start(), calls=%async_computation.17 | async-start | bytes 5242880 | tf_op jit(solution)/shard_map/reduce_scatter | solution.py:336
  444.3 272.8 %reduce-scatter.9.cloned.1.call-start = ((), (), s32[]{:S(2)}) async-start(), calls=%async_computation.18 | async-start | bytes 3932160 | tf_op jit(solution)/shard_map/reduce_scatter | solution.py:336
  508.4 31.0 %collective-permute-start.14 = (bf16[1024,1536]{1,0:T(8,128)(2,1)S(1)}, bf16[1024,1536]{1,0:T(8,128)(2,1)S(1)}, u32[]{:S(2)}, u32[]{:S(2)}) collective-permute-start(bf16[1024,1536]{1,0:T(8,128)(2,1)S(1)} %convolution_convert_fusion.1), channel_id=1, source_target_pairs={{0,1},{1,0},{2,3},{3,2},{4,5},{5,4},{6,7},{7,6},{8,9},{9,8},{10,11... | collective-permute-start | bytes 9437192 | tf_op jit(solution)/shard_map/ppermute | solution.py:330
  535.8 103.7 %collective-permute-start.13 = (bf16[512,2048]{1,0:T(8,128)(2,1)S(1)}, bf16[512,2048]{1,0:T(8,128)(2,1)}, u32[]{:S(2)}, u32[]{:S(2)}) collective-permute-start(bf16[512,2048]{1,0:T(8,128)(2,1)S(1)} %pad_maximum_fusion.7), channel_id=1, source_target_pairs={{8,0},{24,8},{16,24},{0,16},{9,1},{25,9},{17,25},{1,17},{10,2},{26... | collective-permute-start | bytes 6291464 | tf_op jit(solution)/shard_map/ppermute | solution.py:190
  539.1 100.4 %collective-permute-start.12 = (bf16[512,2048]{1,0:T(8,128)(2,1)}, bf16[512,2048]{1,0:T(8,128)(2,1)}, u32[]{:S(2)}, u32[]{:S(2)}) collective-permute-start(bf16[512,2048]{1,0:T(8,128)(2,1)} %pad_maximum_fusion.6), channel_id=1, source_target_pairs={{0,8},{8,24},{24,16},{16,0},{1,9},{9,25},{25,17},{17,1},{2,10},{10... | collective-permute-start | bytes 6291464 | tf_op jit(solution)/shard_map/ppermute | solution.py:189
  617.1 31.9 %collective-permute-start.18 = (bf16[256,2048]{1,0:T(8,128)(2,1)}, bf16[256,2048]{1,0:T(8,128)(2,1)}, u32[]{:S(2)}, u32[]{:S(2)}) collective-permute-start(bf16[256,2048]{1,0:T(8,128)(2,1)} %get-tuple-element.273), channel_id=1, source_target_pairs={{0,8},{8,24},{24,16},{16,0},{1,9},{9,25},{25,17},{17,1},{2,10},{10... | collective-permute-start | bytes 3145736 | tf_op jit(solution)/shard_map/ppermute | solution.py:189
  617.2 35.6 %collective-permute-start.20 = (bf16[256,2048]{1,0:T(8,128)(2,1)}, bf16[256,2048]{1,0:T(8,128)(2,1)S(1)}, u32[]{:S(2)}, u32[]{:S(2)}) collective-permute-start(bf16[256,2048]{1,0:T(8,128)(2,1)} %get-tuple-element.274), channel_id=1, source_target_pairs={{8,0},{24,8},{16,24},{0,16},{9,1},{25,9},{17,25},{1,17},{10,2},{26... | collective-permute-start | bytes 3145736 | tf_op jit(solution)/shard_map/ppermute | solution.py:190
  644.6 62.2 %all-to-all-start.5 = ((bf16[8,512,256]{2,1,0:T(8,128)(2,1)}), bf16[8,512,256]{2,1,0:T(8,128)(2,1)}, u32[]{:S(2)}, u32[]{:S(2)}) async-start(bf16[8,512,256]{2,1,0:T(8,128)(2,1)} %bitcast.146), calls=%async_computation.7 | async-start | bytes 4194304 | tf_op jit(solution)/shard_map/all_to_all | solution.py:198
  652.7 48.3 %collective-permute-start.19 = (bf16[512,2048]{1,0:T(8,128)(2,1)}, bf16[512,2048]{1,0:T(8,128)(2,1)}, u32[]{:S(2)}, u32[]{:S(2)}) collective-permute-start(bf16[512,2048]{1,0:T(8,128)(2,1)} %pad_maximum_fusion.8), channel_id=1, source_target_pairs={{0,8},{8,24},{24,16},{16,0},{1,9},{9,25},{25,17},{17,1},{2,10},{10... | collective-permute-start | bytes 6291464 | tf_op jit(solution)/shard_map/ppermute | solution.py:189
  654.8 48.2 %collective-permute-start.21 = (bf16[512,2048]{1,0:T(8,128)(2,1)}, bf16[512,2048]{1,0:T(8,128)(2,1)}, u32[]{:S(2)}, u32[]{:S(2)}) collective-permute-start(bf16[512,2048]{1,0:T(8,128)(2,1)} %pad_maximum_fusion.9), channel_id=1, source_target_pairs={{8,0},{24,8},{16,24},{0,16},{9,1},{25,9},{17,25},{1,17},{10,2},{26... | collective-permute-start | bytes 6291464 | tf_op jit(solution)/shard_map/ppermute | solution.py:190
  665.9 62.6 %collective-permute-start.24 = (bf16[1024,512]{1,0:T(8,128)(2,1)}, bf16[1024,512]{1,0:T(8,128)(2,1)}, u32[]{:S(2)}, u32[]{:S(2)}) collective-permute-start(bf16[1024,512]{1,0:T(8,128)(2,1)} %convolution_convert_fusion.5), channel_id=1, source_target_pairs={{0,1},{1,0},{2,3},{3,2},{4,5},{5,4},{6,7},{7,6},{8,9},{9,8},{10,11... | collective-permute-start | bytes 3145736 | tf_op jit(solution)/shard_map/ppermute | solution.py:330
  722.8 71.1 %all-to-all-start.7 = ((bf16[8,512,256]{2,1,0:T(8,128)(2,1)}), bf16[8,512,256]{2,1,0:T(8,128)(2,1)}, u32[]{:S(2)}, u32[]{:S(2)}) async-start(bf16[8,512,256]{2,1,0:T(8,128)(2,1)} %bitcast.161), calls=%async_computation.10 | async-start | bytes 4194304 | tf_op jit(solution)/shard_map/all_to_all | solution.py:198
  727.9 61.1 %reduce-scatter.11.cloned.1.call-start = ((), (), s32[]{:S(2)}) async-start(), calls=%async_computation.19 | async-start | bytes 1310720 | tf_op jit(solution)/shard_map/reduce_scatter | solution.py:336
  737.6 27.7 %collective-permute-start.15 = (bf16[2,2,256,256]{3,2,0,1:T(8,128)(2,1)}, bf16[2,2,256,256]{3,2,0,1:T(8,128)(2,1)}, u32[]{:S(2)}, u32[]{:S(2)}) collective-permute-start(bf16[2,2,256,256]{3,2,0,1:T(8,128)(2,1)} %get-tuple-element.277), channel_id=1, source_target_pairs={{0,8},{8,0},{16,24},{24,16},{1,9},{9,1},{17,25},{25,17},{2,10},{10... | collective-permute-start | bytes 1572872 | tf_op jit(solution)/shard_map/ppermute | solution.py:215
  796.9 29.4 %all-to-all-start.8 = ((bf16[4,2,2,256,256]{4,3,1,2,0:T(8,128)(2,1)}), bf16[4,2,2,256,256]{4,3,1,2,0:T(8,128)(2,1)}, u32[]{:S(2)}, u32[]{:S(2)}) async-start(bf16[4,2,2,256,256]{4,3,1,2,0:T(8,128)(2,1)} %copy.86), calls=%async_computation.12 | async-start | bytes 4194304 | tf_op jit(solution)/shard_map/all_to_all | solution.py:206
  (63 other events, 1047.7 us)
Sparse Core Ops, SparseCore 0:
  9.6 91.3 all-gather.3
  193.5 83.5 all-gather.5
  279.3 80.2 all-gather.7
  380.1 75.9 reduce-scatter.4
  458.2 77.2 reduce-scatter.6
  548.6 60.4 reduce-scatter.8
  741.2 47.7 reduce-scatter.10

commit v6 on v3

--- a/solution.py
+++ b/solution.py
@@ -201,8 +201,7 @@
         return b.transpose(1, 0, 2).reshape(block_rows, cols * width)
 
     def from_rows(block, *earlier):
-        b = block.reshape(block_rows, cols, width).transpose(1, 0, 2)
-        b = col_swap(b).reshape(rows, per_row, micro, part, width)
+        b = block.reshape(rows, per_row, micro, part, width)
         if earlier:
             b = lax.all_to_all(after(b, *earlier), "row", split_axis=0, concat_axis=0, tiled=True)
             return b.transpose(2, 1, 0, 3, 4).reshape(micro, own_tokens, width)
@@ -294,14 +293,13 @@
     activated = (expand_pre * phi_sum).astype(BF)
     slope = (phi_sum + expand_pre * density).astype(BF)
     activated, slope = lax.optimization_barrier((activated, slope))
-    branch_ff = mm(activated, reduce_w).astype(BF)
-    cot_seq = ring_gather(cot_part, branch_ff)
+    cot_seq = ring_gather(cot_part, activated)
 
     def scatter_weight(grad):
         return lax.psum_scatter(grad, "col", scatter_dimension=0, tiled=True).astype(F32)
 
-    cot_seq, branch_ff, attend_in, *tables = lax.optimization_barrier(
-        (cot_seq, branch_ff, attend_in) + rotary_tables()
+    cot_seq, attend_in, *tables = lax.optimization_barrier(
+        (cot_seq, attend_in) + rotary_tables()
     )
     reduce_dot = contract_first(cot_seq, activated).astype(BF)
     reduce_grad = scatter_weight(reduce_dot).T
@@ -311,6 +309,7 @@
     expand_dot = contract_first(expand_in, grad_pre).astype(BF)
     expand_grad = scatter_weight(expand_dot)
 
+    branch_ff = mm(after(activated, expand_dot), reduce_w).astype(BF)
     merged_pre = mm(after(attend_in, expand_dot), merged_w) + merged_bias
     grad_mix = mm(after(cot_seq, expand_dot), output_wt).astype(BF)
     mix, grad_merged = attention(
@@ -323,7 +322,6 @@
     )[:2]
     merged_dot = contract_first(attend_late, grad_merged).astype(BF)
     merged_grad = scatter_weight(merged_dot)
-
     grad_merged, grad_pre, half_up, half_down = lax.optimization_barrier(
         (grad_merged, grad_pre) + halves + (merged_dot,)
     )[:4]
@@ -339,6 +337,7 @@
         ]
     )
     grad_hat = (grad_first * gains[0] + grad_second * gains[2]).astype(BF)
+    grad_hat = after(grad_hat, expand_grad)
     halves = ring_open(grad_hat)
     merged_b = jnp.sum(grad_merged.astype(F32), axis=0)
     shift_b = jnp.sum(cotangent.astype(F32), axis=(0, 1))
@@ -350,13 +349,10 @@
         ],
         axis=1,
     ).reshape(cols, -1, 128)
-    spread_sums = lax.all_to_all(sums, "col", split_axis=0, concat_axis=0, tiled=True)
-    mix_late, cot_late = lax.optimization_barrier(
-        (mix, cot_seq, grad_hat, expand_grad, branch, spread_sums)
-    )[:2]
-    output_dot = contract_first(cot_late, mix_late).astype(BF)
-    output_grad = scatter_weight(after(output_dot, merged_grad)).T
-    halves = lax.optimization_barrier(halves + (output_dot,))[:2]
+    branch = col_swap(branch.astype(BF).reshape(block_rows, cols, width).transpose(1, 0, 2))
+    spread_sums = lax.all_to_all(
+        after(sums, branch), "col", split_axis=0, concat_axis=0, tiled=True
+    )
     grad_hat = ring_close(grad_hat, halves)
     sums = jnp.sum(spread_sums.reshape(cols, -1), axis=0)
     merged_b = sums[4 * width : 4 * width + merged_cols]
@@ -372,7 +368,7 @@
         far_tail = broadcast(tail, "row", rows)
         tail = jnp.sum(far_tail, axis=0)
     tail = tail.reshape(5, width)
-    branch = from_rows(branch.astype(BF))
+    branch = from_rows(branch)
     result = inputs.astype(F32) + branch.astype(F32) + output_bias + reduce_bias
     result = result.astype(BF)
 
@@ -383,8 +379,12 @@
         - part_normed * jnp.mean(grad_hat * part_normed, axis=-1, keepdims=True)
     )
 
-    norm_part = after(norm_part.astype(BF), output_grad, merged_grad)
-    input_grad = cotangent.astype(F32) + from_rows(norm_part, result, far_tail).astype(F32)
+    norm_part = after(norm_part.astype(BF), merged_grad, spread_sums)
+    norm_part = col_swap(norm_part.reshape(block_rows, cols, width).transpose(1, 0, 2))
+    mix_late, cot_late = lax.optimization_barrier((mix, cot_seq, grad_hat, far_tail))[:2]
+    output_dot = contract_first(cot_late, mix_late).astype(BF)
+    output_grad = scatter_weight(after(output_dot, norm_part)).T
+    input_grad = cotangent.astype(F32) + from_rows(norm_part, result, output_dot).astype(F32)
     norm_sums, shift_b = tail[:4], tail[4]
     return (
         result,

time: 797 us -> 797 us (level)
  local copies, waits for them, and re-layouts: 62.5 us -> 79.8 us
  other arithmetic: 88.4 us -> 72.1 us
  waiting for transfers between devices: 206 us -> 194 us
    all_to_all x3, waiting for transfers between devices: 50.9 us -> 94.6 us  [col_swap(): return lax.all_to_all(b, 'col', split_axis=0, concat_axis=0, tiled=True)]
    ppermute x8, waiting for transfers between devices: 35.7 us -> 2.77 us  [body(): down = lambda v: lax.ppermute(v, 'row', behind)]
    unnamed x74 -> x86, local copies, waits for them, and re-layouts: 20.8 us -> 33.7 us
    ppermute x3, waiting for transfers between devices: 11.7 us -> 0.01 us  [from_rows(): lax.ppermute(piece, 'row', [(r, partner(r, step)) for r in range(rows)])]
    ppermute x2, waiting for transfers between devices: 11.4 us -> 0.01 us  [body(): far_tail = lax.ppermute(tail, 'row', [(r, r ^ step) for r in range(rows)])]
  transfers between devices with their start and end apart: 33 -> 33, of which waited for: 16 -> 10; matrix products, arithmetic and copies ran while one was open for 45% -> 46% of each run, Pallas kernels for 3% -> 3%
where the time goes in v6:
time: 797 us; the launch traced here: 788 us
  matrix products  229 us (29%)
  waiting for transfers between devices  194 us (24%)
  blocking collectives  125 us (16%)
  local copies, waits for them, and re-layouts  79.8 us (10%)
  other arithmetic  72.1 us (9%)
  starting transfers between devices  51.5 us (6%)
  Pallas kernels  21.4 us (3%)
  between operations  15.2 us (2%)
    all_to_all x3, waiting for transfers between devices, col_swap(): return lax.all_to_all(b, 'col', split_axis=0, concat_axis=0, tiled=True)  94.6 us
    dot_general x4, matrix products, contract_last(): lax.dot_general(left, right, (((1,), (1,)), ((), ())), preferred_element_...  83.6 us
    ppermute x8, waiting for transfers between devices, body(): up = lambda v: lax.ppermute(v, 'row', ahead)  75.3 us
    dot_general x4, matrix products, mm(): return jnp.dot(left, right, preferred_element_type=F32)  74.5 us
    dot_general x4, matrix products, contract_first(): lax.dot_general(left, right, (((0,), (0,)), ((), ())), preferred_element_...  71.1 us
    all_to_all x1, blocking collectives, col_swap(): return lax.all_to_all(b, 'col', split_axis=0, concat_axis=0, tiled=True)  57.9 us
    all_to_all x2, blocking collectives, row_swap(): b = lax.all_to_all(b, 'row', split_axis=0, concat_axis=0, tiled=True)  55.5 us
    unnamed x86, local copies, waits for them, and re-layouts  33.7 us
  transfers between devices with their start and end apart: 33, of which 10 were waited for; matrix products, arithmetic and copies ran while one was open for 46% of the time, Pallas kernels for 3%

profile of v6, /device:TPU:0, one launch (start us, length us, event | category | flops | bytes accessed | tf_op | source)
XLA Modules:
  0.0 788.2 jit_solution(15875712076311703258)
XLA Ops:
  8.7 11.9 %all_to_all.45 = f32[8,4,256]{2,1,0:T(4,128)S(1)} all-to-all(f32[8,4,256]{2,1,0:T(4,128)S(1)} %broadcast_in_dim.21), channel_id=1, replica_groups=mesh['row'=4,'col'=8] {'col'}, dimensions={0} | all-to-all | bytes 65536 | tf_op jit(solution)/shard_map/all_to_all | solution.py:265
  22.6 28.8 %all_to_all.46 = bf16[4,2,2,256,256]{4,3,1,2,0:T(8,128)(2,1)S(1)} all-to-all(bf16[4,2,2,256,256]{4,3,1,2,0:T(8,128)(2,1)S(1)} %copy.91), channel_id=1, replica_groups=mesh['row'=4,'col'=8] {'row'}, dimensions={0} | all-to-all | bytes 4194304 | tf_op jit(solution)/shard_map/all_to_all | solution.py:194
  51.7 26.7 %all_to_all.47 = bf16[4,2,2,256,256]{4,3,1,2,0:T(8,128)(2,1)S(1)} all-to-all(bf16[4,2,2,256,256]{4,3,1,2,0:T(8,128)(2,1)S(1)} %copy.93), channel_id=1, replica_groups=mesh['row'=4,'col'=8] {'row'}, dimensions={0} | all-to-all | bytes 4194304 | tf_op jit(solution)/shard_map/all_to_all | solution.py:194
  79.9 57.9 %all_to_all.48 = bf16[8,512,256]{2,1,0:T(8,128)(2,1)} all-to-all(bf16[8,512,256]{2,1,0:T(8,128)(2,1)S(1)} %bitcast.133), channel_id=1, replica_groups=mesh['row'=4,'col'=8] {'col'}, dimensions={0} | all-to-all | bytes 4194304 | tf_op jit(solution)/shard_map/all_to_all | solution.py:198
  148.5 43.8 %collective-permute-done.3 = bf16[512,2048]{1,0:T(8,128)(2,1)S(1)} collective-permute-done((bf16[512,2048]{1,0:T(8,128)(2,1)S(1)}, bf16[512,2048]{1,0:T(8,128)(2,1)S(1)}, u32[]{:S(2)}, u32[]{:S(2)}) %collective-permute-start.3) | collective-permute-done | bytes 2097184 | tf_op jit(solution)/shard_map/ppermute | solution.py:189
  205.2 41.4 %all-to-all-done.4 = bf16[8,512,256]{2,1,0:T(8,128)(2,1)} async-done(((bf16[8,512,256]{2,1,0:T(8,128)(2,1)}), bf16[8,512,256]{2,1,0:T(8,128)(2,1)}, u32[]{:S(2)}, u32[]{:S(2)}) %all-to-all-start.4) | async-done | bytes 2097184 | tf_op jit(solution)/shard_map/all_to_all | solution.py:198
  269.4 22.8 %convolution_add_fusion.1 = f32[2048,2048]{1,0:T(8,128)S(1)} fusion(bf16[2048,2048]{1,0:T(8,128)(2,1)} %all-gather.4.cloned.1.call-done, f32[2048]{0:T(1024)S(1)} %copy-done.25, bf16[2048,2048]{1,0:T(8,128)(2,1)} %constant_dynamic-update-slice_fusion, f32[2048]{0:T(1024)S(1)} %bitcast.153, f32[2048]{0:T(1024)S(1)} %bitcast.150, ...), kind=kOutput, calls=%fused_computation.29 | convolution fusion | flops 17209229312 | bytes 33595392 | tf_op jit(solution)/shard_map/dot_general | solution.py:24
  300.9 12.3 %collective-permute-done.1 = bf16[512,2048]{0,1:T(8,128)(2,1)} collective-permute-done((bf16[512,2048]{0,1:T(8,128)(2,1)S(1)}, bf16[512,2048]{0,1:T(8,128)(2,1)}, u32[]{:S(2)}, u32[]{:S(2)}) %collective-permute-start.1) | collective-permute-done | bytes 2097184 | tf_op jit(solution)/shard_map/ppermute | solution.py:189
  327.1 12.7 %collective-permute-done.6 = bf16[256,2048]{0,1:T(8,128)(2,1)S(1)} collective-permute-done((bf16[256,2048]{0,1:T(8,128)(2,1)S(1)}, bf16[256,2048]{0,1:T(8,128)(2,1)S(1)}, u32[]{:S(2)}, u32[]{:S(2)}) %collective-permute-start.6) | collective-permute-done | bytes 1048608 | tf_op jit(solution)/shard_map/ppermute | solution.py:189
  345.4 19.5 %convolution_convert_fusion.1 = bf16[2048,2048]{1,0:T(8,128)(2,1)} fusion(bf16[2048,2048]{0,1:T(8,128)(2,1)S(1)} %constant_dynamic-update-slice_fusion.5, bf16[2048,2048]{1,0:T(8,128)(2,1)S(1)} %bitcast.135), kind=kOutput, calls=%fused_computation.31 | convolution fusion | flops 17184063488 | bytes 25165824 | tf_op jit(solution)/shard_map/dot_general | solution.py:32
  365.4 24.4 %convert_reduce_fusion.1 = (f32[2048]{0:T(1024)}, bf16[2048,2048]{1,0:T(8,128)(2,1)S(1)}) fusion(bf16[2048,2048]{1,0:T(8,128)(2,1)} %get-tuple-element.58, bf16[2048,2048]{0,1:T(8,128)(2,1)} %copy-done.10, bf16[2048,2048]{1,0:T(8,128)(2,1)} %all-gather.6.cloned.1.call-done), kind=kOutput, calls=%fused_computation.21 | convolution fusion | flops 17200838656 | bytes 33562624 | tf_op jit(solution)/shard_map/dot_general | solution.py:28
  393.1 22.6 %convolution_convert_fusion = bf16[2048,2048]{1,0:T(8,128)(2,1)} fusion(bf16[2048,2048]{1,0:T(8,128)(2,1)S(1)} %get-tuple-element.72, bf16[2048,2048]{1,0:T(8,128)(2,1)} %constant_dynamic-update-slice_fusion, f32[2048]{0:T(1024)S(1)} %bitcast.154, f32[2048]{0:T(1024)S(1)} %bitcast.151, f32[2048]{0:T(1024)S(1)} %add_rsqrt_fusion, ...), kind=kOutput, calls=%fused_computation.30 | convolution fusion | flops 17209229312 | bytes 25198592 | tf_op jit(solution)/shard_map/dot_general | solution.py:32
  419.3 24.0 %fusion.37 = bf16[2048,2048]{0,1:T(8,128)(2,1)} fusion(bf16[2048,2048]{1,0:T(8,128)(2,1)} %get-tuple-element.65, bf16[2048,2048]{1,0:T(8,128)(2,1)} %all-gather.6.cloned.1.call-done), kind=kOutput, calls=%fused_computation.120 | convolution fusion | flops 17179869184 | bytes 25165824 | tf_op jit(solution)/shard_map/dot_general | solution.py:24
  443.3 10.0 %convolution_convert_fusion.4 = bf16[2048,512]{1,0:T(8,128)(2,1)} fusion(bf16[2048,2048]{0,1:T(8,128)(2,1)} %copy-done.10, bf16[2048,2048]{1,0:T(8,128)(2,1)} %all-gather.8.cloned.1.call-done), kind=kOutput, calls=%fused_computation.52 | convolution fusion | flops 4296015872 | bytes 12582912 | tf_op jit(solution)/shard_map/dot_general | solution.py:24
  453.3 17.8 %convolution_add_fusion = f32[2048,1536]{1,0:T(8,128)} fusion(bf16[2048,2048]{1,0:T(8,128)(2,1)} %fusion.9, f32[1536]{0:T(1024)S(1)} %copy-done.26, bf16[2048,2048]{1,0:T(8,128)(2,1)S(1)} %copy-done.24), kind=kOutput, calls=%fused_computation.28 | convolution fusion | flops 12888047616 | bytes 27271168 | tf_op jit(solution)/shard_map/dot_general | solution.py:24
  471.1 21.4 %attention.1 = (bf16[4,2,256,512]{3,2,1,0:T(8,128)(2,1)}, bf16[4,2,256,1536]{3,2,1,0:T(8,128)(2,1)}) custom-call(s32[4]{0:T(128)} %and_select_fusion.slot_ref, s32[4]{0:T(128)} %reshape.176.starts_ref, f32[4,2,256,1536]{3,2,1,0:T(8,128)} %bitcast.159, bf16[4,2,256,512]{3,2,1,0:T(8,128)(2,1)} %bitcast.162, f32[1024,128]{1,0:T(8,128)} %get-tuple-element.62.cos_ref, ...), custom_call_target="tpu_custom_call" | custom-call | flops 16106127360 | bytes 23068672 | tf_op jit(solution)/shard_map/attention/pallas_call | solution.py:124
  492.5 9.3 %add_convert_fusion.1 = bf16[2048,2048]{0,1:T(8,128)(2,1)S(1)} fusion(bf16[2048,2048]{0,1:T(8,128)(2,1)} %fusion.37, bf16[2048,512]{1,0:T(8,128)(2,1)} %bitcast.160, bf16[2048,2048]{1,0:T(8,128)(2,1)} %all-gather.8.cloned.1.call-done), kind=kOutput, calls=%fused_computation.23 | convolution fusion | flops 4307550208 | bytes 20971520 | tf_op jit(solution)/shard_map/dot_general | solution.py:28
  511.4 19.3 %convolution_convert_fusion.2 = bf16[2048,1536]{1,0:T(8,128)(2,1)} fusion(bf16[2048,2048]{1,0:T(8,128)(2,1)} %fusion.9, bf16[2048,1536]{1,0:T(8,128)(2,1)} %bitcast.136), kind=kOutput, calls=%fused_computation.32 | convolution fusion | flops 12888047616 | bytes 20971520 | tf_op jit(solution)/shard_map/dot_general | solution.py:32
  538.2 24.6 %fusion.38 = f32[2048,2048]{1,0:T(8,128)} fusion(bf16[2048,2048]{1,0:T(8,128)(2,1)} %copy-done.28, bf16[2048,2048]{1,0:T(8,128)(2,1)} %all-gather.4.cloned.1.call-done), kind=kOutput, calls=%fused_computation.121 | convolution fusion | flops 17179869184 | bytes 33554432 | tf_op jit(solution)/shard_map/dot_general | solution.py:28
  562.8 25.3 %fusion.10 = (f32[2048]{0:T(1024)S(1)}, f32[2048]{0:T(1024)S(1)}, f32[2048]{0:T(1024)S(1)}, f32[2048]{0:T(1024)S(1)}, bf16[2048,2048]{1,0:T(8,128)(2,1)}) fusion(bf16[2048,2048]{1,0:T(8,128)(2,1)} %constant_dynamic-update-slice_fusion, f32[2048]{0:T(1024)S(1)} %copy-done.14, f32[2048]{0:T(1024)S(1)} %copy-done.12, f32[2048,2048]{1,0:T(8,128)} %fusion.38, ...), kind=kOutput, calls=%fused_computation.13 | convolution fusion | flops 12939419648 | bytes 46202880 | tf_op jit(solution)/shard_map/dot_general | solution.py:28
  626.8 34.6 %all-to-all-done.5 = bf16[8,512,256]{1,2,0:T(8,128)(2,1)} async-done(((bf16[8,512,256]{1,2,0:T(8,128)(2,1)}), bf16[8,512,256]{1,2,0:T(8,128)(2,1)}, u32[]{:S(2)}, u32[]{:S(2)}) %all-to-all-start.5) | async-done | bytes 2097184 | tf_op jit(solution)/shard_map/all_to_all | solution.py:198
  706.5 9.8 %convolution_convert_fusion.3 = bf16[2048,512]{1,0:T(8,128)(2,1)} fusion(bf16[2048,2048]{0,1:T(8,128)(2,1)} %copy-done.10, bf16[2048,512]{1,0:T(8,128)(2,1)} %bitcast.161), kind=kOutput, calls=%fused_computation.51 | convolution fusion | flops 4296015872 | bytes 12582912 | tf_op jit(solution)/shard_map/dot_general | solution.py:32
  716.3 18.6 %all-to-all-done.7 = bf16[8,512,256]{2,1,0:T(8,128)(2,1)} async-done(((bf16[8,512,256]{2,1,0:T(8,128)(2,1)}), bf16[8,512,256]{2,1,0:T(8,128)(2,1)}, u32[]{:S(2)}, u32[]{:S(2)}) %all-to-all-start.7) | async-done | bytes 2097184 | tf_op jit(solution)/shard_map/all_to_all | solution.py:198
  753.4 20.2 %all-to-all-done.8 = bf16[4,2,2,256,256]{4,3,1,2,0:T(8,128)(2,1)} async-done(((bf16[4,2,2,256,256]{4,3,1,2,0:T(8,128)(2,1)}), bf16[4,2,2,256,256]{4,3,1,2,0:T(8,128)(2,1)}, u32[]{:S(2)}, u32[]{:S(2)}) %all-to-all-start.8) | async-done | bytes 2097184 | tf_op jit(solution)/shard_map/all_to_all | solution.py:206
  (242 shorter events, 213.6 us)
Async XLA Ops:
  7.2 262.2 %all-gather.4.cloned.1.call-start = ((), (), s32[]{:S(2)}) async-start(), calls=%async_computation.13 | async-start | bytes 9437184 | tf_op jit(solution)/shard_map/all_gather | solution.py:272
  7.9 357.4 %all-gather.6.cloned.1.call-start = ((), (), s32[]{:S(2)}) async-start(), calls=%async_computation.14 | async-start | bytes 9437184 | tf_op jit(solution)/shard_map/all_gather | solution.py:276
  137.9 108.7 %all-to-all-start.4 = ((bf16[8,512,256]{2,1,0:T(8,128)(2,1)}), bf16[8,512,256]{2,1,0:T(8,128)(2,1)}, u32[]{:S(2)}, u32[]{:S(2)}) async-start(bf16[8,512,256]{2,1,0:T(8,128)(2,1)} %bitcast.10), calls=%async_computation.4 | async-start | bytes 4194304 | tf_op jit(solution)/shard_map/all_to_all | solution.py:198
  142.3 301.0 %all-gather.8.cloned.1.call-start = ((), (), s32[]{:S(2)}) async-start(), calls=%async_computation.15 | async-start | bytes 9437184 | tf_op jit(solution)/shard_map/all_gather | solution.py:289
  144.4 47.9 %collective-permute-start.3 = (bf16[512,2048]{1,0:T(8,128)(2,1)S(1)}, bf16[512,2048]{1,0:T(8,128)(2,1)S(1)}, u32[]{:S(2)}, u32[]{:S(2)}) collective-permute-start(bf16[512,2048]{1,0:T(8,128)(2,1)S(1)} %bitcast.120), channel_id=1, source_target_pairs={{0,8},{8,24},{24,16},{16,0},{1,9},{9,25},{25,17},{17,1},{2,10},{10... | collective-permute-start | bytes 6291464 | tf_op jit(solution)/shard_map/ppermute | solution.py:189
  145.9 52.7 %collective-permute-start.2 = (bf16[512,2048]{1,0:T(8,128)(2,1)S(1)}, bf16[512,2048]{1,0:T(8,128)(2,1)}, u32[]{:S(2)}, u32[]{:S(2)}) collective-permute-start(bf16[512,2048]{1,0:T(8,128)(2,1)S(1)} %bitcast.121), channel_id=1, source_target_pairs={{8,0},{24,8},{16,24},{0,16},{9,1},{25,9},{17,25},{1,17},{10,2},{26... | collective-permute-start | bytes 6291464 | tf_op jit(solution)/shard_map/ppermute | solution.py:190
  194.6 59.3 %collective-permute-start.4 = (bf16[256,2048]{1,0:T(8,128)(2,1)}, bf16[256,2048]{1,0:T(8,128)(2,1)S(1)}, u32[]{:S(2)}, u32[]{:S(2)}) collective-permute-start(bf16[256,2048]{1,0:T(8,128)(2,1)} %slice.196), channel_id=1, source_target_pairs={{0,8},{8,24},{24,16},{16,0},{1,9},{9,25},{25,17},{17,1},{2,10},{10... | collective-permute-start | bytes 3145736 | tf_op jit(solution)/shard_map/ppermute | solution.py:189
  200.9 54.1 %collective-permute-start.5 = (bf16[256,2048]{1,0:T(8,128)(2,1)}, bf16[256,2048]{1,0:T(8,128)(2,1)}, u32[]{:S(2)}, u32[]{:S(2)}) collective-permute-start(bf16[256,2048]{1,0:T(8,128)(2,1)} %slice.197), channel_id=1, source_target_pairs={{8,0},{24,8},{16,24},{0,16},{9,1},{25,9},{17,25},{1,17},{10,2},{26... | collective-permute-start | bytes 3145736 | tf_op jit(solution)/shard_map/ppermute | solution.py:190
  250.5 258.1 %reduce-scatter.5.cloned.1.call-start = ((), (), s32[]{:S(2)}) async-start(), calls=%async_computation.16 | async-start | bytes 9437184 | tf_op jit(solution)/shard_map/reduce_scatter | solution.py:299
  267.1 46.1 %collective-permute-start.1 = (bf16[512,2048]{0,1:T(8,128)(2,1)S(1)}, bf16[512,2048]{0,1:T(8,128)(2,1)}, u32[]{:S(2)}, u32[]{:S(2)}) collective-permute-start(bf16[512,2048]{0,1:T(8,128)(2,1)S(1)} %bitcast.130), channel_id=1, source_target_pairs={{0,8},{8,24},{24,16},{16,0},{1,9},{9,25},{25,17},{17,1},{2,10},{10... | collective-permute-start | bytes 6291464 | tf_op jit(solution)/shard_map/ppermute | solution.py:189
  268.6 45.9 %collective-permute-start = (bf16[512,2048]{0,1:T(8,128)(2,1)S(1)}, bf16[512,2048]{0,1:T(8,128)(2,1)}, u32[]{:S(2)}, u32[]{:S(2)}) collective-permute-start(bf16[512,2048]{0,1:T(8,128)(2,1)S(1)} %bitcast.131), channel_id=1, source_target_pairs={{8,0},{24,8},{16,24},{0,16},{9,1},{25,9},{17,25},{1,17},{10,2},{26... | collective-permute-start | bytes 6291464 | tf_op jit(solution)/shard_map/ppermute | solution.py:190
  364.9 223.2 %reduce-scatter.7.cloned.1.call-start = ((), (), s32[]{:S(2)}) async-start(), calls=%async_computation.17 | async-start | bytes 9437184 | tf_op jit(solution)/shard_map/reduce_scatter | solution.py:299
  415.7 256.1 %reduce-scatter.9.cloned.1.call-start = ((), (), s32[]{:S(2)}) async-start(), calls=%async_computation.18 | async-start | bytes 7077888 | tf_op jit(solution)/shard_map/reduce_scatter | solution.py:299
  534.6 62.3 %collective-permute-start.11 = (bf16[512,2048]{0,1:T(8,128)(2,1)}, bf16[512,2048]{0,1:T(8,128)(2,1)}, u32[]{:S(2)}, u32[]{:S(2)}) collective-permute-start(bf16[512,2048]{0,1:T(8,128)(2,1)} %pad_maximum_fusion.1), channel_id=1, source_target_pairs={{8,0},{24,8},{16,24},{0,16},{9,1},{25,9},{17,25},{1,17},{10,2},{26... | collective-permute-start | bytes 6291464 | tf_op jit(solution)/shard_map/ppermute | solution.py:190
  537.6 59.3 %collective-permute-start.10 = (bf16[512,2048]{0,1:T(8,128)(2,1)}, bf16[512,2048]{0,1:T(8,128)(2,1)}, u32[]{:S(2)}, u32[]{:S(2)}) collective-permute-start(bf16[512,2048]{0,1:T(8,128)(2,1)} %pad_maximum_fusion), channel_id=1, source_target_pairs={{0,8},{8,24},{24,16},{16,0},{1,9},{9,25},{25,17},{17,1},{2,10},{10... | collective-permute-start | bytes 6291464 | tf_op jit(solution)/shard_map/ppermute | solution.py:189
  602.0 59.4 %all-to-all-start.5 = ((bf16[8,512,256]{1,2,0:T(8,128)(2,1)}), bf16[8,512,256]{1,2,0:T(8,128)(2,1)}, u32[]{:S(2)}, u32[]{:S(2)}) async-start(bf16[8,512,256]{1,2,0:T(8,128)(2,1)} %bitcast.26), calls=%async_computation.6 | async-start | bytes 4194304 | tf_op jit(solution)/shard_map/all_to_all | solution.py:198
  620.9 44.6 %collective-permute-start.18 = (bf16[512,2048]{1,0:T(8,128)(2,1)}, bf16[512,2048]{1,0:T(8,128)(2,1)}, u32[]{:S(2)}, u32[]{:S(2)}) collective-permute-start(bf16[512,2048]{1,0:T(8,128)(2,1)} %pad_maximum_fusion.3), channel_id=1, source_target_pairs={{8,0},{24,8},{16,24},{0,16},{9,1},{25,9},{17,25},{1,17},{10,2},{26... | collective-permute-start | bytes 6291464 | tf_op jit(solution)/shard_map/ppermute | solution.py:190
  622.9 42.6 %collective-permute-start.16 = (bf16[512,2048]{1,0:T(8,128)(2,1)}, bf16[512,2048]{1,0:T(8,128)(2,1)}, u32[]{:S(2)}, u32[]{:S(2)}) collective-permute-start(bf16[512,2048]{1,0:T(8,128)(2,1)} %pad_maximum_fusion.2), channel_id=1, source_target_pairs={{0,8},{8,24},{24,16},{16,0},{1,9},{9,25},{25,17},{17,1},{2,10},{10... | collective-permute-start | bytes 6291464 | tf_op jit(solution)/shard_map/ppermute | solution.py:189
  677.4 57.5 %all-to-all-start.7 = ((bf16[8,512,256]{2,1,0:T(8,128)(2,1)}), bf16[8,512,256]{2,1,0:T(8,128)(2,1)}, u32[]{:S(2)}, u32[]{:S(2)}) async-start(bf16[8,512,256]{2,1,0:T(8,128)(2,1)} %bitcast.129), calls=%async_computation.10 | async-start | bytes 4194304 | tf_op jit(solution)/shard_map/all_to_all | solution.py:198
  685.8 92.6 %reduce-scatter.11.cloned.1.call-start = ((), (), s32[]{:S(2)}) async-start(), calls=%async_computation.19 | async-start | bytes 2359296 | tf_op jit(solution)/shard_map/reduce_scatter | solution.py:299
  703.0 32.3 %collective-permute-start.12 = (bf16[2,2,256,256]{3,2,1,0:T(8,128)(2,1)}, bf16[2,2,256,256]{3,2,1,0:T(8,128)(2,1)}, u32[]{:S(2)}, u32[]{:S(2)}) collective-permute-start(bf16[2,2,256,256]{3,2,1,0:T(8,128)(2,1)} %bitcast.143), channel_id=1, source_target_pairs={{0,8},{8,0},{16,24},{24,16},{1,9},{9,1},{17,25},{25,17},{2,10},{10... | collective-permute-start | bytes 1572872 | tf_op jit(solution)/shard_map/ppermute | solution.py:215
  703.6 32.7 %collective-permute-start.13 = (bf16[2,2,256,256]{3,2,1,0:T(8,128)(2,1)}, bf16[2,2,256,256]{3,2,1,0:T(8,128)(2,1)}, u32[]{:S(2)}, u32[]{:S(2)}) collective-permute-start(bf16[2,2,256,256]{3,2,1,0:T(8,128)(2,1)} %bitcast.142), channel_id=1, source_target_pairs={{0,16},{8,24},{16,0},{24,8},{1,17},{9,25},{17,1},{25,9},{2,18},{10... | collective-permute-start | bytes 1572872 | tf_op jit(solution)/shard_map/ppermute | solution.py:215
  704.1 33.4 %collective-permute-start.14 = (bf16[2,2,256,256]{3,2,1,0:T(8,128)(2,1)}, bf16[2,2,256,256]{3,2,1,0:T(8,128)(2,1)S(1)}, u32[]{:S(2)}, u32[]{:S(2)}) collective-permute-start(bf16[2,2,256,256]{3,2,1,0:T(8,128)(2,1)} %bitcast.141), channel_id=1, source_target_pairs={{0,24},{8,16},{16,8},{24,0},{1,25},{9,17},{17,9},{25,1},{2,26},{10... | collective-permute-start | bytes 1572872 | tf_op jit(solution)/shard_map/ppermute | solution.py:215
  744.3 29.4 %all-to-all-start.8 = ((bf16[4,2,2,256,256]{4,3,1,2,0:T(8,128)(2,1)}), bf16[4,2,2,256,256]{4,3,1,2,0:T(8,128)(2,1)}, u32[]{:S(2)}, u32[]{:S(2)}) async-start(bf16[4,2,2,256,256]{4,3,1,2,0:T(8,128)(2,1)} %copy.105), calls=%async_computation.11 | async-start | bytes 4194304 | tf_op jit(solution)/shard_map/all_to_all | solution.py:206
  (44 other events, 1353.5 us)
Sparse Core Ops, SparseCore 0:
  9.6 91.6 all-gather.3
  138.0 122.7 all-gather.5
  263.0 82.8 all-gather.7
  365.0 92.2 reduce-scatter.4
  459.4 87.9 reduce-scatter.6
  549.6 70.7 reduce-scatter.8
  735.1 34.9 reduce-scatter.10

commit v7 on v6

--- a/solution.py
+++ b/solution.py
@@ -293,13 +293,14 @@
     activated = (expand_pre * phi_sum).astype(BF)
     slope = (phi_sum + expand_pre * density).astype(BF)
     activated, slope = lax.optimization_barrier((activated, slope))
-    cot_seq = ring_gather(cot_part, activated)
+    branch_ff = mm(activated, reduce_w).astype(BF)
+    cot_seq = ring_gather(cot_part, branch_ff)
 
     def scatter_weight(grad):
         return lax.psum_scatter(grad, "col", scatter_dimension=0, tiled=True).astype(F32)
 
-    cot_seq, attend_in, *tables = lax.optimization_barrier(
-        (cot_seq, attend_in) + rotary_tables()
+    cot_seq, branch_ff, attend_in, *tables = lax.optimization_barrier(
+        (cot_seq, branch_ff, attend_in) + rotary_tables()
     )
     reduce_dot = contract_first(cot_seq, activated).astype(BF)
     reduce_grad = scatter_weight(reduce_dot).T
@@ -309,7 +310,6 @@
     expand_dot = contract_first(expand_in, grad_pre).astype(BF)
     expand_grad = scatter_weight(expand_dot)
 
-    branch_ff = mm(after(activated, expand_dot), reduce_w).astype(BF)
     merged_pre = mm(after(attend_in, expand_dot), merged_w) + merged_bias
     grad_mix = mm(after(cot_seq, expand_dot), output_wt).astype(BF)
     mix, grad_merged = attention(
@@ -337,7 +337,6 @@
         ]
     )
     grad_hat = (grad_first * gains[0] + grad_second * gains[2]).astype(BF)
-    grad_hat = after(grad_hat, expand_grad)
     halves = ring_open(grad_hat)
     merged_b = jnp.sum(grad_merged.astype(F32), axis=0)
     shift_b = jnp.sum(cotangent.astype(F32), axis=(0, 1))
@@ -353,6 +352,7 @@
     spread_sums = lax.all_to_all(
         after(sums, branch), "col", split_axis=0, concat_axis=0, tiled=True
     )
+    halves = lax.optimization_barrier(halves + (expand_grad,))[:2]
     grad_hat = ring_close(grad_hat, halves)
     sums = jnp.sum(spread_sums.reshape(cols, -1), axis=0)
     merged_b = sums[4 * width : 4 * width + merged_cols]

time: 797 us -> 797 us (level)
  other arithmetic: 72.1 us -> 89.7 us
  local copies, waits for them, and re-layouts: 79.8 us -> 64.8 us
    ppermute x8, waiting for transfers between devices: 2.77 us -> 57.3 us  [body(): down = lambda v: lax.ppermute(v, 'row', behind)]
    all_to_all x3, waiting for transfers between devices: 94.6 us -> 51.7 us  [col_swap(): return lax.all_to_all(b, 'col', split_axis=0, concat_axis=0, tiled=True)]
    unnamed x86 -> x74, local copies, waits for them, and re-layouts: 33.7 us -> 21.9 us
    ppermute x8, waiting for transfers between devices: 75.3 us -> 67 us  [body(): up = lambda v: lax.ppermute(v, 'row', ahead)]
  transfers between devices with their start and end apart: 33 -> 33, of which waited for: 10 -> 13; matrix products, arithmetic and copies ran while one was open for 46% -> 46% of each run, Pallas kernels for 3% -> 3%
where the time goes in v7:
time: 797 us; the launch traced here: 789 us
  matrix products  227 us (28%)
  waiting for transfers between devices  201 us (25%)
  blocking collectives  125 us (16%)
  other arithmetic  89.7 us (11%)
  local copies, waits for them, and re-layouts  64.8 us (8%)
  starting transfers between devices  45.1 us (6%)
  Pallas kernels  21 us (3%)
  between operations  15 us (2%)
    dot_general x4, matrix products, contract_last(): lax.dot_general(left, right, (((1,), (1,)), ((), ())), preferred_element_...  82.7 us
    dot_general x4, matrix products, mm(): return jnp.dot(left, right, preferred_element_type=F32)  73.2 us
    dot_general x4, matrix products, contract_first(): lax.dot_general(left, right, (((0,), (0,)), ((), ())), preferred_element_...  71.2 us
    ppermute x8, waiting for transfers between devices, body(): up = lambda v: lax.ppermute(v, 'row', ahead)  67 us
    all_to_all x1, blocking collectives, col_swap(): return lax.all_to_all(b, 'col', split_axis=0, concat_axis=0, tiled=True)  57.9 us
    ppermute x8, waiting for transfers between devices, body(): down = lambda v: lax.ppermute(v, 'row', behind)  57.3 us
    all_to_all x2, blocking collectives, row_swap(): b = lax.all_to_all(b, 'row', split_axis=0, concat_axis=0, tiled=True)  55.5 us
    all_to_all x3, waiting for transfers between devices, col_swap(): return lax.all_to_all(b, 'col', split_axis=0, concat_axis=0, tiled=True)  51.7 us
  transfers between devices with their start and end apart: 33, of which 13 were waited for; matrix products, arithmetic and copies ran while one was open for 46% of the time, Pallas kernels for 3%

profile of v7, /device:TPU:0, one launch (start us, length us, event | category | flops | bytes accessed | tf_op | source)
XLA Modules:
  0.0 788.7 jit_solution(11105082172043699838)
XLA Ops:
  8.7 11.9 %all_to_all.45 = f32[8,4,256]{2,1,0:T(4,128)S(1)} all-to-all(f32[8,4,256]{2,1,0:T(4,128)S(1)} %broadcast_in_dim.21), channel_id=1, replica_groups=mesh['row'=4,'col'=8] {'col'}, dimensions={0} | all-to-all | bytes 65536 | tf_op jit(solution)/shard_map/all_to_all | solution.py:265
  22.6 28.8 %all_to_all.46 = bf16[4,2,2,256,256]{4,3,1,2,0:T(8,128)(2,1)S(1)} all-to-all(bf16[4,2,2,256,256]{4,3,1,2,0:T(8,128)(2,1)S(1)} %copy.98), channel_id=1, replica_groups=mesh['row'=4,'col'=8] {'row'}, dimensions={0} | all-to-all | bytes 4194304 | tf_op jit(solution)/shard_map/all_to_all | solution.py:194
  51.7 26.7 %all_to_all.47 = bf16[4,2,2,256,256]{4,3,1,2,0:T(8,128)(2,1)S(1)} all-to-all(bf16[4,2,2,256,256]{4,3,1,2,0:T(8,128)(2,1)S(1)} %copy.100), channel_id=1, replica_groups=mesh['row'=4,'col'=8] {'row'}, dimensions={0} | all-to-all | bytes 4194304 | tf_op jit(solution)/shard_map/all_to_all | solution.py:194
  79.9 57.9 %all_to_all.48 = bf16[8,512,256]{2,1,0:T(8,128)(2,1)} all-to-all(bf16[8,512,256]{2,1,0:T(8,128)(2,1)S(1)} %bitcast.141), channel_id=1, replica_groups=mesh['row'=4,'col'=8] {'col'}, dimensions={0} | all-to-all | bytes 4194304 | tf_op jit(solution)/shard_map/all_to_all | solution.py:198
  149.4 38.1 %collective-permute-done.3 = bf16[512,2048]{1,0:T(8,128)(2,1)} collective-permute-done((bf16[512,2048]{1,0:T(8,128)(2,1)S(1)}, bf16[512,2048]{1,0:T(8,128)(2,1)}, u32[]{:S(2)}, u32[]{:S(2)}) %collective-permute-start.3) | collective-permute-done | bytes 2097184 | tf_op jit(solution)/shard_map/ppermute | solution.py:189
  202.0 12.4 %collective-permute-done.4 = bf16[256,2048]{1,0:T(8,128)(2,1)} collective-permute-done((bf16[256,2048]{1,0:T(8,128)(2,1)}, bf16[256,2048]{1,0:T(8,128)(2,1)}, u32[]{:S(2)}, u32[]{:S(2)}) %collective-permute-start.4) | collective-permute-done | bytes 1048608 | tf_op jit(solution)/shard_map/ppermute | solution.py:189
  226.6 23.9 %all-to-all-done.4 = bf16[8,512,256]{2,1,0:T(8,128)(2,1)} async-done(((bf16[8,512,256]{2,1,0:T(8,128)(2,1)}), bf16[8,512,256]{2,1,0:T(8,128)(2,1)}, u32[]{:S(2)}, u32[]{:S(2)}) %all-to-all-start.4) | async-done | bytes 2097184 | tf_op jit(solution)/shard_map/all_to_all | solution.py:198
  256.0 21.8 %convolution_add_fusion.1 = f32[2048,2048]{1,0:T(8,128)S(1)} fusion(bf16[2048,2048]{1,0:T(8,128)(2,1)} %all-gather.4.cloned.1.call-done, f32[2048]{0:T(1024)S(1)} %copy-done.25, bf16[2048,2048]{1,0:T(8,128)(2,1)} %copy-done, f32[2048]{0:T(1024)S(1)} %bitcast.157, f32[2048]{0:T(1024)S(1)} %bitcast.154, f32[2048]{0:T(1024)S(1)} %add_rsqrt_fusion, ...), kind=kOutput, calls=%fused_computation.29 | convolution fusion | flops 17209229312 | bytes 33595392 | tf_op jit(solution)/shard_map/dot_general | solution.py:24
  286.5 23.6 %convolution_convert_fusion.2 = bf16[2048,2048]{1,0:T(8,128)(2,1)} fusion(bf16[2048,2048]{1,0:T(8,128)(2,1)} %get-tuple-element.52, bf16[2048,2048]{1,0:T(8,128)(2,1)} %all-gather.6.cloned.1.call-done), kind=kOutput, calls=%fused_computation.32 | convolution fusion | flops 17184063488 | bytes 25165824 | tf_op jit(solution)/shard_map/dot_general | solution.py:24
  325.9 12.4 %collective-permute-done.6 = bf16[256,2048]{0,1:T(8,128)(2,1)S(1)} collective-permute-done((bf16[256,2048]{0,1:T(8,128)(2,1)S(1)}, bf16[256,2048]{0,1:T(8,128)(2,1)S(1)}, u32[]{:S(2)}, u32[]{:S(2)}) %collective-permute-start.6) | collective-permute-done | bytes 1048608 | tf_op jit(solution)/shard_map/ppermute | solution.py:189
  343.9 19.5 %convolution_convert_fusion.1 = bf16[2048,2048]{1,0:T(8,128)(2,1)} fusion(bf16[2048,2048]{0,1:T(8,128)(2,1)S(1)} %constant_dynamic-update-slice_fusion.5, bf16[2048,2048]{1,0:T(8,128)(2,1)S(1)} %bitcast.144), kind=kOutput, calls=%fused_computation.31 | convolution fusion | flops 17184063488 | bytes 25165824 | tf_op jit(solution)/shard_map/dot_general | solution.py:32
  363.8 25.2 %convert_reduce_fusion.1 = (f32[2048]{0:T(1024)}, bf16[2048,2048]{1,0:T(8,128)(2,1)S(1)}) fusion(bf16[2048,2048]{1,0:T(8,128)(2,1)} %get-tuple-element.59, bf16[2048,2048]{0,1:T(8,128)(2,1)} %copy-done.7, bf16[2048,2048]{1,0:T(8,128)(2,1)} %all-gather.6.cloned.1.call-done), kind=kOutput, calls=%fused_computation.21 | convolution fusion | flops 17200838656 | bytes 33562624 | tf_op jit(solution)/shard_map/dot_general | solution.py:28
  392.4 22.6 %convolution_convert_fusion = bf16[2048,2048]{1,0:T(8,128)(2,1)} fusion(bf16[2048,2048]{1,0:T(8,128)(2,1)S(1)} %get-tuple-element.73, bf16[2048,2048]{1,0:T(8,128)(2,1)} %copy-done, f32[2048]{0:T(1024)S(1)} %bitcast.158, f32[2048]{0:T(1024)S(1)} %bitcast.155, f32[2048]{0:T(1024)S(1)} %add_rsqrt_fusion, f32[2048]{0:T(1024)S(1)} %broadcast_multiply_fusion), kind=kOutput, calls=%fused_computation.30 | convolution fusion | flops 17209229312 | bytes 25198592 | tf_op jit(solution)/shard_map/dot_general | solution.py:32
  418.7 10.1 %convolution_convert_fusion.5 = bf16[2048,512]{1,0:T(8,128)(2,1)} fusion(bf16[2048,2048]{0,1:T(8,128)(2,1)} %copy-done.7, bf16[2048,2048]{1,0:T(8,128)(2,1)} %all-gather.8.cloned.1.call-done), kind=kOutput, calls=%fused_computation.53 | convolution fusion | flops 4296015872 | bytes 12582912 | tf_op jit(solution)/shard_map/dot_general | solution.py:24
  428.9 17.7 %convolution_add_fusion = f32[2048,1536]{1,0:T(8,128)} fusion(bf16[2048,2048]{1,0:T(8,128)(2,1)} %fusion.9, f32[1536]{0:T(1024)S(1)} %copy-done.26, bf16[2048,2048]{1,0:T(8,128)(2,1)S(1)} %copy-done.24), kind=kOutput, calls=%fused_computation.28 | convolution fusion | flops 12888047616 | bytes 27271168 | tf_op jit(solution)/shard_map/dot_general | solution.py:24
  446.5 21.0 %attention.1 = (bf16[4,2,256,512]{3,2,1,0:T(8,128)(2,1)}, bf16[4,2,256,1536]{3,2,1,0:T(8,128)(2,1)}) custom-call(s32[4]{0:T(128)} %and_select_fusion.slot_ref, s32[4]{0:T(128)} %reshape.176.starts_ref, f32[4,2,256,1536]{3,2,1,0:T(8,128)} %bitcast.163, bf16[4,2,256,512]{3,2,1,0:T(8,128)(2,1)} %bitcast.166, f32[1024,128]{1,0:T(8,128)} %get-tuple-element.63.cos_ref, ...), custom_call_target="tpu_custom_call" | custom-call | flops 16106127360 | bytes 23068672 | tf_op jit(solution)/shard_map/attention/pallas_call | solution.py:124
  490.5 19.3 %convolution_convert_fusion.3 = bf16[2048,1536]{1,0:T(8,128)(2,1)} fusion(bf16[2048,2048]{1,0:T(8,128)(2,1)} %fusion.9, bf16[2048,1536]{1,0:T(8,128)(2,1)} %bitcast.145), kind=kOutput, calls=%fused_computation.33 | convolution fusion | flops 12888047616 | bytes 20971520 | tf_op jit(solution)/shard_map/dot_general | solution.py:32
  517.6 24.8 %fusion.38 = f32[2048,2048]{1,0:T(8,128)} fusion(bf16[2048,2048]{1,0:T(8,128)(2,1)} %copy-done.28, bf16[2048,2048]{1,0:T(8,128)(2,1)} %all-gather.4.cloned.1.call-done), kind=kOutput, calls=%fused_computation.123 | convolution fusion | flops 17179869184 | bytes 33554432 | tf_op jit(solution)/shard_map/dot_general | solution.py:28
  542.4 25.7 %fusion.10 = (f32[2048]{0:T(1024)S(1)}, f32[2048]{0:T(1024)S(1)}, f32[2048]{0:T(1024)S(1)}, f32[2048]{0:T(1024)S(1)}, bf16[2048,2048]{1,0:T(8,128)(2,1)}) fusion(bf16[2048,2048]{1,0:T(8,128)(2,1)} %copy-done, f32[2048]{0:T(1024)S(1)} %copy-done.11, f32[2048]{0:T(1024)S(1)} %copy-done.9, f32[2048,2048]{1,0:T(8,128)} %fusion.38, f32[2048]{0:T(1024)S(1)} %bitcast.156, ...), kind=kOutput, calls=%fused_computation.13 | convolution fusion | flops 12939419648 | bytes 46202880 | tf_op jit(solution)/shard_map/dot_general | solution.py:28
  577.0 16.3 %collective-permute-done.16 = bf16[256,2048]{1,0:T(8,128)(2,1)S(1)} collective-permute-done((bf16[256,2048]{1,0:T(8,128)(2,1)}, bf16[256,2048]{1,0:T(8,128)(2,1)S(1)}, u32[]{:S(2)}, u32[]{:S(2)}) %collective-permute-start.16) | collective-permute-done | bytes 1048608 | tf_op jit(solution)/shard_map/ppermute | solution.py:190
  622.1 35.4 %collective-permute-done.18 = bf16[512,2048]{1,0:T(8,128)(2,1)} collective-permute-done((bf16[512,2048]{1,0:T(8,128)(2,1)}, bf16[512,2048]{1,0:T(8,128)(2,1)}, u32[]{:S(2)}, u32[]{:S(2)}) %collective-permute-start.18) | collective-permute-done | bytes 2097184 | tf_op jit(solution)/shard_map/ppermute | solution.py:190
  697.9 9.9 %convolution_convert_fusion.4 = bf16[2048,512]{1,0:T(8,128)(2,1)} fusion(bf16[2048,2048]{0,1:T(8,128)(2,1)} %copy-done.7, bf16[2048,512]{1,0:T(8,128)(2,1)} %bitcast.165), kind=kOutput, calls=%fused_computation.52 | convolution fusion | flops 4296015872 | bytes 12582912 | tf_op jit(solution)/shard_map/dot_general | solution.py:32
  707.8 27.9 %all-to-all-done.7 = bf16[8,512,256]{2,1,0:T(8,128)(2,1)} async-done(((bf16[8,512,256]{2,1,0:T(8,128)(2,1)}), bf16[8,512,256]{2,1,0:T(8,128)(2,1)}, u32[]{:S(2)}, u32[]{:S(2)}) %all-to-all-start.7) | async-done | bytes 2097184 | tf_op jit(solution)/shard_map/all_to_all | solution.py:198
  754.3 20.1 %all-to-all-done.8 = bf16[4,2,2,256,256]{4,3,1,2,0:T(8,128)(2,1)} async-done(((bf16[4,2,2,256,256]{4,3,1,2,0:T(8,128)(2,1)}), bf16[4,2,2,256,256]{4,3,1,2,0:T(8,128)(2,1)}, u32[]{:S(2)}, u32[]{:S(2)}) %all-to-all-start.8) | async-done | bytes 2097184 | tf_op jit(solution)/shard_map/all_to_all | solution.py:206
  (229 shorter events, 220.8 us)
Async XLA Ops:
  7.2 248.7 %all-gather.4.cloned.1.call-start = ((), (), s32[]{:S(2)}) async-start(), calls=%async_computation.13 | async-start | bytes 9437184 | tf_op jit(solution)/shard_map/all_gather | solution.py:272
  7.9 278.6 %all-gather.6.cloned.1.call-start = ((), (), s32[]{:S(2)}) async-start(), calls=%async_computation.14 | async-start | bytes 9437184 | tf_op jit(solution)/shard_map/all_gather | solution.py:276
  139.7 47.8 %collective-permute-start.3 = (bf16[512,2048]{1,0:T(8,128)(2,1)S(1)}, bf16[512,2048]{1,0:T(8,128)(2,1)}, u32[]{:S(2)}, u32[]{:S(2)}) collective-permute-start(bf16[512,2048]{1,0:T(8,128)(2,1)S(1)} %bitcast.127), channel_id=1, source_target_pairs={{0,8},{8,24},{24,16},{16,0},{1,9},{9,25},{25,17},{17,1},{2,10},{10... | collective-permute-start | bytes 6291464 | tf_op jit(solution)/shard_map/ppermute | solution.py:189
  141.3 53.6 %collective-permute-start.2 = (bf16[512,2048]{1,0:T(8,128)(2,1)S(1)}, bf16[512,2048]{1,0:T(8,128)(2,1)}, u32[]{:S(2)}, u32[]{:S(2)}) collective-permute-start(bf16[512,2048]{1,0:T(8,128)(2,1)S(1)} %bitcast.128), channel_id=1, source_target_pairs={{8,0},{24,8},{16,24},{0,16},{9,1},{25,9},{17,25},{1,17},{10,2},{26... | collective-permute-start | bytes 6291464 | tf_op jit(solution)/shard_map/ppermute | solution.py:190
  145.0 105.5 %all-to-all-start.4 = ((bf16[8,512,256]{2,1,0:T(8,128)(2,1)}), bf16[8,512,256]{2,1,0:T(8,128)(2,1)}, u32[]{:S(2)}, u32[]{:S(2)}) async-start(bf16[8,512,256]{2,1,0:T(8,128)(2,1)} %bitcast.136), calls=%async_computation.4 | async-start | bytes 4194304 | tf_op jit(solution)/shard_map/all_to_all | solution.py:198
  149.4 269.4 %all-gather.8.cloned.1.call-start = ((), (), s32[]{:S(2)}) async-start(), calls=%async_computation.15 | async-start | bytes 9437184 | tf_op jit(solution)/shard_map/all_gather | solution.py:289
  189.8 24.6 %collective-permute-start.4 = (bf16[256,2048]{1,0:T(8,128)(2,1)}, bf16[256,2048]{1,0:T(8,128)(2,1)}, u32[]{:S(2)}, u32[]{:S(2)}) collective-permute-start(bf16[256,2048]{1,0:T(8,128)(2,1)} %slice.196), channel_id=1, source_target_pairs={{0,8},{8,24},{24,16},{16,0},{1,9},{9,25},{25,17},{17,1},{2,10},{10... | collective-permute-start | bytes 3145736 | tf_op jit(solution)/shard_map/ppermute | solution.py:189
  253.6 56.5 %collective-permute-start.1 = (bf16[512,2048]{0,1:T(8,128)(2,1)S(1)}, bf16[512,2048]{0,1:T(8,128)(2,1)}, u32[]{:S(2)}, u32[]{:S(2)}) collective-permute-start(bf16[512,2048]{0,1:T(8,128)(2,1)S(1)} %bitcast.138), channel_id=1, source_target_pairs={{0,8},{8,24},{24,16},{16,0},{1,9},{9,25},{25,17},{17,1},{2,10},{10... | collective-permute-start | bytes 6291464 | tf_op jit(solution)/shard_map/ppermute | solution.py:189
  255.1 55.0 %collective-permute-start = (bf16[512,2048]{0,1:T(8,128)(2,1)S(1)}, bf16[512,2048]{0,1:T(8,128)(2,1)}, u32[]{:S(2)}, u32[]{:S(2)}) collective-permute-start(bf16[512,2048]{0,1:T(8,128)(2,1)S(1)} %bitcast.139), channel_id=1, source_target_pairs={{8,0},{24,8},{16,24},{0,16},{9,1},{25,9},{17,25},{1,17},{10,2},{26... | collective-permute-start | bytes 6291464 | tf_op jit(solution)/shard_map/ppermute | solution.py:190
  255.7 231.9 %reduce-scatter.5.cloned.1.call-start = ((), (), s32[]{:S(2)}) async-start(), calls=%async_computation.16 | async-start | bytes 9437184 | tf_op jit(solution)/shard_map/reduce_scatter | solution.py:300
  312.7 25.8 %collective-permute-start.7 = (bf16[256,2048]{0,1:T(8,128)(2,1)S(1)}, bf16[256,2048]{0,1:T(8,128)(2,1)S(1)}, u32[]{:S(2)}, u32[]{:S(2)}) collective-permute-start(bf16[256,2048]{0,1:T(8,128)(2,1)S(1)} %slice.162), channel_id=1, source_target_pairs={{8,0},{24,8},{16,24},{0,16},{9,1},{25,9},{17,25},{1,17},{10,2},{26... | collective-permute-start | bytes 3145736 | tf_op jit(solution)/shard_map/ppermute | solution.py:190
  363.4 210.8 %reduce-scatter.7.cloned.1.call-start = ((), (), s32[]{:S(2)}) async-start(), calls=%async_computation.17 | async-start | bytes 9437184 | tf_op jit(solution)/shard_map/reduce_scatter | solution.py:300
  415.0 260.8 %reduce-scatter.9.cloned.1.call-start = ((), (), s32[]{:S(2)}) async-start(), calls=%async_computation.18 | async-start | bytes 7077888 | tf_op jit(solution)/shard_map/reduce_scatter | solution.py:300
  514.0 83.4 %collective-permute-start.11 = (bf16[512,2048]{1,0:T(8,128)(2,1)}, bf16[512,2048]{1,0:T(8,128)(2,1)}, u32[]{:S(2)}, u32[]{:S(2)}) collective-permute-start(bf16[512,2048]{1,0:T(8,128)(2,1)} %pad_maximum_fusion.1), channel_id=1, source_target_pairs={{8,0},{24,8},{16,24},{0,16},{9,1},{25,9},{17,25},{1,17},{10,2},{26... | collective-permute-start | bytes 6291464 | tf_op jit(solution)/shard_map/ppermute | solution.py:190
  517.0 80.4 %collective-permute-start.10 = (bf16[512,2048]{1,0:T(8,128)(2,1)}, bf16[512,2048]{1,0:T(8,128)(2,1)}, u32[]{:S(2)}, u32[]{:S(2)}) collective-permute-start(bf16[512,2048]{1,0:T(8,128)(2,1)} %pad_maximum_fusion), channel_id=1, source_target_pairs={{0,8},{8,24},{24,16},{16,0},{1,9},{9,25},{25,17},{17,1},{2,10},{10... | collective-permute-start | bytes 6291464 | tf_op jit(solution)/shard_map/ppermute | solution.py:189
  603.1 63.3 %all-to-all-start.5 = ((bf16[8,512,256]{2,1,0:T(8,128)(2,1)}), bf16[8,512,256]{2,1,0:T(8,128)(2,1)}, u32[]{:S(2)}, u32[]{:S(2)}) async-start(bf16[8,512,256]{2,1,0:T(8,128)(2,1)} %bitcast.126), calls=%async_computation.6 | async-start | bytes 4194304 | tf_op jit(solution)/shard_map/all_to_all | solution.py:198
  609.2 48.3 %collective-permute-start.18 = (bf16[512,2048]{1,0:T(8,128)(2,1)}, bf16[512,2048]{1,0:T(8,128)(2,1)}, u32[]{:S(2)}, u32[]{:S(2)}) collective-permute-start(bf16[512,2048]{1,0:T(8,128)(2,1)} %pad_maximum_fusion.3), channel_id=1, source_target_pairs={{8,0},{24,8},{16,24},{0,16},{9,1},{25,9},{17,25},{1,17},{10,2},{26... | collective-permute-start | bytes 6291464 | tf_op jit(solution)/shard_map/ppermute | solution.py:190
  613.4 48.0 %collective-permute-start.17 = (bf16[512,2048]{1,0:T(8,128)(2,1)}, bf16[512,2048]{1,0:T(8,128)(2,1)}, u32[]{:S(2)}, u32[]{:S(2)}) collective-permute-start(bf16[512,2048]{1,0:T(8,128)(2,1)} %pad_maximum_fusion.2), channel_id=1, source_target_pairs={{0,8},{8,24},{24,16},{16,0},{1,9},{9,25},{25,17},{17,1},{2,10},{10... | collective-permute-start | bytes 6291464 | tf_op jit(solution)/shard_map/ppermute | solution.py:189
  682.1 53.6 %all-to-all-start.7 = ((bf16[8,512,256]{2,1,0:T(8,128)(2,1)}), bf16[8,512,256]{2,1,0:T(8,128)(2,1)}, u32[]{:S(2)}, u32[]{:S(2)}) async-start(bf16[8,512,256]{2,1,0:T(8,128)(2,1)} %bitcast.137), calls=%async_computation.10 | async-start | bytes 4194304 | tf_op jit(solution)/shard_map/all_to_all | solution.py:198
  686.5 92.6 %reduce-scatter.11.cloned.1.call-start = ((), (), s32[]{:S(2)}) async-start(), calls=%async_computation.19 | async-start | bytes 2359296 | tf_op jit(solution)/shard_map/reduce_scatter | solution.py:300
  694.4 43.7 %collective-permute-start.14 = (bf16[2,2,256,256]{3,2,0,1:T(8,128)(2,1)}, bf16[2,2,256,256]{3,2,0,1:T(8,128)(2,1)S(1)}, u32[]{:S(2)}, u32[]{:S(2)}) collective-permute-start(bf16[2,2,256,256]{3,2,0,1:T(8,128)(2,1)} %get-tuple-element.190), channel_id=1, source_target_pairs={{0,24},{8,16},{16,8},{24,0},{1,25},{9,17},{17,9},{25,1},{2,26},{10... | collective-permute-start | bytes 1572872 | tf_op jit(solution)/shard_map/ppermute | solution.py:215
  695.7 41.3 %collective-permute-start.13 = (bf16[2,2,256,256]{3,2,0,1:T(8,128)(2,1)}, bf16[2,2,256,256]{3,2,0,1:T(8,128)(2,1)}, u32[]{:S(2)}, u32[]{:S(2)}) collective-permute-start(bf16[2,2,256,256]{3,2,0,1:T(8,128)(2,1)} %get-tuple-element.191), channel_id=1, source_target_pairs={{0,16},{8,24},{16,0},{24,8},{1,17},{9,25},{17,1},{25,9},{2,18},{10... | collective-permute-start | bytes 1572872 | tf_op jit(solution)/shard_map/ppermute | solution.py:215
  696.4 39.6 %collective-permute-start.12 = (bf16[2,2,256,256]{3,2,0,1:T(8,128)(2,1)}, bf16[2,2,256,256]{3,2,0,1:T(8,128)(2,1)}, u32[]{:S(2)}, u32[]{:S(2)}) collective-permute-start(bf16[2,2,256,256]{3,2,0,1:T(8,128)(2,1)} %get-tuple-element.192), channel_id=1, source_target_pairs={{0,8},{8,0},{16,24},{24,16},{1,9},{9,1},{17,25},{25,17},{2,10},{10... | collective-permute-start | bytes 1572872 | tf_op jit(solution)/shard_map/ppermute | solution.py:215
  745.1 29.2 %all-to-all-start.8 = ((bf16[4,2,2,256,256]{4,3,1,2,0:T(8,128)(2,1)}), bf16[4,2,2,256,256]{4,3,1,2,0:T(8,128)(2,1)}, u32[]{:S(2)}, u32[]{:S(2)}) async-start(bf16[4,2,2,256,256]{4,3,1,2,0:T(8,128)(2,1)} %copy.114), calls=%async_computation.11 | async-start | bytes 4194304 | tf_op jit(solution)/shard_map/all_to_all | solution.py:206
  (40 other events, 1251.5 us)
Sparse Core Ops, SparseCore 0:
  9.6 91.6 all-gather.3
  138.0 125.3 all-gather.5
  265.6 81.9 all-gather.7
  363.5 87.1 reduce-scatter.4
  452.8 87.9 reduce-scatter.6
  543.0 68.1 reduce-scatter.8
  735.8 33.3 reduce-scatter.10

commit v8 on v7

--- a/solution.py
+++ b/solution.py
@@ -297,13 +297,13 @@
     cot_seq = ring_gather(cot_part, branch_ff)
 
     def scatter_weight(grad):
-        return lax.psum_scatter(grad, "col", scatter_dimension=0, tiled=True).astype(F32)
+        return lax.psum_scatter(grad, "col", scatter_dimension=0, tiled=True)
 
     cot_seq, branch_ff, attend_in, *tables = lax.optimization_barrier(
         (cot_seq, branch_ff, attend_in) + rotary_tables()
     )
     reduce_dot = contract_first(cot_seq, activated).astype(BF)
-    reduce_grad = scatter_weight(reduce_dot).T
+    reduce_grad = scatter_weight(reduce_dot)
     grad_act = contract_last(after(cot_seq, reduce_dot), reduce_w)
     grad_pre = (grad_act * slope.astype(F32)).astype(BF)
     expand_b = jnp.sum(grad_pre.astype(F32), axis=0)
@@ -383,7 +383,7 @@
     norm_part = col_swap(norm_part.reshape(block_rows, cols, width).transpose(1, 0, 2))
     mix_late, cot_late = lax.optimization_barrier((mix, cot_seq, grad_hat, far_tail))[:2]
     output_dot = contract_first(cot_late, mix_late).astype(BF)
-    output_grad = scatter_weight(after(output_dot, norm_part)).T
+    output_grad = scatter_weight(after(output_dot, norm_part))
     input_grad = cotangent.astype(F32) + from_rows(norm_part, result, output_dot).astype(F32)
     norm_sums, shift_b = tail[:4], tail[4]
     return (
@@ -393,13 +393,13 @@
         norm_sums[1],
         norm_sums[2],
         norm_sums[3],
-        merged_grad,
+        merged_grad.astype(F32),
         merged_b,
-        output_grad,
+        output_grad.T.astype(F32),
         shift_b,
-        expand_grad,
+        expand_grad.astype(F32),
         expand_b,
-        reduce_grad,
+        reduce_grad.T.astype(F32),
         shift_b,
     )
 

time: 797 us -> 796 us (level)
    unnamed x74 -> x76, local copies, waits for them, and re-layouts: 21.9 us -> 21.9 us
  transfers between devices with their start and end apart: 33 -> 33, of which waited for: 13 -> 14; matrix products, arithmetic and copies ran while one was open for 46% -> 46% of each run, Pallas kernels for 3% -> 3%
where the time goes in v8:
time: 796 us; the launch traced here: 788 us
  matrix products  227 us (29%)
  waiting for transfers between devices  201 us (25%)
  blocking collectives  125 us (16%)
  other arithmetic  88.2 us (11%)
  local copies, waits for them, and re-layouts  64.9 us (8%)
  starting transfers between devices  45.2 us (6%)
  Pallas kernels  21 us (3%)
  between operations  15 us (2%)
    dot_general x4, matrix products, contract_last(): lax.dot_general(left, right, (((1,), (1,)), ((), ())), preferred_element_...  82.7 us
    dot_general x4, matrix products, mm(): return jnp.dot(left, right, preferred_element_type=F32)  73.2 us
    dot_general x4, matrix products, contract_first(): lax.dot_general(left, right, (((0,), (0,)), ((), ())), preferred_element_...  71.1 us
    ppermute x8, waiting for transfers between devices, body(): up = lambda v: lax.ppermute(v, 'row', ahead)  68 us
    ppermute x8, waiting for transfers between devices, body(): down = lambda v: lax.ppermute(v, 'row', behind)  61.1 us
    all_to_all x1, blocking collectives, col_swap(): return lax.all_to_all(b, 'col', split_axis=0, concat_axis=0, tiled=True)  57.9 us
    all_to_all x2, blocking collectives, row_swap(): b = lax.all_to_all(b, 'row', split_axis=0, concat_axis=0, tiled=True)  55.5 us
    all_to_all x3, waiting for transfers between devices, col_swap(): return lax.all_to_all(b, 'col', split_axis=0, concat_axis=0, tiled=True)  51.8 us
  transfers between devices with their start and end apart: 33, of which 14 were waited for; matrix products, arithmetic and copies ran while one was open for 46% of the time, Pallas kernels for 3%

profile of v8, /device:TPU:0, one launch (start us, length us, event | category | flops | bytes accessed | tf_op | source)
XLA Modules:
  0.0 787.7 jit_solution(3342089233847342390)
XLA Ops:
  8.7 11.9 %all_to_all.45 = f32[8,4,256]{2,1,0:T(4,128)S(1)} all-to-all(f32[8,4,256]{2,1,0:T(4,128)S(1)} %broadcast_in_dim.21), channel_id=1, replica_groups=mesh['row'=4,'col'=8] {'col'}, dimensions={0} | all-to-all | bytes 65536 | tf_op jit(solution)/shard_map/all_to_all | solution.py:265
  22.6 28.8 %all_to_all.46 = bf16[4,2,2,256,256]{4,3,1,2,0:T(8,128)(2,1)S(1)} all-to-all(bf16[4,2,2,256,256]{4,3,1,2,0:T(8,128)(2,1)S(1)} %copy.98), channel_id=1, replica_groups=mesh['row'=4,'col'=8] {'row'}, dimensions={0} | all-to-all | bytes 4194304 | tf_op jit(solution)/shard_map/all_to_all | solution.py:194
  51.7 26.7 %all_to_all.47 = bf16[4,2,2,256,256]{4,3,1,2,0:T(8,128)(2,1)S(1)} all-to-all(bf16[4,2,2,256,256]{4,3,1,2,0:T(8,128)(2,1)S(1)} %copy.100), channel_id=1, replica_groups=mesh['row'=4,'col'=8] {'row'}, dimensions={0} | all-to-all | bytes 4194304 | tf_op jit(solution)/shard_map/all_to_all | solution.py:194
  79.9 57.9 %all_to_all.48 = bf16[8,512,256]{2,1,0:T(8,128)(2,1)} all-to-all(bf16[8,512,256]{2,1,0:T(8,128)(2,1)S(1)} %bitcast.141), channel_id=1, replica_groups=mesh['row'=4,'col'=8] {'col'}, dimensions={0} | all-to-all | bytes 4194304 | tf_op jit(solution)/shard_map/all_to_all | solution.py:198
  149.4 38.1 %collective-permute-done.3 = bf16[512,2048]{1,0:T(8,128)(2,1)} collective-permute-done((bf16[512,2048]{1,0:T(8,128)(2,1)S(1)}, bf16[512,2048]{1,0:T(8,128)(2,1)}, u32[]{:S(2)}, u32[]{:S(2)}) %collective-permute-start.3) | collective-permute-done | bytes 2097184 | tf_op jit(solution)/shard_map/ppermute | solution.py:189
  202.0 12.4 %collective-permute-done.4 = bf16[256,2048]{1,0:T(8,128)(2,1)} collective-permute-done((bf16[256,2048]{1,0:T(8,128)(2,1)}, bf16[256,2048]{1,0:T(8,128)(2,1)}, u32[]{:S(2)}, u32[]{:S(2)}) %collective-permute-start.4) | collective-permute-done | bytes 1048608 | tf_op jit(solution)/shard_map/ppermute | solution.py:189
  226.6 23.9 %all-to-all-done.4 = bf16[8,512,256]{2,1,0:T(8,128)(2,1)} async-done(((bf16[8,512,256]{2,1,0:T(8,128)(2,1)}), bf16[8,512,256]{2,1,0:T(8,128)(2,1)}, u32[]{:S(2)}, u32[]{:S(2)}) %all-to-all-start.4) | async-done | bytes 2097184 | tf_op jit(solution)/shard_map/all_to_all | solution.py:198
  256.0 21.8 %convolution_add_fusion.1 = f32[2048,2048]{1,0:T(8,128)S(1)} fusion(bf16[2048,2048]{1,0:T(8,128)(2,1)} %all-gather.4.cloned.1.call-done, f32[2048]{0:T(1024)S(1)} %copy-done.26, bf16[2048,2048]{1,0:T(8,128)(2,1)} %copy-done, f32[2048]{0:T(1024)S(1)} %bitcast.157, f32[2048]{0:T(1024)S(1)} %bitcast.154, f32[2048]{0:T(1024)S(1)} %add_rsqrt_fusion, ...), kind=kOutput, calls=%fused_computation.29 | convolution fusion | flops 17209229312 | bytes 33595392 | tf_op jit(solution)/shard_map/dot_general | solution.py:24
  286.5 23.6 %convolution_convert_fusion.2 = bf16[2048,2048]{1,0:T(8,128)(2,1)} fusion(bf16[2048,2048]{1,0:T(8,128)(2,1)} %get-tuple-element.52, bf16[2048,2048]{1,0:T(8,128)(2,1)} %all-gather.6.cloned.1.call-done), kind=kOutput, calls=%fused_computation.32 | convolution fusion | flops 17184063488 | bytes 25165824 | tf_op jit(solution)/shard_map/dot_general | solution.py:24
  325.9 12.5 %collective-permute-done.6 = bf16[256,2048]{0,1:T(8,128)(2,1)S(1)} collective-permute-done((bf16[256,2048]{0,1:T(8,128)(2,1)S(1)}, bf16[256,2048]{0,1:T(8,128)(2,1)S(1)}, u32[]{:S(2)}, u32[]{:S(2)}) %collective-permute-start.6) | collective-permute-done | bytes 1048608 | tf_op jit(solution)/shard_map/ppermute | solution.py:189
  343.9 19.5 %convolution_convert_fusion.1 = bf16[2048,2048]{1,0:T(8,128)(2,1)} fusion(bf16[2048,2048]{0,1:T(8,128)(2,1)S(1)} %constant_dynamic-update-slice_fusion.5, bf16[2048,2048]{1,0:T(8,128)(2,1)S(1)} %bitcast.144), kind=kOutput, calls=%fused_computation.31 | convolution fusion | flops 17184063488 | bytes 25165824 | tf_op jit(solution)/shard_map/dot_general | solution.py:32
  363.8 25.2 %convert_reduce_fusion.1 = (f32[2048]{0:T(1024)}, bf16[2048,2048]{1,0:T(8,128)(2,1)S(1)}) fusion(bf16[2048,2048]{1,0:T(8,128)(2,1)} %get-tuple-element.59, bf16[2048,2048]{0,1:T(8,128)(2,1)} %copy-done.8, bf16[2048,2048]{1,0:T(8,128)(2,1)} %all-gather.6.cloned.1.call-done), kind=kOutput, calls=%fused_computation.21 | convolution fusion | flops 17200838656 | bytes 33562624 | tf_op jit(solution)/shard_map/dot_general | solution.py:28
  392.4 22.6 %convolution_convert_fusion = bf16[2048,2048]{1,0:T(8,128)(2,1)} fusion(bf16[2048,2048]{1,0:T(8,128)(2,1)S(1)} %get-tuple-element.73, bf16[2048,2048]{1,0:T(8,128)(2,1)} %copy-done, f32[2048]{0:T(1024)S(1)} %bitcast.158, f32[2048]{0:T(1024)S(1)} %bitcast.155, f32[2048]{0:T(1024)S(1)} %add_rsqrt_fusion, f32[2048]{0:T(1024)S(1)} %broadcast_multiply_fusion), kind=kOutput, calls=%fused_computation.30 | convolution fusion | flops 17209229312 | bytes 25198592 | tf_op jit(solution)/shard_map/dot_general | solution.py:32
  418.7 10.1 %convolution_convert_fusion.5 = bf16[2048,512]{1,0:T(8,128)(2,1)} fusion(bf16[2048,2048]{0,1:T(8,128)(2,1)} %copy-done.8, bf16[2048,2048]{1,0:T(8,128)(2,1)} %all-gather.8.cloned.1.call-done), kind=kOutput, calls=%fused_computation.53 | convolution fusion | flops 4296015872 | bytes 12582912 | tf_op jit(solution)/shard_map/dot_general | solution.py:24
  428.9 17.7 %convolution_add_fusion = f32[2048,1536]{1,0:T(8,128)} fusion(bf16[2048,2048]{1,0:T(8,128)(2,1)} %fusion.9, f32[1536]{0:T(1024)S(1)} %copy-done.27, bf16[2048,2048]{1,0:T(8,128)(2,1)S(1)} %copy-done.25), kind=kOutput, calls=%fused_computation.28 | convolution fusion | flops 12888047616 | bytes 27271168 | tf_op jit(solution)/shard_map/dot_general | solution.py:24
  446.5 21.0 %attention.1 = (bf16[4,2,256,512]{3,2,1,0:T(8,128)(2,1)}, bf16[4,2,256,1536]{3,2,1,0:T(8,128)(2,1)}) custom-call(s32[4]{0:T(128)} %and_select_fusion.slot_ref, s32[4]{0:T(128)} %reshape.176.starts_ref, f32[4,2,256,1536]{3,2,1,0:T(8,128)} %bitcast.163, bf16[4,2,256,512]{3,2,1,0:T(8,128)(2,1)} %bitcast.166, f32[1024,128]{1,0:T(8,128)} %get-tuple-element.63.cos_ref, ...), custom_call_target="tpu_custom_call" | custom-call | flops 16106127360 | bytes 23068672 | tf_op jit(solution)/shard_map/attention/pallas_call | solution.py:124
  487.6 19.2 %convolution_convert_fusion.3 = bf16[2048,1536]{1,0:T(8,128)(2,1)} fusion(bf16[2048,2048]{1,0:T(8,128)(2,1)} %fusion.9, bf16[2048,1536]{1,0:T(8,128)(2,1)} %bitcast.145), kind=kOutput, calls=%fused_computation.33 | convolution fusion | flops 12888047616 | bytes 20971520 | tf_op jit(solution)/shard_map/dot_general | solution.py:32
  517.6 24.8 %fusion.38 = f32[2048,2048]{1,0:T(8,128)} fusion(bf16[2048,2048]{1,0:T(8,128)(2,1)} %copy-done.29, bf16[2048,2048]{1,0:T(8,128)(2,1)} %all-gather.4.cloned.1.call-done), kind=kOutput, calls=%fused_computation.123 | convolution fusion | flops 17179869184 | bytes 33554432 | tf_op jit(solution)/shard_map/dot_general | solution.py:28
  542.4 25.7 %fusion.10 = (f32[2048]{0:T(1024)S(1)}, f32[2048]{0:T(1024)S(1)}, f32[2048]{0:T(1024)S(1)}, f32[2048]{0:T(1024)S(1)}, bf16[2048,2048]{1,0:T(8,128)(2,1)}) fusion(bf16[2048,2048]{1,0:T(8,128)(2,1)} %copy-done, f32[2048]{0:T(1024)S(1)} %copy-done.12, f32[2048]{0:T(1024)S(1)} %copy-done.10, f32[2048,2048]{1,0:T(8,128)} %fusion.38, f32[2048]{0:T(1024)S(1)} %bitcast.156, ...), kind=kOutput, calls=%fused_computation.13 | convolution fusion | flops 12939419648 | bytes 46202880 | tf_op jit(solution)/shard_map/dot_general | solution.py:28
  574.2 18.6 %collective-permute-done.16 = bf16[256,2048]{1,0:T(8,128)(2,1)S(1)} collective-permute-done((bf16[256,2048]{1,0:T(8,128)(2,1)}, bf16[256,2048]{1,0:T(8,128)(2,1)S(1)}, u32[]{:S(2)}, u32[]{:S(2)}) %collective-permute-start.16) | collective-permute-done | bytes 1048608 | tf_op jit(solution)/shard_map/ppermute | solution.py:190
  621.5 35.3 %collective-permute-done.18 = bf16[512,2048]{1,0:T(8,128)(2,1)} collective-permute-done((bf16[512,2048]{1,0:T(8,128)(2,1)}, bf16[512,2048]{1,0:T(8,128)(2,1)}, u32[]{:S(2)}, u32[]{:S(2)}) %collective-permute-start.18) | collective-permute-done | bytes 2097184 | tf_op jit(solution)/shard_map/ppermute | solution.py:190
  696.8 9.9 %convolution_convert_fusion.4 = bf16[2048,512]{1,0:T(8,128)(2,1)} fusion(bf16[2048,2048]{0,1:T(8,128)(2,1)} %copy-done.8, bf16[2048,512]{1,0:T(8,128)(2,1)} %bitcast.165), kind=kOutput, calls=%fused_computation.52 | convolution fusion | flops 4296015872 | bytes 12582912 | tf_op jit(solution)/shard_map/dot_general | solution.py:32
  706.7 27.9 %all-to-all-done.7 = bf16[8,512,256]{2,1,0:T(8,128)(2,1)} async-done(((bf16[8,512,256]{2,1,0:T(8,128)(2,1)}), bf16[8,512,256]{2,1,0:T(8,128)(2,1)}, u32[]{:S(2)}, u32[]{:S(2)}) %all-to-all-start.7) | async-done | bytes 2097184 | tf_op jit(solution)/shard_map/all_to_all | solution.py:198
  760.1 13.3 %all-to-all-done.8 = bf16[4,2,2,256,256]{4,3,1,2,0:T(8,128)(2,1)} async-done(((bf16[4,2,2,256,256]{4,3,1,2,0:T(8,128)(2,1)}), bf16[4,2,2,256,256]{4,3,1,2,0:T(8,128)(2,1)}, u32[]{:S(2)}, u32[]{:S(2)}) %all-to-all-start.8) | async-done | bytes 2097184 | tf_op jit(solution)/shard_map/all_to_all | solution.py:206
  (231 shorter events, 224.4 us)
Async XLA Ops:
  7.2 248.7 %all-gather.4.cloned.1.call-start = ((), (), s32[]{:S(2)}) async-start(), calls=%async_computation.13 | async-start | bytes 9437184 | tf_op jit(solution)/shard_map/all_gather | solution.py:272
  7.9 278.5 %all-gather.6.cloned.1.call-start = ((), (), s32[]{:S(2)}) async-start(), calls=%async_computation.14 | async-start | bytes 9437184 | tf_op jit(solution)/shard_map/all_gather | solution.py:276
  139.7 47.8 %collective-permute-start.3 = (bf16[512,2048]{1,0:T(8,128)(2,1)S(1)}, bf16[512,2048]{1,0:T(8,128)(2,1)}, u32[]{:S(2)}, u32[]{:S(2)}) collective-permute-start(bf16[512,2048]{1,0:T(8,128)(2,1)S(1)} %bitcast.127), channel_id=1, source_target_pairs={{0,8},{8,24},{24,16},{16,0},{1,9},{9,25},{25,17},{17,1},{2,10},{10... | collective-permute-start | bytes 6291464 | tf_op jit(solution)/shard_map/ppermute | solution.py:189
  141.3 53.5 %collective-permute-start.2 = (bf16[512,2048]{1,0:T(8,128)(2,1)S(1)}, bf16[512,2048]{1,0:T(8,128)(2,1)}, u32[]{:S(2)}, u32[]{:S(2)}) collective-permute-start(bf16[512,2048]{1,0:T(8,128)(2,1)S(1)} %bitcast.128), channel_id=1, source_target_pairs={{8,0},{24,8},{16,24},{0,16},{9,1},{25,9},{17,25},{1,17},{10,2},{26... | collective-permute-start | bytes 6291464 | tf_op jit(solution)/shard_map/ppermute | solution.py:190
  145.0 105.5 %all-to-all-start.4 = ((bf16[8,512,256]{2,1,0:T(8,128)(2,1)}), bf16[8,512,256]{2,1,0:T(8,128)(2,1)}, u32[]{:S(2)}, u32[]{:S(2)}) async-start(bf16[8,512,256]{2,1,0:T(8,128)(2,1)} %bitcast.136), calls=%async_computation.4 | async-start | bytes 4194304 | tf_op jit(solution)/shard_map/all_to_all | solution.py:198
  149.4 269.4 %all-gather.8.cloned.1.call-start = ((), (), s32[]{:S(2)}) async-start(), calls=%async_computation.15 | async-start | bytes 9437184 | tf_op jit(solution)/shard_map/all_gather | solution.py:289
  189.8 24.6 %collective-permute-start.4 = (bf16[256,2048]{1,0:T(8,128)(2,1)}, bf16[256,2048]{1,0:T(8,128)(2,1)}, u32[]{:S(2)}, u32[]{:S(2)}) collective-permute-start(bf16[256,2048]{1,0:T(8,128)(2,1)} %slice.196), channel_id=1, source_target_pairs={{0,8},{8,24},{24,16},{16,0},{1,9},{9,25},{25,17},{17,1},{2,10},{10... | collective-permute-start | bytes 3145736 | tf_op jit(solution)/shard_map/ppermute | solution.py:189
  253.6 56.5 %collective-permute-start.1 = (bf16[512,2048]{0,1:T(8,128)(2,1)S(1)}, bf16[512,2048]{0,1:T(8,128)(2,1)}, u32[]{:S(2)}, u32[]{:S(2)}) collective-permute-start(bf16[512,2048]{0,1:T(8,128)(2,1)S(1)} %bitcast.138), channel_id=1, source_target_pairs={{0,8},{8,24},{24,16},{16,0},{1,9},{9,25},{25,17},{17,1},{2,10},{10... | collective-permute-start | bytes 6291464 | tf_op jit(solution)/shard_map/ppermute | solution.py:189
  255.1 55.0 %collective-permute-start = (bf16[512,2048]{0,1:T(8,128)(2,1)S(1)}, bf16[512,2048]{0,1:T(8,128)(2,1)}, u32[]{:S(2)}, u32[]{:S(2)}) collective-permute-start(bf16[512,2048]{0,1:T(8,128)(2,1)S(1)} %bitcast.139), channel_id=1, source_target_pairs={{8,0},{24,8},{16,24},{0,16},{9,1},{25,9},{17,25},{1,17},{10,2},{26... | collective-permute-start | bytes 6291464 | tf_op jit(solution)/shard_map/ppermute | solution.py:190
  255.7 231.9 %reduce-scatter.5.cloned.1.call-start = ((), (), s32[]{:S(2)}) async-start(), calls=%async_computation.16 | async-start | bytes 9437184 | tf_op jit(solution)/shard_map/reduce_scatter | solution.py:300
  312.7 25.8 %collective-permute-start.7 = (bf16[256,2048]{0,1:T(8,128)(2,1)S(1)}, bf16[256,2048]{0,1:T(8,128)(2,1)S(1)}, u32[]{:S(2)}, u32[]{:S(2)}) collective-permute-start(bf16[256,2048]{0,1:T(8,128)(2,1)S(1)} %slice.162), channel_id=1, source_target_pairs={{8,0},{24,8},{16,24},{0,16},{9,1},{25,9},{17,25},{1,17},{10,2},{26... | collective-permute-start | bytes 3145736 | tf_op jit(solution)/shard_map/ppermute | solution.py:190
  363.4 210.8 %reduce-scatter.7.cloned.1.call-start = ((), (), s32[]{:S(2)}) async-start(), calls=%async_computation.17 | async-start | bytes 9437184 | tf_op jit(solution)/shard_map/reduce_scatter | solution.py:300
  415.0 263.1 %reduce-scatter.9.cloned.1.call-start = ((), (), s32[]{:S(2)}) async-start(), calls=%async_computation.18 | async-start | bytes 7077888 | tf_op jit(solution)/shard_map/reduce_scatter | solution.py:300
  514.0 82.8 %collective-permute-start.11 = (bf16[512,2048]{1,0:T(8,128)(2,1)}, bf16[512,2048]{1,0:T(8,128)(2,1)}, u32[]{:S(2)}, u32[]{:S(2)}) collective-permute-start(bf16[512,2048]{1,0:T(8,128)(2,1)} %pad_maximum_fusion.1), channel_id=1, source_target_pairs={{8,0},{24,8},{16,24},{0,16},{9,1},{25,9},{17,25},{1,17},{10,2},{26... | collective-permute-start | bytes 6291464 | tf_op jit(solution)/shard_map/ppermute | solution.py:190
  516.2 80.6 %collective-permute-start.10 = (bf16[512,2048]{1,0:T(8,128)(2,1)}, bf16[512,2048]{1,0:T(8,128)(2,1)}, u32[]{:S(2)}, u32[]{:S(2)}) collective-permute-start(bf16[512,2048]{1,0:T(8,128)(2,1)} %pad_maximum_fusion), channel_id=1, source_target_pairs={{0,8},{8,24},{24,16},{16,0},{1,9},{9,25},{25,17},{17,1},{2,10},{10... | collective-permute-start | bytes 6291464 | tf_op jit(solution)/shard_map/ppermute | solution.py:189
  602.4 63.0 %all-to-all-start.5 = ((bf16[8,512,256]{2,1,0:T(8,128)(2,1)}), bf16[8,512,256]{2,1,0:T(8,128)(2,1)}, u32[]{:S(2)}, u32[]{:S(2)}) async-start(bf16[8,512,256]{2,1,0:T(8,128)(2,1)} %bitcast.126), calls=%async_computation.6 | async-start | bytes 4194304 | tf_op jit(solution)/shard_map/all_to_all | solution.py:198
  608.4 48.4 %collective-permute-start.18 = (bf16[512,2048]{1,0:T(8,128)(2,1)}, bf16[512,2048]{1,0:T(8,128)(2,1)}, u32[]{:S(2)}, u32[]{:S(2)}) collective-permute-start(bf16[512,2048]{1,0:T(8,128)(2,1)} %pad_maximum_fusion.3), channel_id=1, source_target_pairs={{8,0},{24,8},{16,24},{0,16},{9,1},{25,9},{17,25},{1,17},{10,2},{26... | collective-permute-start | bytes 6291464 | tf_op jit(solution)/shard_map/ppermute | solution.py:190
  612.5 47.9 %collective-permute-start.17 = (bf16[512,2048]{1,0:T(8,128)(2,1)}, bf16[512,2048]{1,0:T(8,128)(2,1)}, u32[]{:S(2)}, u32[]{:S(2)}) collective-permute-start(bf16[512,2048]{1,0:T(8,128)(2,1)} %pad_maximum_fusion.2), channel_id=1, source_target_pairs={{0,8},{8,24},{24,16},{16,0},{1,9},{9,25},{25,17},{17,1},{2,10},{10... | collective-permute-start | bytes 6291464 | tf_op jit(solution)/shard_map/ppermute | solution.py:189
  681.1 53.4 %all-to-all-start.7 = ((bf16[8,512,256]{2,1,0:T(8,128)(2,1)}), bf16[8,512,256]{2,1,0:T(8,128)(2,1)}, u32[]{:S(2)}, u32[]{:S(2)}) async-start(bf16[8,512,256]{2,1,0:T(8,128)(2,1)} %bitcast.137), calls=%async_computation.10 | async-start | bytes 4194304 | tf_op jit(solution)/shard_map/all_to_all | solution.py:198
  685.5 92.6 %reduce-scatter.11.cloned.1.call-start = ((), (), s32[]{:S(2)}) async-start(), calls=%async_computation.19 | async-start | bytes 2359296 | tf_op jit(solution)/shard_map/reduce_scatter | solution.py:300
  693.3 42.7 %collective-permute-start.14 = (bf16[2,2,256,256]{3,2,0,1:T(8,128)(2,1)}, bf16[2,2,256,256]{3,2,0,1:T(8,128)(2,1)}, u32[]{:S(2)}, u32[]{:S(2)}) collective-permute-start(bf16[2,2,256,256]{3,2,0,1:T(8,128)(2,1)} %get-tuple-element.190), channel_id=1, source_target_pairs={{0,24},{8,16},{16,8},{24,0},{1,25},{9,17},{17,9},{25,1},{2,26},{10... | collective-permute-start | bytes 1572872 | tf_op jit(solution)/shard_map/ppermute | solution.py:215
  694.9 40.0 %collective-permute-start.13 = (bf16[2,2,256,256]{3,2,0,1:T(8,128)(2,1)}, bf16[2,2,256,256]{3,2,0,1:T(8,128)(2,1)}, u32[]{:S(2)}, u32[]{:S(2)}) collective-permute-start(bf16[2,2,256,256]{3,2,0,1:T(8,128)(2,1)} %get-tuple-element.191), channel_id=1, source_target_pairs={{0,16},{8,24},{16,0},{24,8},{1,17},{9,25},{17,1},{25,9},{2,18},{10... | collective-permute-start | bytes 1572872 | tf_op jit(solution)/shard_map/ppermute | solution.py:215
  695.5 39.3 %collective-permute-start.12 = (bf16[2,2,256,256]{3,2,0,1:T(8,128)(2,1)}, bf16[2,2,256,256]{3,2,0,1:T(8,128)(2,1)S(1)}, u32[]{:S(2)}, u32[]{:S(2)}) collective-permute-start(bf16[2,2,256,256]{3,2,0,1:T(8,128)(2,1)} %get-tuple-element.192), channel_id=1, source_target_pairs={{0,8},{8,0},{16,24},{24,16},{1,9},{9,1},{17,25},{25,17},{2,10},{10... | collective-permute-start | bytes 1572872 | tf_op jit(solution)/shard_map/ppermute | solution.py:215
  744.1 29.2 %all-to-all-start.8 = ((bf16[4,2,2,256,256]{4,3,1,2,0:T(8,128)(2,1)}), bf16[4,2,2,256,256]{4,3,1,2,0:T(8,128)(2,1)}, u32[]{:S(2)}, u32[]{:S(2)}) async-start(bf16[4,2,2,256,256]{4,3,1,2,0:T(8,128)(2,1)} %copy.114), calls=%async_computation.11 | async-start | bytes 4194304 | tf_op jit(solution)/shard_map/all_to_all | solution.py:206
  (41 other events, 1263.0 us)
Sparse Core Ops, SparseCore 0:
  9.6 91.6 all-gather.3
  138.0 125.3 all-gather.5
  265.6 81.9 all-gather.7
  363.5 87.1 reduce-scatter.4
  452.8 87.9 reduce-scatter.6
  543.0 68.1 reduce-scatter.8
  734.7 33.4 reduce-scatter.10

commit v9 on v8

--- a/solution.py
+++ b/solution.py
@@ -267,12 +267,20 @@
         )
 
     gains = jnp.stack([first_gain, first_shift, second_gain, second_shift])
-    spread_gains = broadcast(gains, "col", cols)
+    if cols & (cols - 1):
+        spread_gains = broadcast(gains, "col", cols)
+    else:
+        mine = lax.broadcasted_iota(jnp.int32, (cols, 1, 1), 0) == lax.axis_index("col")
+        spread_gains = jnp.where(mine, gains[None], 0.0)
+        step = 1
+        while step < cols:
+            spread_gains += lax.ppermute(spread_gains, "col", [(c, c ^ step) for c in range(cols)])
+            step *= 2
     gains = spread_gains.transpose(1, 0, 2).reshape(4, cols * width)
     expand_w = lax.all_gather(expand_weight, "col", axis=0, tiled=True)
-    x_half = row_swap(after(inputs, spread_gains))
+    x_half = row_swap(inputs)
     cot_half = row_swap(after(cotangent, x_half))
-    x_part = col_swap(after(x_half, cot_half))
+    x_part = col_swap(after(x_half, cot_half, spread_gains))
     reduce_w = lax.all_gather(after(reduce_weight, x_part), "col", axis=1, tiled=True)
     mixed_weight = jnp.concatenate([merged_weight, output_weight.T], axis=1)
     cot_part = col_swap(after(cot_half, x_part))

time: 796 us -> 797 us (level)
  blocking collectives: 125 us -> 95 us
  waiting for transfers between devices: 201 us -> 219 us
  starting transfers between devices: 45.2 us -> 54.9 us
    all_to_all x2 -> x1, blocking collectives: 55.5 us -> 30.5 us  [row_swap(): b = lax.all_to_all(b, 'row', split_axis=0, concat_axis=0, tiled=True)]
    all_to_all x1 -> x0, blocking collectives: 11.9 us -> none  [broadcast(): lax.all_to_all(jnp.broadcast_to(value, (size,) + value.shape), axis, spli...]
    ppermute x0 -> x3, waiting for transfers between devices: none -> 11.5 us  [body(): lax.ppermute(spread_gains, 'col', [(c, c ^ step) for c in range(cols)])]
    unnamed x76 -> x86, local copies, waits for them, and re-layouts: 21.9 us -> 21.9 us
  transfers between devices with their start and end apart: 33 -> 37, of which waited for: 14 -> 18; matrix products, arithmetic and copies ran while one was open for 46% -> 47% of each run, Pallas kernels for 3% -> 3%
where the time goes in v9:
time: 797 us; the launch traced here: 789 us
  matrix products  227 us (28%)
  waiting for transfers between devices  219 us (27%)
  blocking collectives  95 us (12%)
  other arithmetic  87.6 us (11%)
  local copies, waits for them, and re-layouts  68.9 us (9%)
  starting transfers between devices  54.9 us (7%)
  Pallas kernels  21 us (3%)
  between operations  15.1 us (2%)
    dot_general x4, matrix products, contract_last(): lax.dot_general(left, right, (((1,), (1,)), ((), ())), preferred_element_...  82.7 us
    dot_general x4, matrix products, mm(): return jnp.dot(left, right, preferred_element_type=F32)  73.3 us
    dot_general x4, matrix products, contract_first(): lax.dot_general(left, right, (((0,), (0,)), ((), ())), preferred_element_...  71.1 us
    ppermute x8, waiting for transfers between devices, body(): up = lambda v: lax.ppermute(v, 'row', ahead)  68.1 us
    all_to_all x1, blocking collectives, col_swap(): return lax.all_to_all(b, 'col', split_axis=0, concat_axis=0, tiled=True)  64.5 us
    ppermute x8, waiting for transfers between devices, body(): down = lambda v: lax.ppermute(v, 'row', behind)  61.2 us
    all_to_all x3, waiting for transfers between devices, col_swap(): return lax.all_to_all(b, 'col', split_axis=0, concat_axis=0, tiled=True)  51.5 us
    all_to_all x1, blocking collectives, row_swap(): b = lax.all_to_all(b, 'row', split_axis=0, concat_axis=0, tiled=True)  30.5 us
  transfers between devices with their start and end apart: 37, of which 18 were waited for; matrix products, arithmetic and copies ran while one was open for 47% of the time, Pallas kernels for 3%

profile of v9, /device:TPU:0, one launch (start us, length us, event | category | flops | bytes accessed | tf_op | source)
XLA Modules:
  0.0 789.0 jit_solution(15390444525965953118)
XLA Ops:
  9.7 30.5 %all_to_all.40 = bf16[4,2,2,256,256]{4,3,1,2,0:T(8,128)(2,1)S(1)} all-to-all(bf16[4,2,2,256,256]{4,3,1,2,0:T(8,128)(2,1)S(1)} %copy.98), channel_id=1, replica_groups=mesh['row'=4,'col'=8] {'row'}, dimensions={0} | all-to-all | bytes 4194304 | tf_op jit(solution)/shard_map/all_to_all | solution.py:194
  74.7 64.5 %all_to_all.41 = bf16[8,512,256]{2,1,0:T(8,128)(2,1)} all-to-all(bf16[8,512,256]{2,1,0:T(8,128)(2,1)S(1)} %bitcast.138), channel_id=1, replica_groups=mesh['row'=4,'col'=8] {'col'}, dimensions={0} | all-to-all | bytes 4194304 | tf_op jit(solution)/shard_map/all_to_all | solution.py:198
  150.7 38.1 %collective-permute-done.6 = bf16[512,2048]{1,0:T(8,128)(2,1)} collective-permute-done((bf16[512,2048]{1,0:T(8,128)(2,1)S(1)}, bf16[512,2048]{1,0:T(8,128)(2,1)}, u32[]{:S(2)}, u32[]{:S(2)}) %collective-permute-start.6) | collective-permute-done | bytes 2097184 | tf_op jit(solution)/shard_map/ppermute | solution.py:189
  203.3 12.5 %collective-permute-done.7 = bf16[256,2048]{1,0:T(8,128)(2,1)} collective-permute-done((bf16[256,2048]{1,0:T(8,128)(2,1)}, bf16[256,2048]{1,0:T(8,128)(2,1)}, u32[]{:S(2)}, u32[]{:S(2)}) %collective-permute-start.7) | collective-permute-done | bytes 1048608 | tf_op jit(solution)/shard_map/ppermute | solution.py:189
  228.2 23.6 %all-to-all-done.3 = bf16[8,512,256]{2,1,0:T(8,128)(2,1)} async-done(((bf16[8,512,256]{2,1,0:T(8,128)(2,1)}), bf16[8,512,256]{2,1,0:T(8,128)(2,1)}, u32[]{:S(2)}, u32[]{:S(2)}) %all-to-all-start.3) | async-done | bytes 2097184 | tf_op jit(solution)/shard_map/all_to_all | solution.py:198
  257.3 21.8 %convolution_add_fusion.1 = f32[2048,2048]{1,0:T(8,128)S(1)} fusion(bf16[2048,2048]{1,0:T(8,128)(2,1)} %all-gather.4.cloned.1.call-done, f32[2048]{0:T(1024)S(1)} %copy-done.31, bf16[2048,2048]{1,0:T(8,128)(2,1)} %copy-done, f32[2048]{0:T(1024)S(1)} %bitcast.157, f32[2048]{0:T(1024)S(1)} %bitcast.154, f32[2048]{0:T(1024)S(1)} %add_rsqrt_fusion, ...), kind=kOutput, calls=%fused_computation.29 | convolution fusion | flops 17209229312 | bytes 33595392 | tf_op jit(solution)/shard_map/dot_general | solution.py:24
  279.1 8.7 %fusion.17 = (bf16[2048,2048]{1,0:T(8,128)(2,1)}, bf16[2048,2048]{1,0:T(8,128)(2,1)}) fusion(f32[2048,2048]{1,0:T(8,128)S(1)} %convolution_add_fusion.1), kind=kLoop, calls=%fused_computation.20 | loop fusion | flops 46137344 | bytes 33554432 | tf_op jit(solution)/shard_map/convert_element_type | solution.py:302
  287.8 23.6 %convolution_convert_fusion.2 = bf16[2048,2048]{1,0:T(8,128)(2,1)} fusion(bf16[2048,2048]{1,0:T(8,128)(2,1)} %get-tuple-element.50, bf16[2048,2048]{1,0:T(8,128)(2,1)} %all-gather.6.cloned.1.call-done), kind=kOutput, calls=%fused_computation.32 | convolution fusion | flops 17184063488 | bytes 25165824 | tf_op jit(solution)/shard_map/dot_general | solution.py:24
  316.1 8.6 %fusion.9 = bf16[2048,2048]{1,0:T(8,128)(2,1)} fusion(bf16[2048,2048]{1,0:T(8,128)(2,1)} %copy-done, f32[2048]{0:T(1024)S(1)} %bitcast.153, f32[2048]{0:T(1024)S(1)} %bitcast.151, f32[2048]{0:T(1024)S(1)} %add_rsqrt_fusion, f32[2048]{0:T(1024)S(1)} %broadcast_multiply_fusion), kind=kLoop, calls=%fused_computation.12 | loop fusion | flops 25165824 | bytes 16809984 | tf_op jit(solution)/shard_map/convert_element_type | solution.py:292
  327.2 12.6 %collective-permute-done.9 = bf16[256,2048]{0,1:T(8,128)(2,1)S(1)} collective-permute-done((bf16[256,2048]{0,1:T(8,128)(2,1)S(1)}, bf16[256,2048]{0,1:T(8,128)(2,1)S(1)}, u32[]{:S(2)}, u32[]{:S(2)}) %collective-permute-start.9) | collective-permute-done | bytes 1048608 | tf_op jit(solution)/shard_map/ppermute | solution.py:189
  345.3 19.5 %convolution_convert_fusion.1 = bf16[2048,2048]{1,0:T(8,128)(2,1)} fusion(bf16[2048,2048]{0,1:T(8,128)(2,1)S(1)} %constant_dynamic-update-slice_fusion.5, bf16[2048,2048]{1,0:T(8,128)(2,1)S(1)} %bitcast.144), kind=kOutput, calls=%fused_computation.31 | convolution fusion | flops 17184063488 | bytes 25165824 | tf_op jit(solution)/shard_map/dot_general | solution.py:32
  365.3 25.2 %convert_reduce_fusion.1 = (f32[2048]{0:T(1024)}, bf16[2048,2048]{1,0:T(8,128)(2,1)S(1)}) fusion(bf16[2048,2048]{1,0:T(8,128)(2,1)} %get-tuple-element.57, bf16[2048,2048]{0,1:T(8,128)(2,1)} %copy-done.9, bf16[2048,2048]{1,0:T(8,128)(2,1)} %all-gather.6.cloned.1.call-done), kind=kOutput, calls=%fused_computation.21 | convolution fusion | flops 17200838656 | bytes 33562624 | tf_op jit(solution)/shard_map/dot_general | solution.py:28
  393.8 22.6 %convolution_convert_fusion = bf16[2048,2048]{1,0:T(8,128)(2,1)} fusion(bf16[2048,2048]{1,0:T(8,128)(2,1)S(1)} %get-tuple-element.71, bf16[2048,2048]{1,0:T(8,128)(2,1)} %copy-done, f32[2048]{0:T(1024)S(1)} %bitcast.158, f32[2048]{0:T(1024)S(1)} %bitcast.155, f32[2048]{0:T(1024)S(1)} %add_rsqrt_fusion, f32[2048]{0:T(1024)S(1)} %broadcast_multiply_fusion), kind=kOutput, calls=%fused_computation.30 | convolution fusion | flops 17209229312 | bytes 25198592 | tf_op jit(solution)/shard_map/dot_general | solution.py:32
  420.2 10.1 %convolution_convert_fusion.5 = bf16[2048,512]{1,0:T(8,128)(2,1)} fusion(bf16[2048,2048]{0,1:T(8,128)(2,1)} %copy-done.9, bf16[2048,2048]{1,0:T(8,128)(2,1)} %all-gather.8.cloned.1.call-done), kind=kOutput, calls=%fused_computation.53 | convolution fusion | flops 4296015872 | bytes 12582912 | tf_op jit(solution)/shard_map/dot_general | solution.py:24
  430.3 17.7 %convolution_add_fusion = f32[2048,1536]{1,0:T(8,128)} fusion(bf16[2048,2048]{1,0:T(8,128)(2,1)} %fusion.9, f32[1536]{0:T(1024)S(1)} %copy-done.32, bf16[2048,2048]{1,0:T(8,128)(2,1)S(1)} %copy-done.30), kind=kOutput, calls=%fused_computation.28 | convolution fusion | flops 12888047616 | bytes 27271168 | tf_op jit(solution)/shard_map/dot_general | solution.py:24
  448.0 21.0 %attention.1 = (bf16[4,2,256,512]{3,2,1,0:T(8,128)(2,1)}, bf16[4,2,256,1536]{3,2,1,0:T(8,128)(2,1)}) custom-call(s32[4]{0:T(128)} %and_select_fusion.slot_ref, s32[4]{0:T(128)} %reshape.182.starts_ref, f32[4,2,256,1536]{3,2,1,0:T(8,128)} %bitcast.163, bf16[4,2,256,512]{3,2,1,0:T(8,128)(2,1)} %bitcast.166, f32[1024,128]{1,0:T(8,128)} %get-tuple-element.61.cos_ref, ...), custom_call_target="tpu_custom_call" | custom-call | flops 16106127360 | bytes 23068672 | tf_op jit(solution)/shard_map/attention/pallas_call | solution.py:124
  489.1 19.2 %convolution_convert_fusion.3 = bf16[2048,1536]{1,0:T(8,128)(2,1)} fusion(bf16[2048,2048]{1,0:T(8,128)(2,1)} %fusion.9, bf16[2048,1536]{1,0:T(8,128)(2,1)} %bitcast.145), kind=kOutput, calls=%fused_computation.33 | convolution fusion | flops 12888047616 | bytes 20971520 | tf_op jit(solution)/shard_map/dot_general | solution.py:32
  519.0 24.8 %fusion.39 = f32[2048,2048]{1,0:T(8,128)} fusion(bf16[2048,2048]{1,0:T(8,128)(2,1)} %copy-done.34, bf16[2048,2048]{1,0:T(8,128)(2,1)} %all-gather.4.cloned.1.call-done), kind=kOutput, calls=%fused_computation.126 | convolution fusion | flops 17179869184 | bytes 33554432 | tf_op jit(solution)/shard_map/dot_general | solution.py:28
  543.9 25.7 %fusion.10 = (f32[2048]{0:T(1024)S(1)}, f32[2048]{0:T(1024)S(1)}, f32[2048]{0:T(1024)S(1)}, f32[2048]{0:T(1024)S(1)}, bf16[2048,2048]{1,0:T(8,128)(2,1)}) fusion(bf16[2048,2048]{1,0:T(8,128)(2,1)} %copy-done, f32[2048]{0:T(1024)S(1)} %copy-done.13, f32[2048]{0:T(1024)S(1)} %copy-done.11, f32[2048,2048]{1,0:T(8,128)} %fusion.39, f32[2048]{0:T(1024)S(1)} %bitcast.156, ...), kind=kOutput, calls=%fused_computation.13 | convolution fusion | flops 12939419648 | bytes 46202880 | tf_op jit(solution)/shard_map/dot_general | solution.py:28
  575.6 18.5 %collective-permute-done.19 = bf16[256,2048]{1,0:T(8,128)(2,1)S(1)} collective-permute-done((bf16[256,2048]{1,0:T(8,128)(2,1)}, bf16[256,2048]{1,0:T(8,128)(2,1)S(1)}, u32[]{:S(2)}, u32[]{:S(2)}) %collective-permute-start.19) | collective-permute-done | bytes 1048608 | tf_op jit(solution)/shard_map/ppermute | solution.py:190
  622.8 35.3 %collective-permute-done.21 = bf16[512,2048]{1,0:T(8,128)(2,1)} collective-permute-done((bf16[512,2048]{1,0:T(8,128)(2,1)}, bf16[512,2048]{1,0:T(8,128)(2,1)}, u32[]{:S(2)}, u32[]{:S(2)}) %collective-permute-start.21) | collective-permute-done | bytes 2097184 | tf_op jit(solution)/shard_map/ppermute | solution.py:190
  698.1 9.8 %convolution_convert_fusion.4 = bf16[2048,512]{1,0:T(8,128)(2,1)} fusion(bf16[2048,2048]{0,1:T(8,128)(2,1)} %copy-done.9, bf16[2048,512]{1,0:T(8,128)(2,1)} %bitcast.165), kind=kOutput, calls=%fused_computation.52 | convolution fusion | flops 4296015872 | bytes 12582912 | tf_op jit(solution)/shard_map/dot_general | solution.py:32
  708.0 27.9 %all-to-all-done.6 = bf16[8,512,256]{2,1,0:T(8,128)(2,1)} async-done(((bf16[8,512,256]{2,1,0:T(8,128)(2,1)}), bf16[8,512,256]{2,1,0:T(8,128)(2,1)}, u32[]{:S(2)}, u32[]{:S(2)}) %all-to-all-start.6) | async-done | bytes 2097184 | tf_op jit(solution)/shard_map/all_to_all | solution.py:198
  761.4 13.2 %all-to-all-done.7 = bf16[4,2,2,256,256]{4,3,1,2,0:T(8,128)(2,1)} async-done(((bf16[4,2,2,256,256]{4,3,1,2,0:T(8,128)(2,1)}), bf16[4,2,2,256,256]{4,3,1,2,0:T(8,128)(2,1)}, u32[]{:S(2)}, u32[]{:S(2)}) %all-to-all-start.7) | async-done | bytes 2097184 | tf_op jit(solution)/shard_map/all_to_all | solution.py:206
  (251 shorter events, 238.6 us)
Async XLA Ops:
  7.2 250.1 %all-gather.4.cloned.1.call-start = ((), (), s32[]{:S(2)}) async-start(), calls=%async_computation.12 | async-start | bytes 9437184 | tf_op jit(solution)/shard_map/all_gather | solution.py:280
  43.1 28.4 %all-to-all-start.1 = ((bf16[4,2,2,256,256]{4,3,1,2,0:T(8,128)(2,1)}), bf16[4,2,2,256,256]{4,3,1,2,0:T(8,128)(2,1)}, u32[]{:S(2)}, u32[]{:S(2)}) async-start(bf16[4,2,2,256,256]{4,3,1,2,0:T(8,128)(2,1)} %copy.100), calls=%async_computation.1 | async-start | bytes 4194304 | tf_op jit(solution)/shard_map/all_to_all | solution.py:194
  47.7 240.1 %all-gather.6.cloned.1.call-start = ((), (), s32[]{:S(2)}) async-start(), calls=%async_computation.13 | async-start | bytes 9437184 | tf_op jit(solution)/shard_map/all_gather | solution.py:284
  141.1 47.8 %collective-permute-start.6 = (bf16[512,2048]{1,0:T(8,128)(2,1)S(1)}, bf16[512,2048]{1,0:T(8,128)(2,1)}, u32[]{:S(2)}, u32[]{:S(2)}) collective-permute-start(bf16[512,2048]{1,0:T(8,128)(2,1)S(1)} %bitcast.127), channel_id=1, source_target_pairs={{0,8},{8,24},{24,16},{16,0},{1,9},{9,25},{25,17},{17,1},{2,10},{10... | collective-permute-start | bytes 6291464 | tf_op jit(solution)/shard_map/ppermute | solution.py:189
  142.5 53.7 %collective-permute-start.5 = (bf16[512,2048]{1,0:T(8,128)(2,1)S(1)}, bf16[512,2048]{1,0:T(8,128)(2,1)}, u32[]{:S(2)}, u32[]{:S(2)}) collective-permute-start(bf16[512,2048]{1,0:T(8,128)(2,1)S(1)} %bitcast.128), channel_id=1, source_target_pairs={{8,0},{24,8},{16,24},{0,16},{9,1},{25,9},{17,25},{1,17},{10,2},{26... | collective-permute-start | bytes 6291464 | tf_op jit(solution)/shard_map/ppermute | solution.py:190
  146.3 105.6 %all-to-all-start.3 = ((bf16[8,512,256]{2,1,0:T(8,128)(2,1)}), bf16[8,512,256]{2,1,0:T(8,128)(2,1)}, u32[]{:S(2)}, u32[]{:S(2)}) async-start(bf16[8,512,256]{2,1,0:T(8,128)(2,1)} %bitcast.136), calls=%async_computation.3 | async-start | bytes 4194304 | tf_op jit(solution)/shard_map/all_to_all | solution.py:198
  150.7 269.5 %all-gather.8.cloned.1.call-start = ((), (), s32[]{:S(2)}) async-start(), calls=%async_computation.14 | async-start | bytes 9437184 | tf_op jit(solution)/shard_map/all_gather | solution.py:297
  254.9 56.5 %collective-permute-start.4 = (bf16[512,2048]{0,1:T(8,128)(2,1)S(1)}, bf16[512,2048]{0,1:T(8,128)(2,1)}, u32[]{:S(2)}, u32[]{:S(2)}) collective-permute-start(bf16[512,2048]{0,1:T(8,128)(2,1)S(1)} %bitcast.139), channel_id=1, source_target_pairs={{0,8},{8,24},{24,16},{16,0},{1,9},{9,25},{25,17},{17,1},{2,10},{10... | collective-permute-start | bytes 6291464 | tf_op jit(solution)/shard_map/ppermute | solution.py:189
  256.6 54.8 %collective-permute-start.3 = (bf16[512,2048]{0,1:T(8,128)(2,1)S(1)}, bf16[512,2048]{0,1:T(8,128)(2,1)}, u32[]{:S(2)}, u32[]{:S(2)}) collective-permute-start(bf16[512,2048]{0,1:T(8,128)(2,1)S(1)} %bitcast.140), channel_id=1, source_target_pairs={{8,0},{24,8},{16,24},{0,16},{9,1},{25,9},{17,25},{1,17},{10,2},{26... | collective-permute-start | bytes 6291464 | tf_op jit(solution)/shard_map/ppermute | solution.py:190
  257.0 232.1 %reduce-scatter.5.cloned.1.call-start = ((), (), s32[]{:S(2)}) async-start(), calls=%async_computation.15 | async-start | bytes 9437184 | tf_op jit(solution)/shard_map/reduce_scatter | solution.py:308
  314.0 25.9 %collective-permute-start.10 = (bf16[256,2048]{0,1:T(8,128)(2,1)S(1)}, bf16[256,2048]{0,1:T(8,128)(2,1)S(1)}, u32[]{:S(2)}, u32[]{:S(2)}) collective-permute-start(bf16[256,2048]{0,1:T(8,128)(2,1)S(1)} %slice.162), channel_id=1, source_target_pairs={{8,0},{24,8},{16,24},{0,16},{9,1},{25,9},{17,25},{1,17},{10,2},{26... | collective-permute-start | bytes 3145736 | tf_op jit(solution)/shard_map/ppermute | solution.py:190
  364.8 210.8 %reduce-scatter.7.cloned.1.call-start = ((), (), s32[]{:S(2)}) async-start(), calls=%async_computation.16 | async-start | bytes 9437184 | tf_op jit(solution)/shard_map/reduce_scatter | solution.py:308
  416.4 262.9 %reduce-scatter.9.cloned.1.call-start = ((), (), s32[]{:S(2)}) async-start(), calls=%async_computation.17 | async-start | bytes 7077888 | tf_op jit(solution)/shard_map/reduce_scatter | solution.py:308
  515.4 82.7 %collective-permute-start.14 = (bf16[512,2048]{1,0:T(8,128)(2,1)}, bf16[512,2048]{1,0:T(8,128)(2,1)}, u32[]{:S(2)}, u32[]{:S(2)}) collective-permute-start(bf16[512,2048]{1,0:T(8,128)(2,1)} %pad_maximum_fusion.1), channel_id=1, source_target_pairs={{8,0},{24,8},{16,24},{0,16},{9,1},{25,9},{17,25},{1,17},{10,2},{26... | collective-permute-start | bytes 6291464 | tf_op jit(solution)/shard_map/ppermute | solution.py:190
  517.7 80.5 %collective-permute-start.13 = (bf16[512,2048]{1,0:T(8,128)(2,1)}, bf16[512,2048]{1,0:T(8,128)(2,1)}, u32[]{:S(2)}, u32[]{:S(2)}) collective-permute-start(bf16[512,2048]{1,0:T(8,128)(2,1)} %pad_maximum_fusion), channel_id=1, source_target_pairs={{0,8},{8,24},{24,16},{16,0},{1,9},{9,25},{25,17},{17,1},{2,10},{10... | collective-permute-start | bytes 6291464 | tf_op jit(solution)/shard_map/ppermute | solution.py:189
  603.8 63.0 %all-to-all-start.4 = ((bf16[8,512,256]{2,1,0:T(8,128)(2,1)}), bf16[8,512,256]{2,1,0:T(8,128)(2,1)}, u32[]{:S(2)}, u32[]{:S(2)}) async-start(bf16[8,512,256]{2,1,0:T(8,128)(2,1)} %bitcast.126), calls=%async_computation.5 | async-start | bytes 4194304 | tf_op jit(solution)/shard_map/all_to_all | solution.py:198
  609.8 48.4 %collective-permute-start.21 = (bf16[512,2048]{1,0:T(8,128)(2,1)}, bf16[512,2048]{1,0:T(8,128)(2,1)}, u32[]{:S(2)}, u32[]{:S(2)}) collective-permute-start(bf16[512,2048]{1,0:T(8,128)(2,1)} %pad_maximum_fusion.3), channel_id=1, source_target_pairs={{8,0},{24,8},{16,24},{0,16},{9,1},{25,9},{17,25},{1,17},{10,2},{26... | collective-permute-start | bytes 6291464 | tf_op jit(solution)/shard_map/ppermute | solution.py:190
  613.8 47.9 %collective-permute-start.20 = (bf16[512,2048]{1,0:T(8,128)(2,1)}, bf16[512,2048]{1,0:T(8,128)(2,1)}, u32[]{:S(2)}, u32[]{:S(2)}) collective-permute-start(bf16[512,2048]{1,0:T(8,128)(2,1)} %pad_maximum_fusion.2), channel_id=1, source_target_pairs={{0,8},{8,24},{24,16},{16,0},{1,9},{9,25},{25,17},{17,1},{2,10},{10... | collective-permute-start | bytes 6291464 | tf_op jit(solution)/shard_map/ppermute | solution.py:189
  682.4 53.4 %all-to-all-start.6 = ((bf16[8,512,256]{2,1,0:T(8,128)(2,1)}), bf16[8,512,256]{2,1,0:T(8,128)(2,1)}, u32[]{:S(2)}, u32[]{:S(2)}) async-start(bf16[8,512,256]{2,1,0:T(8,128)(2,1)} %bitcast.137), calls=%async_computation.9 | async-start | bytes 4194304 | tf_op jit(solution)/shard_map/all_to_all | solution.py:198
  686.8 92.6 %reduce-scatter.11.cloned.1.call-start = ((), (), s32[]{:S(2)}) async-start(), calls=%async_computation.18 | async-start | bytes 2359296 | tf_op jit(solution)/shard_map/reduce_scatter | solution.py:308
  694.6 42.7 %collective-permute-start.17 = (bf16[2,2,256,256]{3,2,0,1:T(8,128)(2,1)}, bf16[2,2,256,256]{3,2,0,1:T(8,128)(2,1)}, u32[]{:S(2)}, u32[]{:S(2)}) collective-permute-start(bf16[2,2,256,256]{3,2,0,1:T(8,128)(2,1)} %get-tuple-element.188), channel_id=1, source_target_pairs={{0,24},{8,16},{16,8},{24,0},{1,25},{9,17},{17,9},{25,1},{2,26},{10... | collective-permute-start | bytes 1572872 | tf_op jit(solution)/shard_map/ppermute | solution.py:215
  696.2 40.0 %collective-permute-start.16 = (bf16[2,2,256,256]{3,2,0,1:T(8,128)(2,1)}, bf16[2,2,256,256]{3,2,0,1:T(8,128)(2,1)}, u32[]{:S(2)}, u32[]{:S(2)}) collective-permute-start(bf16[2,2,256,256]{3,2,0,1:T(8,128)(2,1)} %get-tuple-element.189), channel_id=1, source_target_pairs={{0,16},{8,24},{16,0},{24,8},{1,17},{9,25},{17,1},{25,9},{2,18},{10... | collective-permute-start | bytes 1572872 | tf_op jit(solution)/shard_map/ppermute | solution.py:215
  696.9 39.2 %collective-permute-start.15 = (bf16[2,2,256,256]{3,2,0,1:T(8,128)(2,1)}, bf16[2,2,256,256]{3,2,0,1:T(8,128)(2,1)S(1)}, u32[]{:S(2)}, u32[]{:S(2)}) collective-permute-start(bf16[2,2,256,256]{3,2,0,1:T(8,128)(2,1)} %get-tuple-element.190), channel_id=1, source_target_pairs={{0,8},{8,0},{16,24},{24,16},{1,9},{9,1},{17,25},{25,17},{2,10},{10... | collective-permute-start | bytes 1572872 | tf_op jit(solution)/shard_map/ppermute | solution.py:215
  745.4 29.2 %all-to-all-start.7 = ((bf16[4,2,2,256,256]{4,3,1,2,0:T(8,128)(2,1)}), bf16[4,2,2,256,256]{4,3,1,2,0:T(8,128)(2,1)}, u32[]{:S(2)}, u32[]{:S(2)}) async-start(bf16[4,2,2,256,256]{4,3,1,2,0:T(8,128)(2,1)} %copy.114), calls=%async_computation.10 | async-start | bytes 4194304 | tf_op jit(solution)/shard_map/all_to_all | solution.py:206
  (50 other events, 1477.7 us)
Sparse Core Ops, SparseCore 0:
  9.6 101.1 all-gather.3
  139.3 125.3 all-gather.5
  266.9 81.9 all-gather.7
  364.9 86.9 reduce-scatter.4
  454.1 87.9 reduce-scatter.6
  544.3 68.1 reduce-scatter.8
  736.0 33.6 reduce-scatter.10
